TPU v7x, 32 devices: a whole 2x2x4 slice. The times are simulated.
32 devices in a mesh: row: 16 (over z, x, core), col: 2 (over y).
Axes of the slice: x: 2, y: 2, z: 4, core: 2. Of those that a mesh axis runs over, the one named last changes fastest.
Arguments:
- features: bfloat16 [4096, 256], P(('row', 'col')), may hold values from -6 to 6
- weight: bfloat16 [256, 256], replicated, may hold values from -0.375 to 0.375
- grad_out: bfloat16 [4096, 256], P(('row', 'col')), may hold values from -6 to 6
- tiles: bfloat16 [16, 2, 24, 128, 128], P('row', 'col'), may hold values from -0.109375 to 0.109375
- slots: int32 [16, 2, 24], P('row', 'col'), may hold values from 0 to 31, as said below
Outputs:
- activated: bfloat16 [4096, 256], P(('row', 'col'))
- grad_weight: float32 [256, 256], replicated
- grad_in: bfloat16 [4096, 256], P(('row', 'col'))
Inputs may be any that keep to these rules, and one draw needn't show every extreme that they name: `slots`: within one tile the 24 entries are distinct.
All inputs are finite; a program needn't handle non-finite values.
Results may differ from a plain program's by a relative error of at most 0.0061.
Values may be sent and summed in bfloat16 or wider, within the bound.
No kernel may reach another device: no remote copies, remote signals or barrier semaphores. Data moves between devices by JAX's collectives and lax.ppermute only.
A program may use at most 128 MiB of HBM per device.

v0:
```python
import math

import jax
import jax.numpy as jnp
from jax import lax
from jax.sharding import PartitionSpec as P


def local(features, weight, grad_out, tiles, slots):
    tile_blocks = tiles[0, 0]
    tile_slots = slots[0, 0]
    own_rows, width = features.shape
    side = tile_blocks.shape[1]
    row_count = lax.axis_size("row")
    col_count = lax.axis_size("col")
    row_blocks = col_count * own_rows // side
    col_blocks = row_count * own_rows // side
    dense_tile = (
        jnp.zeros((row_blocks * col_blocks, side, side), jnp.bfloat16)
        .at[tile_slots]
        .set(tile_blocks)
    )
    dense_tile = dense_tile.reshape(row_blocks, col_blocks, side, side)
    column_panel = lax.all_gather(features, "row", axis=0, tiled=True).reshape(
        col_blocks, side, width
    )
    row_partial = jnp.einsum(
        "bcij,cjf->bif", dense_tile, column_panel, preferred_element_type=jnp.float32
    )
    row_partial = row_partial.reshape(row_blocks * side, width)
    aggregated = lax.psum_scatter(row_partial, "col", scatter_dimension=0, tiled=True).astype(
        jnp.bfloat16
    )
    pre = jnp.dot(aggregated, weight, preferred_element_type=jnp.float32)
    sigmoid_pre = jax.nn.sigmoid(pre)
    activated = (pre * sigmoid_pre).astype(jnp.bfloat16)
    grad_pre = (
        grad_out.astype(jnp.float32) * sigmoid_pre * (1.0 + pre * (1.0 - sigmoid_pre))
    ).astype(jnp.bfloat16)
    weight_term = jnp.dot(aggregated.T, grad_pre, preferred_element_type=jnp.float32)
    total_nodes = own_rows * row_count * col_count
    grad_weight = lax.psum(weight_term, ("row", "col")) * (1.0 / math.sqrt(total_nodes))
    grad_agg = jnp.dot(grad_pre, weight.T, preferred_element_type=jnp.float32).astype(jnp.bfloat16)
    row_panel = lax.all_gather(grad_agg, "col", axis=0, tiled=True).reshape(row_blocks, side, width)
    col_partial = jnp.einsum(
        "bcij,bif->cjf", dense_tile, row_panel, preferred_element_type=jnp.float32
    )
    col_partial = col_partial.reshape(col_blocks * side, width)
    summed = lax.psum_scatter(col_partial, "row", scatter_dimension=0, tiled=True)
    grad_in = summed.astype(jnp.bfloat16)
    return (activated, grad_weight, grad_in)


def solution(mesh):
    in_specs = (
        P(("row", "col"), None),
        P(),
        P(("row", "col"), None),
        P("row", "col", None, None, None),
        P("row", "col", None),
    )
    out_specs = (P(("row", "col"), None), P(), P(("row", "col"), None))
    return jax.shard_map(local, mesh=mesh, in_specs=in_specs, out_specs=out_specs, check_vma=False)
```

profile of v0, /device:TPU:0, one launch (start us, length us, event | category | flops | bytes accessed | tf_op | source)
XLA Modules:
  0.0 269.0 jit_solution(17586135211824430519)
XLA Ops:
  7.2 0.0 all-gather.2.cloned.1.call-start
  7.2 0.7 all-gather.2.cloned.1.call-update
  7.9 0.0 reduce-scatter.3.cloned.1.call-start
  8.0 0.7 fusion.4
  8.6 0.2 broadcast_in_dim.4
  8.9 3.5 %scatter_fusion = bf16[32,128,128]{2,1,0:T(8,128)(2,1)S(1)} fusion(bf16[32,128,128]{2,1,0:T(8,128)(2,1)S(1)} %broadcast_in_dim.4, s32[24]{0:T(128)S(1)} %fusion.4, bf16[24,128,128]{2,1,0:T(8,128)(2,1)} %bitcast.29), kind=kCustom, calls=%fused_computation | custom fusion | bytes 2359392 | tf_op jit(solution)/shard_map/scatter | solution.py:21
  12.4 0.1 copy.9
  12.5 38.4 %all-gather.2.cloned.1.call-done = bf16[2048,256]{1,0:T(8,128)(2,1)} async-done(((bf16[128,256]{1,0:T(8,128)(2,1)}), bf16[2048,256]{1,0:T(8,128)(2,1)}) %all-gather.2.cloned.1.call-update) | async-done | bytes 1048592 | tf_op jit(solution)/shard_map/all_gather | solution.py:24
  50.8 2.4 convolution_bitcast_fusion.1
  53.2 0.0 reduce-scatter.3.cloned.1.call-update
  53.2 0.0 all-reduce.2.cloned.1.call-start
  53.3 0.7 copy.10
  54.0 10.3 %reduce-scatter.3.cloned.1.call-done = f32[128,256]{1,0:T(8,128)} async-done(((f32[256,256]{1,0:T(8,128)}), f32[128,256]{1,0:T(8,128)}) %reduce-scatter.3.cloned.1.call-update) | async-done | bytes 131088 | tf_op jit(solution)/shard_map/reduce_scatter | solution.py:31
  64.3 1.7 multiply_convert_fusion.1
  66.0 0.2 convolution_convert_fusion
  66.2 1.8 fusion
  68.0 0.0 all-reduce.2.cloned.1.call-update
  68.1 0.0 reduce-scatter.5.cloned.1.call-start
  68.1 4.9 %all_gather.7 = bf16[256,256]{1,0:T(8,128)(2,1)S(1)} all-gather(bf16[128,256]{1,0:T(8,128)(2,1)S(1)} %convolution_convert_fusion), channel_id=1, replica_groups=mesh['row'=16,'col'=2] {'col'}, dimensions={0}, use_global_device_ids=true | all-gather | bytes 196608 | tf_op jit(solution)/shard_map/all_gather | solution.py:44
  73.1 1.8 convolution_bitcast_fusion
  74.9 121.4 %all-reduce.2.cloned.1.call-done = f32[256,256]{1,0:T(8,128)} async-done(((f32[256,256]{1,0:T(8,128)}), f32[256,256]{1,0:T(8,128)}) %all-reduce.2.cloned.1.call-update) | async-done | bytes 262160 | tf_op jit(solution)/shard_map/psum | solution.py:42
  196.3 1.7 broadcast_multiply_fusion
  197.9 63.0 %reduce-scatter.5.cloned.1.call-done = f32[128,256]{1,0:T(8,128)} async-done(((f32[2048,256]{1,0:T(8,128)}), f32[128,256]{1,0:T(8,128)}) %reduce-scatter.5.cloned.1.call-update) | async-done | bytes 131088 | tf_op jit(solution)/shard_map/reduce_scatter | solution.py:49
  260.9 1.5 convert_element_type.23
  (5 shorter events, 0.0 us)
Async XLA Ops:
  7.2 57.1 %copy-start = (bf16[256,256]{1,0:T(8,128)(2,1)S(1)}, bf16[256,256]{1,0:T(8,128)(2,1)}, u32[]{:S(2)}) copy-start(bf16[256,256]{1,0:T(8,128)(2,1)} %param.6) | copy-start | bytes 393220
  7.2 43.7 %all-gather.2.cloned.1.call-start = ((), (), s32[]{:S(2)}) async-start(), calls=%async_computation.2 | async-start | bytes 1114112 | tf_op jit(solution)/shard_map/all_gather | solution.py:24
  7.9 56.4 %reduce-scatter.3.cloned.1.call-start = ((), (), s32[]{:S(2)}) async-start(), calls=%async_computation.3 | async-start | bytes 393216 | tf_op jit(solution)/shard_map/reduce_scatter | solution.py:31
  53.2 12.8 %copy-start.1 = (bf16[128,256]{1,0:T(8,128)(2,1)S(1)}, bf16[128,256]{1,0:T(8,128)(2,1)}, u32[]{:S(2)}) copy-start(bf16[128,256]{1,0:T(8,128)(2,1)} %param.7) | copy-start | bytes 196612
  53.2 143.0 %all-reduce.2.cloned.1.call-start = ((), (), s32[]{:S(2)}) async-start(), calls=%async_computation.4 | async-start | bytes 524288 | tf_op jit(solution)/shard_map/psum | solution.py:42
  68.1 192.9 %reduce-scatter.5.cloned.1.call-start = ((), (), s32[]{:S(2)}) async-start(), calls=%async_computation.5 | async-start | bytes 2228224 | tf_op jit(solution)/shard_map/reduce_scatter | solution.py:49
Sparse Core Ops, SparseCore 0:
  10.2 40.6 all-gather.1
  53.6 10.5 reduce-scatter.2
  71.3 124.9 all-reduce.1
  200.3 60.5 reduce-scatter.4
where the time goes:
time: 269 us
  waiting for transfers between devices  234 us (87%)
  between operations  13.8 us (5%)
  matrix products  7.9 us (3%)
  blocking collectives  4.94 us (2%)
  local copies, waits for them, and re-layouts  4.5 us (2%)
  other arithmetic  3.87 us (1%)
    psum x1, waiting for transfers between devices, local(): lax.psum(weight_term, ('row', 'col')) * (1.0 / math.sqrt(total_nodes))  121 us
    reduce_scatter x1, waiting for transfers between devices, local(): lax.psum_scatter(col_partial, 'row', scatter_dimension=0, tiled=True)  63 us
    all_gather x1, waiting for transfers between devices, local(): lax.all_gather(features, 'row', axis=0, tiled=True)  38.4 us
    reduce_scatter x1, waiting for transfers between devices, local(): lax.psum_scatter(row_partial, 'col', scatter_dimension=0, tiled=True)  10.3 us
  transfers between devices with their start and end apart: 4, of which 4 were waited for; matrix products, arithmetic and copies ran while one was open for 3% of the time, Pallas kernels for 0%

commit v1 on v0

v1 whole, which is shorter than its diff:
```python
import math

import jax
import jax.numpy as jnp
from jax import lax
from jax.sharding import PartitionSpec as P


def swap(x, axis, bit):
    return lax.ppermute(x, axis, [(i, i ^ bit) for i in range(lax.axis_size(axis))])


def bits(count):
    return [1 << k for k in range(count.bit_length() - 1)]


def tree_sum(terms):
    while len(terms) > 1:
        terms = [a + b for a, b in zip(terms[::2], terms[1::2])]
    return terms[0]


def gather_panel(features, row_count):
    depth = row_count // 4
    panel = jnp.concatenate([features] + [swap(features, "row", 4 * k) for k in range(1, depth)])
    panel = jnp.concatenate([panel, swap(panel, "row", 2)])
    return jnp.concatenate([panel, swap(panel, "row", 1)])


def scatter_sum(dense, row_panel, row_count):
    depth = row_count // 4
    half = row_count // 2
    spec = "bpij,bif->pjf"
    theirs = jnp.einsum(spec, dense[:, half:], row_panel, preferred_element_type=jnp.float32)
    theirs = swap(theirs.astype(jnp.bfloat16), "row", 1)
    mine = jnp.einsum(spec, dense[:, :half], row_panel, preferred_element_type=jnp.float32)
    mine = mine + theirs
    mine = mine[:depth] + swap(mine[depth:].astype(jnp.bfloat16), "row", 2)
    sent = mine[1:].astype(jnp.bfloat16)
    got = [swap(sent[k - 1], "row", 4 * k) for k in range(1, depth)]
    return tree_sum([mine[0]] + [g.astype(jnp.float32) for g in got])


def total_sum(term, row, row_count, col_count):
    depth = row_count // 4
    rows = term.shape[0] // 2
    core = row % 2
    pair = term.reshape(2, rows, -1)
    half = lax.dynamic_index_in_dim(pair, core, 0, False) + swap(
        lax.dynamic_index_in_dim(pair, 1 - core, 0, False), "row", 1
    )
    for bit in bits(col_count):
        sent = half.astype(jnp.bfloat16)
        half = sent.astype(jnp.float32) + swap(sent, "col", bit).astype(jnp.float32)
    sent = half.astype(jnp.bfloat16)
    terms = [sent] + [swap(sent, "row", 4 * k) for k in range(1, depth)]
    half = tree_sum([t.astype(jnp.float32) for t in terms])
    sent = half.astype(jnp.bfloat16)
    half = sent.astype(jnp.float32) + swap(sent, "row", 2).astype(jnp.float32)
    other = swap(half, "row", 1)
    low = jnp.where(core == 0, half, other)
    high = jnp.where(core == 0, other, half)
    return jnp.concatenate([low, high])


def local(features, weight, grad_out, tiles, slots):
    tile_blocks = tiles[0, 0]
    tile_slots = slots[0, 0]
    own_rows, width = features.shape
    side = tile_blocks.shape[1]
    row_count = lax.axis_size("row")
    col_count = lax.axis_size("col")
    row = lax.axis_index("row")
    col = lax.axis_index("col")
    relative = (tile_slots % row_count) ^ row
    position = (relative % 2) * (row_count // 2) + (relative // 2 % 2) * (row_count // 4) + relative // 4
    position = ((tile_slots // row_count) ^ col) * row_count + position
    dense = (
        jnp.zeros((col_count * row_count, side, side), jnp.bfloat16).at[position].set(tile_blocks)
    )
    dense = dense.reshape(col_count, row_count, side, side)

    panel = gather_panel(features, row_count).reshape(row_count, side, width)
    partial = jnp.einsum("bpij,pjf->bif", dense, panel, preferred_element_type=jnp.float32)
    cotangent = grad_out[None]
    for bit in bits(col_count):
        cotangent = jnp.concatenate([cotangent, swap(cotangent, "col", bit)])
        got = swap(partial.astype(jnp.bfloat16), "col", bit)
        got = got.reshape(-1, 2, bit, side, width)[:, ::-1].reshape(partial.shape)
        partial = partial + got
    aggregated = partial.astype(jnp.bfloat16).reshape(-1, width)
    cotangent = cotangent.reshape(-1, width)
    pre = jnp.dot(aggregated, weight, preferred_element_type=jnp.float32)
    sigmoid_pre = jax.nn.sigmoid(pre)
    activated = (pre[:own_rows] * sigmoid_pre[:own_rows]).astype(jnp.bfloat16)
    grad_pre = (
        cotangent.astype(jnp.float32) * sigmoid_pre * (1.0 + pre * (1.0 - sigmoid_pre))
    ).astype(jnp.bfloat16)
    weight_term = jnp.dot(
        aggregated[:own_rows].T, grad_pre[:own_rows], preferred_element_type=jnp.float32
    )
    grad_agg = jnp.dot(grad_pre, weight.T, preferred_element_type=jnp.float32).astype(jnp.bfloat16)
    grad_in = scatter_sum(dense, grad_agg.reshape(col_count, side, width), row_count)
    total_nodes = own_rows * row_count * col_count
    grad_weight = total_sum(weight_term, row, row_count, col_count) * (1.0 / math.sqrt(total_nodes))
    return (activated, grad_weight, grad_in.astype(jnp.bfloat16))


def solution(mesh):
    in_specs = (
        P(("row", "col"), None),
        P(),
        P(("row", "col"), None),
        P("row", "col", None, None, None),
        P("row", "col", None),
    )
    out_specs = (P(("row", "col"), None), P(), P(("row", "col"), None))
    return jax.shard_map(local, mesh=mesh, in_specs=in_specs, out_specs=out_specs, check_vma=False)
```

time: 269 us -> 68.3 us (0.25)
  waiting for transfers between devices: 234 us -> 34 us
  starting transfers between devices: 0.16 us -> 21.2 us
  between operations: 13.8 us -> 0.88 us
  matrix products: 7.9 us -> 1.78 us
  blocking collectives: 4.94 us -> 0 us
    psum x1 -> x0, waiting for transfers between devices: 121 us -> none  [local(): lax.psum(weight_term, ('row', 'col')) * (1.0 / math.sqrt(total_nodes))]
    reduce_scatter x2 -> x0, waiting for transfers between devices: 73.3 us -> none  [the longest x1 63 us: local(): lax.psum_scatter(col_partial, 'row', scatter_dimension=0, tiled=True)]
    all_gather x1 -> x0, waiting for transfers between devices: 38.4 us -> none  [local(): lax.all_gather(features, 'row', axis=0, tiled=True)]
    ppermute x0 -> x19, waiting for transfers between devices: none -> 34 us  [swap(): lax.ppermute(x, axis, [(i, i ^ bit) for i in range(lax.axis_size(axis))])]
    ppermute x0 -> x19, starting transfers between devices: none -> 21.2 us  [swap(): lax.ppermute(x, axis, [(i, i ^ bit) for i in range(lax.axis_size(axis))])]
    all_gather x1 -> x0, blocking collectives: 4.94 us -> none  [local(): lax.all_gather(grad_agg, 'col', axis=0, tiled=True)]
    dot_general x3 -> x4, matrix products: 5.97 us -> 1.29 us  [the longest x1 0.44 us: local(): jnp.einsum('bpij,pjf->bif', dense, panel, preferred_element_type=jnp.floa...]
    unnamed x4 -> x12, local copies, waits for them, and re-layouts: 0.01 us -> 4.08 us
  transfers between devices with their start and end apart: 4 -> 19, of which waited for: 4 -> 12; matrix products, arithmetic and copies ran while one was open for 3% -> 13% of each run, Pallas kernels for 0% -> 0%
where the time goes in v1:
time: 68.3 us; the launch traced here: 68 us
  waiting for transfers between devices  34 us (50%)
  starting transfers between devices  21.2 us (31%)
  local copies, waits for them, and re-layouts  6.96 us (10%)
  other arithmetic  3.18 us (5%)
  matrix products  1.78 us (3%)
  between operations  0.88 us (1%)
    ppermute x19, waiting for transfers between devices, swap(): lax.ppermute(x, axis, [(i, i ^ bit) for i in range(lax.axis_size(axis))])  34 us
    ppermute x19, starting transfers between devices, swap(): lax.ppermute(x, axis, [(i, i ^ bit) for i in range(lax.axis_size(axis))])  21.2 us
    unnamed x12, local copies, waits for them, and re-layouts  4.08 us
    scatter x1, local copies, waits for them, and re-layouts, local(): jnp.zeros((col_count * row_count, side, side), jnp.bfloat16).at[position]  1.69 us
  transfers between devices with their start and end apart: 19, of which 12 were waited for; matrix products, arithmetic and copies ran while one was open for 13% of the time, Pallas kernels for 0%

profile of v1, /device:TPU:0, one launch (start us, length us, event | category | flops | bytes accessed | tf_op | source)
XLA Modules:
  0.0 68.0 jit_solution(11501263798545597150)
XLA Ops:
  0.7 3.1 %collective-permute-start = (bf16[128,256]{1,0:T(8,128)(2,1)}, bf16[128,256]{1,0:T(8,128)(2,1)S(1)}, u32[]{:S(2)}, u32[]{:S(2)}) collective-permute-start(bf16[128,256]{1,0:T(8,128)(2,1)} %param.5), channel_id=1, source_target_pairs={{0,8},{2,10},{4,12},{6,14},{8,0},{10,2},{12,4},{14,6},{16,24},{18,... | collective-permute-start | bytes 196616 | tf_op jit(solution)/shard_map/ppermute | solution.py:10
  3.7 2.6 %collective-permute-start.1 = (bf16[128,256]{1,0:T(8,128)(2,1)}, bf16[128,256]{1,0:T(8,128)(2,1)S(1)}, u32[]{:S(2)}, u32[]{:S(2)}) collective-permute-start(bf16[128,256]{1,0:T(8,128)(2,1)} %param.5), channel_id=1, source_target_pairs={{0,16},{2,18},{4,20},{6,22},{8,24},{10,26},{12,28},{14,30},{16,0},... | collective-permute-start | bytes 196616 | tf_op jit(solution)/shard_map/ppermute | solution.py:10
  6.3 1.5 %constant_dynamic-update-slice_fusion.4 = (bf16[1024,256]{1,0:T(8,128)(2,1)}, bf16[2048,256]{1,0:T(8,128)(2,1)S(1)}) fusion(bf16[128,256]{1,0:T(8,128)(2,1)} %param.5), kind=kLoop, calls=%fused_computation.41 | loop fusion | bytes 196608
  7.9 3.4 %collective-permute-done.1 = bf16[128,256]{1,0:T(8,128)(2,1)S(1)} collective-permute-done((bf16[128,256]{1,0:T(8,128)(2,1)}, bf16[128,256]{1,0:T(8,128)(2,1)S(1)}, u32[]{:S(2)}, u32[]{:S(2)}) %collective-permute-start.1) | collective-permute-done | bytes 65568 | tf_op jit(solution)/shard_map/ppermute | solution.py:10
  11.2 1.4 %collective-permute-done.2 = bf16[128,256]{1,0:T(8,128)(2,1)S(1)} collective-permute-done((bf16[128,256]{1,0:T(8,128)(2,1)}, bf16[128,256]{1,0:T(8,128)(2,1)S(1)}, u32[]{:S(2)}, u32[]{:S(2)}) %collective-permute-start.2) | collective-permute-done | bytes 65568 | tf_op jit(solution)/shard_map/ppermute | solution.py:10
  12.7 1.6 %collective-permute-start.3 = (bf16[512,256]{1,0:T(8,128)(2,1)S(1)}, bf16[512,256]{1,0:T(8,128)(2,1)S(1)}, u32[]{:S(2)}, u32[]{:S(2)}) collective-permute-start(bf16[512,256]{1,0:T(8,128)(2,1)S(1)} %pad_maximum_fusion), channel_id=1, source_target_pairs={{0,4},{2,6},{4,0},{6,2},{8,12},{10,14},{12,8},{14,10},{16,20},{18,... | collective-permute-start | bytes 786440 | tf_op jit(solution)/shard_map/ppermute | solution.py:10
  16.1 3.0 %collective-permute-done.3 = bf16[512,256]{1,0:T(8,128)(2,1)S(1)} collective-permute-done((bf16[512,256]{1,0:T(8,128)(2,1)S(1)}, bf16[512,256]{1,0:T(8,128)(2,1)S(1)}, u32[]{:S(2)}, u32[]{:S(2)}) %collective-permute-start.3) | collective-permute-done | bytes 262176 | tf_op jit(solution)/shard_map/ppermute | solution.py:10
  19.9 1.5 %collective-permute-start.6 = (bf16[1,128,256]{2,1,0:T(8,128)(2,1)}, bf16[1,128,256]{2,1,0:T(8,128)(2,1)}, u32[]{:S(2)}, u32[]{:S(2)}) collective-permute-start(bf16[1,128,256]{2,1,0:T(8,128)(2,1)} %bitcast.12), channel_id=1, source_target_pairs={{0,1},{1,0},{2,3},{3,2},{4,5},{5,4},{6,7},{7,6},{8,9},{9,8},{10,11... | collective-permute-start | bytes 196616 | tf_op jit(solution)/shard_map/ppermute | solution.py:10
  22.3 1.7 %scatter_fusion = bf16[32,128,128]{2,1,0:T(8,128)(2,1)S(1)} fusion(bf16[32,128,128]{2,1,0:T(8,128)(2,1)S(1)} %broadcast_in_dim.7, s32[24]{0:T(128)S(1)} %fusion.15, bf16[24,128,128]{2,1,0:T(8,128)(2,1)S(1)} %bitcast.91), kind=kCustom, calls=%fused_computation | custom fusion | bytes 2359392 | tf_op jit(solution)/shard_map/scatter | solution.py:79
  25.1 0.9 %pad_maximum_fusion.1 = bf16[2,128,256]{2,1,0:T(8,128)(2,1)S(1)} fusion(bf16[1,128,256]{2,1,0:T(8,128)(2,1)} %collective-permute-done.6, bf16[1,128,256]{2,1,0:T(8,128)(2,1)} %bitcast.12), kind=kLoop, calls=%fused_computation.22 | loop fusion | flops 65536 | bytes 262144 | tf_op jit(solution)/shard_map/concatenate | solution.py:87
  26.0 4.2 %collective-permute-done.5 = bf16[2,128,256]{2,1,0:T(8,128)(2,1)S(1)} collective-permute-done((bf16[2,128,256]{2,1,0:T(8,128)(2,1)S(1)}, bf16[2,128,256]{2,1,0:T(8,128)(2,1)S(1)}, u32[]{:S(2)}, u32[]{:S(2)}) %collective-permute-start.5) | collective-permute-done | bytes 131104 | tf_op jit(solution)/shard_map/ppermute | solution.py:10
  31.0 1.3 %collective-permute-done.7 = f32[128,256]{1,0:T(8,128)S(1)} collective-permute-done((f32[128,256]{1,0:T(8,128)S(1)}, f32[128,256]{1,0:T(8,128)S(1)}, u32[]{:S(2)}, u32[]{:S(2)}) %collective-permute-start.7) | collective-permute-done | bytes 131104 | tf_op jit(solution)/shard_map/ppermute | solution.py:10
  33.1 3.5 %collective-permute-done.8 = bf16[128,256]{1,0:T(8,128)(2,1)S(1)} collective-permute-done((bf16[128,256]{1,0:T(8,128)(2,1)S(1)}, bf16[128,256]{1,0:T(8,128)(2,1)S(1)}, u32[]{:S(2)}, u32[]{:S(2)}) %collective-permute-start.8) | collective-permute-done | bytes 65568 | tf_op jit(solution)/shard_map/ppermute | solution.py:10
  36.7 2.1 %collective-permute-start.10 = (bf16[128,256]{1,0:T(8,128)(2,1)S(1)}, bf16[128,256]{1,0:T(8,128)(2,1)S(1)}, u32[]{:S(2)}, u32[]{:S(2)}) collective-permute-start(bf16[128,256]{1,0:T(8,128)(2,1)S(1)} %add_convert_fusion.2), channel_id=1, source_target_pairs={{0,16},{2,18},{4,20},{6,22},{8,24},{10,26},{12,28},{14,30},{16,0},... | collective-permute-start | bytes 196616 | tf_op jit(solution)/shard_map/ppermute | solution.py:10
  38.7 1.0 %collective-permute-start.11 = (bf16[128,256]{1,0:T(8,128)(2,1)S(1)}, bf16[128,256]{1,0:T(8,128)(2,1)S(1)}, u32[]{:S(2)}, u32[]{:S(2)}) collective-permute-start(bf16[128,256]{1,0:T(8,128)(2,1)S(1)} %add_convert_fusion.2), channel_id=1, source_target_pairs={{0,24},{2,26},{4,28},{6,30},{8,16},{10,18},{12,20},{14,22},{16,8},... | collective-permute-start | bytes 196616 | tf_op jit(solution)/shard_map/ppermute | solution.py:10
  40.7 2.8 %collective-permute-done.10 = bf16[128,256]{1,0:T(8,128)(2,1)S(1)} collective-permute-done((bf16[128,256]{1,0:T(8,128)(2,1)S(1)}, bf16[128,256]{1,0:T(8,128)(2,1)S(1)}, u32[]{:S(2)}, u32[]{:S(2)}) %collective-permute-start.10) | collective-permute-done | bytes 65568 | tf_op jit(solution)/shard_map/ppermute | solution.py:10
  43.4 1.4 %collective-permute-done.11 = bf16[128,256]{1,0:T(8,128)(2,1)S(1)} collective-permute-done((bf16[128,256]{1,0:T(8,128)(2,1)S(1)}, bf16[128,256]{1,0:T(8,128)(2,1)S(1)}, u32[]{:S(2)}, u32[]{:S(2)}) %collective-permute-start.11) | collective-permute-done | bytes 65568 | tf_op jit(solution)/shard_map/ppermute | solution.py:10
  44.9 1.6 %collective-permute-start.12 = (bf16[128,256]{1,0:T(8,128)(2,1)S(1)}, bf16[128,256]{1,0:T(8,128)(2,1)S(1)}, u32[]{:S(2)}, u32[]{:S(2)}) collective-permute-start(bf16[128,256]{1,0:T(8,128)(2,1)S(1)} %add_convert_fusion.1), channel_id=1, source_target_pairs={{0,4},{2,6},{4,0},{6,2},{8,12},{10,14},{12,8},{14,10},{16,20},{18,... | collective-permute-start | bytes 196616 | tf_op jit(solution)/shard_map/ppermute | solution.py:10
  46.4 2.8 %collective-permute-done.12 = bf16[128,256]{1,0:T(8,128)(2,1)S(1)} collective-permute-done((bf16[128,256]{1,0:T(8,128)(2,1)S(1)}, bf16[128,256]{1,0:T(8,128)(2,1)S(1)}, u32[]{:S(2)}, u32[]{:S(2)}) %collective-permute-start.12) | collective-permute-done | bytes 65568 | tf_op jit(solution)/shard_map/ppermute | solution.py:10
  49.7 1.6 %collective-permute-start.15 = (bf16[4,128,256]{2,1,0:T(8,128)(2,1)S(1)}, bf16[4,128,256]{2,1,0:T(8,128)(2,1)S(1)}, u32[]{:S(2)}, u32[]{:S(2)}) collective-permute-start(bf16[4,128,256]{2,1,0:T(8,128)(2,1)S(1)} %slice.87), channel_id=1, source_target_pairs={{0,4},{2,6},{4,0},{6,2},{8,12},{10,14},{12,8},{14,10},{16,20},{18,... | collective-permute-start | bytes 786440 | tf_op jit(solution)/shard_map/ppermute | solution.py:10
  51.9 6.5 %collective-permute-done.15 = bf16[4,128,256]{2,1,0:T(8,128)(2,1)S(1)} collective-permute-done((bf16[4,128,256]{2,1,0:T(8,128)(2,1)S(1)}, bf16[4,128,256]{2,1,0:T(8,128)(2,1)S(1)}, u32[]{:S(2)}, u32[]{:S(2)}) %collective-permute-start.15) | collective-permute-done | bytes 262176 | tf_op jit(solution)/shard_map/ppermute | solution.py:10
  58.7 2.5 %collective-permute-start.17 = (bf16[128,256]{1,0:T(8,128)(2,1)S(1)}, bf16[128,256]{1,0:T(8,128)(2,1)S(1)}, u32[]{:S(2)}, u32[]{:S(2)}) collective-permute-start(bf16[128,256]{1,0:T(8,128)(2,1)S(1)} %get-tuple-element.7), channel_id=1, source_target_pairs={{0,16},{2,18},{4,20},{6,22},{8,24},{10,26},{12,28},{14,30},{16,0},... | collective-permute-start | bytes 196616 | tf_op jit(solution)/shard_map/ppermute | solution.py:10
  61.2 1.8 %collective-permute-start.18 = (bf16[128,256]{1,0:T(8,128)(2,1)S(1)}, bf16[128,256]{1,0:T(8,128)(2,1)S(1)}, u32[]{:S(2)}, u32[]{:S(2)}) collective-permute-start(bf16[128,256]{1,0:T(8,128)(2,1)S(1)} %get-tuple-element.6), channel_id=1, source_target_pairs={{0,24},{2,26},{4,28},{6,30},{8,16},{10,18},{12,20},{14,22},{16,8},... | collective-permute-start | bytes 196616 | tf_op jit(solution)/shard_map/ppermute | solution.py:10
  63.8 2.8 %collective-permute-done.17 = bf16[128,256]{1,0:T(8,128)(2,1)S(1)} collective-permute-done((bf16[128,256]{1,0:T(8,128)(2,1)S(1)}, bf16[128,256]{1,0:T(8,128)(2,1)S(1)}, u32[]{:S(2)}, u32[]{:S(2)}) %collective-permute-start.17) | collective-permute-done | bytes 65568 | tf_op jit(solution)/shard_map/ppermute | solution.py:10
  (54 shorter events, 10.5 us)
Async XLA Ops:
  0.6 29.8 %copy-start = (bf16[256,256]{1,0:T(8,128)(2,1)S(1)}, bf16[256,256]{1,0:T(8,128)(2,1)}, u32[]{:S(2)}) copy-start(bf16[256,256]{1,0:T(8,128)(2,1)} %param.6) | copy-start | bytes 393220
  0.6 12.0 %copy-start.2 = (bf16[128,256]{1,0:T(8,128)(2,1)S(1)}, bf16[128,256]{1,0:T(8,128)(2,1)}, u32[]{:S(2)}) copy-start(bf16[128,256]{1,0:T(8,128)(2,1)} %param.5) | copy-start | bytes 196612
  0.7 7.2 %collective-permute-start = (bf16[128,256]{1,0:T(8,128)(2,1)}, bf16[128,256]{1,0:T(8,128)(2,1)S(1)}, u32[]{:S(2)}, u32[]{:S(2)}) collective-permute-start(bf16[128,256]{1,0:T(8,128)(2,1)} %param.5), channel_id=1, source_target_pairs={{0,8},{2,10},{4,12},{6,14},{8,0},{10,2},{12,4},{14,6},{16,24},{18,... | collective-permute-start | bytes 196616 | tf_op jit(solution)/shard_map/ppermute | solution.py:10
  3.7 7.5 %collective-permute-start.1 = (bf16[128,256]{1,0:T(8,128)(2,1)}, bf16[128,256]{1,0:T(8,128)(2,1)S(1)}, u32[]{:S(2)}, u32[]{:S(2)}) collective-permute-start(bf16[128,256]{1,0:T(8,128)(2,1)} %param.5), channel_id=1, source_target_pairs={{0,16},{2,18},{4,20},{6,22},{8,24},{10,26},{12,28},{14,30},{16,0},... | collective-permute-start | bytes 196616 | tf_op jit(solution)/shard_map/ppermute | solution.py:10
  6.3 6.3 %collective-permute-start.2 = (bf16[128,256]{1,0:T(8,128)(2,1)}, bf16[128,256]{1,0:T(8,128)(2,1)S(1)}, u32[]{:S(2)}, u32[]{:S(2)}) collective-permute-start(bf16[128,256]{1,0:T(8,128)(2,1)} %param.5), channel_id=1, source_target_pairs={{0,24},{2,26},{4,28},{6,30},{8,16},{10,18},{12,20},{14,22},{16,8},... | collective-permute-start | bytes 196616 | tf_op jit(solution)/shard_map/ppermute | solution.py:10
  12.7 6.5 %collective-permute-start.3 = (bf16[512,256]{1,0:T(8,128)(2,1)S(1)}, bf16[512,256]{1,0:T(8,128)(2,1)S(1)}, u32[]{:S(2)}, u32[]{:S(2)}) collective-permute-start(bf16[512,256]{1,0:T(8,128)(2,1)S(1)} %pad_maximum_fusion), channel_id=1, source_target_pairs={{0,4},{2,6},{4,0},{6,2},{8,12},{10,14},{12,8},{14,10},{16,20},{18,... | collective-permute-start | bytes 786440 | tf_op jit(solution)/shard_map/ppermute | solution.py:10
  19.1 3.2 %copy-start.1 = (bf16[1,1,24,128,128]{4,3,2,1,0:T(8,128)(2,1)S(1)}, bf16[1,1,24,128,128]{4,3,2,1,0:T(8,128)(2,1)}, u32[]{:S(2)}) copy-start(bf16[1,1,24,128,128]{4,3,2,1,0:T(8,128)(2,1)} %param.8) | copy-start | bytes 2359300
  19.9 4.2 %collective-permute-start.4 = (bf16[1024,256]{1,0:T(8,128)(2,1)}, bf16[1024,256]{1,0:T(8,128)(2,1)S(1)}, u32[]{:S(2)}, u32[]{:S(2)}) collective-permute-start(bf16[1024,256]{1,0:T(8,128)(2,1)} %get-tuple-element.12), channel_id=1, source_target_pairs={{0,2},{2,0},{4,6},{6,4},{8,10},{10,8},{12,14},{14,12},{16,18},{18,... | collective-permute-start | bytes 1572872 | tf_op jit(solution)/shard_map/ppermute | solution.py:10
  19.9 5.2 %collective-permute-start.6 = (bf16[1,128,256]{2,1,0:T(8,128)(2,1)}, bf16[1,128,256]{2,1,0:T(8,128)(2,1)}, u32[]{:S(2)}, u32[]{:S(2)}) collective-permute-start(bf16[1,128,256]{2,1,0:T(8,128)(2,1)} %bitcast.12), channel_id=1, source_target_pairs={{0,1},{1,0},{2,3},{3,2},{4,5},{5,4},{6,7},{7,6},{8,9},{9,8},{10,11... | collective-permute-start | bytes 196616 | tf_op jit(solution)/shard_map/ppermute | solution.py:10
  21.4 0.7 copy-start.3
  24.5 5.7 %collective-permute-start.5 = (bf16[2,128,256]{2,1,0:T(8,128)(2,1)S(1)}, bf16[2,128,256]{2,1,0:T(8,128)(2,1)S(1)}, u32[]{:S(2)}, u32[]{:S(2)}) collective-permute-start(bf16[2,128,256]{2,1,0:T(8,128)(2,1)S(1)} %get-tuple-element.22), channel_id=1, source_target_pairs={{0,1},{1,0},{2,3},{3,2},{4,5},{5,4},{6,7},{7,6},{8,9},{9,8},{10,11... | collective-permute-start | bytes 393224 | tf_op jit(solution)/shard_map/ppermute | solution.py:10
  30.9 1.4 %collective-permute-start.7 = (f32[128,256]{1,0:T(8,128)S(1)}, f32[128,256]{1,0:T(8,128)S(1)}, u32[]{:S(2)}, u32[]{:S(2)}) collective-permute-start(f32[128,256]{1,0:T(8,128)S(1)} %dynamic-slice_bitcast_fusion), channel_id=1, source_target_pairs={{0,2},{2,0},{4,6},{6,4},{8,10},{10,8},{12,14},{14,12},{16,18},{18,... | collective-permute-start | bytes 393224 | tf_op jit(solution)/shard_map/ppermute | solution.py:10
  32.3 4.3 %collective-permute-start.8 = (bf16[128,256]{1,0:T(8,128)(2,1)S(1)}, bf16[128,256]{1,0:T(8,128)(2,1)S(1)}, u32[]{:S(2)}, u32[]{:S(2)}) collective-permute-start(bf16[128,256]{1,0:T(8,128)(2,1)S(1)} %fusion.7), channel_id=1, source_target_pairs={{0,1},{1,0},{2,3},{3,2},{4,5},{5,4},{6,7},{7,6},{8,9},{9,8},{10,11... | collective-permute-start | bytes 196616 | tf_op jit(solution)/shard_map/ppermute | solution.py:10
  36.7 6.8 %collective-permute-start.10 = (bf16[128,256]{1,0:T(8,128)(2,1)S(1)}, bf16[128,256]{1,0:T(8,128)(2,1)S(1)}, u32[]{:S(2)}, u32[]{:S(2)}) collective-permute-start(bf16[128,256]{1,0:T(8,128)(2,1)S(1)} %add_convert_fusion.2), channel_id=1, source_target_pairs={{0,16},{2,18},{4,20},{6,22},{8,24},{10,26},{12,28},{14,30},{16,0},... | collective-permute-start | bytes 196616 | tf_op jit(solution)/shard_map/ppermute | solution.py:10
  38.7 6.1 %collective-permute-start.11 = (bf16[128,256]{1,0:T(8,128)(2,1)S(1)}, bf16[128,256]{1,0:T(8,128)(2,1)S(1)}, u32[]{:S(2)}, u32[]{:S(2)}) collective-permute-start(bf16[128,256]{1,0:T(8,128)(2,1)S(1)} %add_convert_fusion.2), channel_id=1, source_target_pairs={{0,24},{2,26},{4,28},{6,30},{8,16},{10,18},{12,20},{14,22},{16,8},... | collective-permute-start | bytes 196616 | tf_op jit(solution)/shard_map/ppermute | solution.py:10
  39.8 5.1 %collective-permute-start.9 = (bf16[128,256]{1,0:T(8,128)(2,1)S(1)}, bf16[128,256]{1,0:T(8,128)(2,1)S(1)}, u32[]{:S(2)}, u32[]{:S(2)}) collective-permute-start(bf16[128,256]{1,0:T(8,128)(2,1)S(1)} %add_convert_fusion.2), channel_id=1, source_target_pairs={{0,8},{2,10},{4,12},{6,14},{8,0},{10,2},{12,4},{14,6},{16,24},{18,... | collective-permute-start | bytes 196616 | tf_op jit(solution)/shard_map/ppermute | solution.py:10
  40.6 8.7 %collective-permute-start.14 = (bf16[8,128,256]{2,1,0:T(8,128)(2,1)S(1)}, bf16[8,128,256]{2,1,0:T(8,128)(2,1)S(1)}, u32[]{:S(2)}, u32[]{:S(2)}) collective-permute-start(bf16[8,128,256]{2,1,0:T(8,128)(2,1)S(1)} %fusion), channel_id=1, source_target_pairs={{0,2},{2,0},{4,6},{6,4},{8,10},{10,8},{12,14},{14,12},{16,18},{18,... | collective-permute-start | bytes 1572872 | tf_op jit(solution)/shard_map/ppermute | solution.py:10
  44.9 4.3 %collective-permute-start.12 = (bf16[128,256]{1,0:T(8,128)(2,1)S(1)}, bf16[128,256]{1,0:T(8,128)(2,1)S(1)}, u32[]{:S(2)}, u32[]{:S(2)}) collective-permute-start(bf16[128,256]{1,0:T(8,128)(2,1)S(1)} %add_convert_fusion.1), channel_id=1, source_target_pairs={{0,4},{2,6},{4,0},{6,2},{8,12},{10,14},{12,8},{14,10},{16,20},{18,... | collective-permute-start | bytes 196616 | tf_op jit(solution)/shard_map/ppermute | solution.py:10
  49.2 2.7 %collective-permute-start.13 = (f32[128,256]{1,0:T(8,128)S(1)}, f32[128,256]{1,0:T(8,128)S(1)}, u32[]{:S(2)}, u32[]{:S(2)}) collective-permute-start(f32[128,256]{1,0:T(8,128)S(1)} %convert_add_fusion.1), channel_id=1, source_target_pairs={{0,2},{2,0},{4,6},{6,4},{8,10},{10,8},{12,14},{14,12},{16,18},{18,... | collective-permute-start | bytes 393224 | tf_op jit(solution)/shard_map/ppermute | solution.py:10
  49.7 8.8 %collective-permute-start.15 = (bf16[4,128,256]{2,1,0:T(8,128)(2,1)S(1)}, bf16[4,128,256]{2,1,0:T(8,128)(2,1)S(1)}, u32[]{:S(2)}, u32[]{:S(2)}) collective-permute-start(bf16[4,128,256]{2,1,0:T(8,128)(2,1)S(1)} %slice.87), channel_id=1, source_target_pairs={{0,4},{2,6},{4,0},{6,2},{8,12},{10,14},{12,8},{14,10},{16,20},{18,... | collective-permute-start | bytes 786440 | tf_op jit(solution)/shard_map/ppermute | solution.py:10
  58.6 5.2 %collective-permute-start.16 = (bf16[128,256]{1,0:T(8,128)(2,1)S(1)}, bf16[128,256]{1,0:T(8,128)(2,1)S(1)}, u32[]{:S(2)}, u32[]{:S(2)}) collective-permute-start(bf16[128,256]{1,0:T(8,128)(2,1)S(1)} %get-tuple-element.5), channel_id=1, source_target_pairs={{0,8},{2,10},{4,12},{6,14},{8,0},{10,2},{12,4},{14,6},{16,24},{18,... | collective-permute-start | bytes 196616 | tf_op jit(solution)/shard_map/ppermute | solution.py:10
  58.7 7.9 %collective-permute-start.17 = (bf16[128,256]{1,0:T(8,128)(2,1)S(1)}, bf16[128,256]{1,0:T(8,128)(2,1)S(1)}, u32[]{:S(2)}, u32[]{:S(2)}) collective-permute-start(bf16[128,256]{1,0:T(8,128)(2,1)S(1)} %get-tuple-element.7), channel_id=1, source_target_pairs={{0,16},{2,18},{4,20},{6,22},{8,24},{10,26},{12,28},{14,30},{16,0},... | collective-permute-start | bytes 196616 | tf_op jit(solution)/shard_map/ppermute | solution.py:10
  61.2 6.2 %collective-permute-start.18 = (bf16[128,256]{1,0:T(8,128)(2,1)S(1)}, bf16[128,256]{1,0:T(8,128)(2,1)S(1)}, u32[]{:S(2)}, u32[]{:S(2)}) collective-permute-start(bf16[128,256]{1,0:T(8,128)(2,1)S(1)} %get-tuple-element.6), channel_id=1, source_target_pairs={{0,24},{2,26},{4,28},{6,30},{8,16},{10,18},{12,20},{14,22},{16,8},... | collective-permute-start | bytes 196616 | tf_op jit(solution)/shard_map/ppermute | solution.py:10

commit v2 on v0

v2 whole, which is shorter than its diff:
```python
import math

import jax
import jax.numpy as jnp
from jax import lax
from jax.sharding import PartitionSpec as P


def swap(x, axis, bit):
    return lax.ppermute(x, axis, [(i, i ^ bit) for i in range(lax.axis_size(axis))])


def bits(count):
    return [1 << k for k in range(count.bit_length() - 1)]


def tree_sum(terms):
    while len(terms) > 1:
        terms = [a + b for a, b in zip(terms[::2], terms[1::2])]
    return terms[0]


def rounded(x):
    return lax.optimization_barrier(x.astype(jnp.bfloat16))


def local(features, weight, grad_out, tiles, slots):
    tile_blocks = tiles[0, 0]
    tile_slots = slots[0, 0]
    own_rows, width = features.shape
    side = tile_blocks.shape[1]
    row_count = lax.axis_size("row")
    col_count = lax.axis_size("col")
    row = lax.axis_index("row")
    col = lax.axis_index("col")
    core = row & 1
    depth = row_count // 4
    f32 = jnp.float32
    bf16 = jnp.bfloat16

    relative = (tile_slots % row_count) ^ row
    position = (relative % 2) * (row_count // 2) + (relative // 2 % 2) * depth + relative // 4
    position = tile_slots // row_count * row_count + position
    dense = jnp.zeros((col_count * row_count, side, side), bf16).at[position].set(tile_blocks)
    cotangent = grad_out
    for bit in bits(col_count):
        got = swap(cotangent, "col", bit)
        low = jnp.where(col & bit == 0, cotangent, got)
        high = jnp.where(col & bit == 0, got, cotangent)
        cotangent = jnp.concatenate([low, high])
    panel = jnp.concatenate([features] + [swap(features, "row", 4 * k) for k in range(1, depth)])
    panel, dense, cotangent = lax.optimization_barrier((panel, dense, cotangent))
    dense = dense.reshape(col_count, 4, depth, side, side)

    def forward(quarter, block):
        return jnp.einsum(
            "bpij,pjf->bif",
            dense[:, quarter],
            block.reshape(depth, side, width),
            preferred_element_type=f32,
        )

    def backward(quarter, row_panel):
        return jnp.einsum(
            "bpij,bif->pjf", dense[:, quarter], row_panel, preferred_element_type=f32
        )

    panel_x = swap(panel, "row", 2)
    panel_c = swap(panel, "row", 1)
    partial = forward(0, panel) + forward(2, panel_c)
    panel_xc = swap(panel_x, "row", 1)
    partial = partial + forward(1, panel_x) + forward(3, panel_xc)
    for bit in bits(col_count):
        sent = rounded(partial)
        partial = sent.astype(f32) + swap(sent, "col", bit).astype(f32)
    aggregated = partial.astype(bf16).reshape(-1, width)
    pre = jnp.dot(aggregated, weight, preferred_element_type=f32)
    sigmoid_pre = jax.nn.sigmoid(pre)
    grad_pre = (
        cotangent.astype(f32) * sigmoid_pre * (1.0 + pre * (1.0 - sigmoid_pre))
    ).astype(bf16)
    grad_agg = jnp.dot(grad_pre, weight.T, preferred_element_type=f32).astype(bf16)
    row_panel = grad_agg.reshape(col_count, side, width)

    sent_xc = backward(3, row_panel).astype(bf16)
    sent_xc, aggregated = lax.optimization_barrier((sent_xc, aggregated))
    got_xc = swap(sent_xc, "row", 1)
    term = jnp.dot(aggregated.T, grad_pre, preferred_element_type=f32)
    got_c = swap(backward(2, row_panel).astype(bf16), "row", 1)

    sent_x = (backward(1, row_panel) + got_xc.astype(f32)).astype(bf16)
    sent_x, term = lax.optimization_barrier((sent_x, term))
    got_x = swap(sent_x, "row", 2)
    mine = backward(0, row_panel) + got_c.astype(f32)

    pair = term.reshape(2, term.shape[0] // 2, -1)
    half = lax.dynamic_index_in_dim(pair, core, 0, False) + swap(
        lax.dynamic_index_in_dim(pair, 1 - core, 0, False), "row", 1
    )
    for bit in bits(depth):
        sent = rounded(half)
        half = sent.astype(f32) + swap(sent, "row", 4 * bit).astype(f32)

    mine = mine + got_x.astype(f32)
    sent_z = [mine[k].astype(bf16) for k in range(1, depth)]
    *sent_z, sent = lax.optimization_barrier((*sent_z, half.astype(bf16)))
    got_z = [swap(sent_z[k - 1], "row", 4 * k).astype(f32) for k in range(1, depth)]
    grad_in = tree_sum([mine[0]] + got_z)

    half = sent.astype(f32) + swap(sent, "row", 2).astype(f32)
    other = swap(half, "row", 1)
    low = jnp.where(core == 0, half, other)
    high = jnp.where(core == 0, other, half)
    total_nodes = own_rows * row_count * col_count
    grad_weight = jnp.concatenate([low, high]) * (1.0 / math.sqrt(total_nodes))

    start = col * own_rows
    own_pre = lax.dynamic_slice_in_dim(pre, start, own_rows)
    own_sigmoid = lax.dynamic_slice_in_dim(sigmoid_pre, start, own_rows)
    activated = (own_pre * own_sigmoid).astype(bf16)
    return (activated, grad_weight, grad_in.astype(bf16))


def solution(mesh):
    in_specs = (
        P(("row", "col"), None),
        P(),
        P(("row", "col"), None),
        P("row", "col", None, None, None),
        P("row", "col", None),
    )
    out_specs = (P(("row", "col"), None), P(), P(("row", "col"), None))
    return jax.shard_map(local, mesh=mesh, in_specs=in_specs, out_specs=out_specs, check_vma=False)
```

time: 269 us -> 52.8 us (0.20)
  waiting for transfers between devices: 234 us -> 23.8 us
  starting transfers between devices: 0.16 us -> 20.2 us
  between operations: 13.8 us -> 0.91 us
  matrix products: 7.9 us -> 2.6 us
  blocking collectives: 4.94 us -> 0 us
    psum x1 -> x0, waiting for transfers between devices: 121 us -> none  [local(): lax.psum(weight_term, ('row', 'col')) * (1.0 / math.sqrt(total_nodes))]
    reduce_scatter x2 -> x0, waiting for transfers between devices: 73.3 us -> none  [the longest x1 63 us: local(): lax.psum_scatter(col_partial, 'row', scatter_dimension=0, tiled=True)]
    all_gather x1 -> x0, waiting for transfers between devices: 38.4 us -> none  [local(): lax.all_gather(features, 'row', axis=0, tiled=True)]
    ppermute x0 -> x19, waiting for transfers between devices: none -> 23.8 us  [swap(): lax.ppermute(x, axis, [(i, i ^ bit) for i in range(lax.axis_size(axis))])]
    ppermute x0 -> x19, starting transfers between devices: none -> 20.2 us  [swap(): lax.ppermute(x, axis, [(i, i ^ bit) for i in range(lax.axis_size(axis))])]
    dot_general x5 -> x11, matrix products: 7.9 us -> 2.6 us  [the longest x4 1.08 us: backward(): jnp.einsum('bpij,bif->pjf', dense[:, quarter], row_panel, preferred_eleme...]
    all_gather x1 -> x0, blocking collectives: 4.94 us -> none  [local(): lax.all_gather(grad_agg, 'col', axis=0, tiled=True)]
  transfers between devices with their start and end apart: 4 -> 19, of which waited for: 4 -> 11; matrix products, arithmetic and copies ran while one was open for 3% -> 10% of each run, Pallas kernels for 0% -> 0%
where the time goes in v2:
time: 52.8 us; the launch traced here: 52.7 us
  waiting for transfers between devices  23.8 us (45%)
  starting transfers between devices  20.2 us (38%)
  other arithmetic  3.08 us (6%)
  matrix products  2.6 us (5%)
  local copies, waits for them, and re-layouts  2.14 us (4%)
  between operations  0.91 us (2%)
    ppermute x19, waiting for transfers between devices, swap(): lax.ppermute(x, axis, [(i, i ^ bit) for i in range(lax.axis_size(axis))])  23.8 us
    ppermute x19, starting transfers between devices, swap(): lax.ppermute(x, axis, [(i, i ^ bit) for i in range(lax.axis_size(axis))])  20.2 us
    scatter x1, local copies, waits for them, and re-layouts, local(): jnp.zeros((col_count * row_count, side, side), bf16).at[position]  1.69 us
    dot_general x4, matrix products, backward(): jnp.einsum('bpij,bif->pjf', dense[:, quarter], row_panel, preferred_eleme...  1.08 us
  transfers between devices with their start and end apart: 19, of which 11 were waited for; matrix products, arithmetic and copies ran while one was open for 10% of the time, Pallas kernels for 0%

profile of v2, /device:TPU:0, one launch (start us, length us, event | category | flops | bytes accessed | tf_op | source)
XLA Modules:
  0.0 52.7 jit_solution(3559196431594254638)
XLA Ops:
  0.7 5.1 %collective-permute-start.2 = (bf16[128,256]{1,0:T(8,128)(2,1)}, bf16[128,256]{1,0:T(8,128)(2,1)S(1)}, u32[]{:S(2)}, u32[]{:S(2)}) collective-permute-start(bf16[128,256]{1,0:T(8,128)(2,1)} %param.5), channel_id=1, source_target_pairs={{0,24},{2,26},{4,28},{6,30},{8,16},{10,18},{12,20},{14,22},{16,8},... | collective-permute-start | bytes 196616 | tf_op jit(solution)/shard_map/ppermute | solution.py:10
  5.8 0.6 %collective-permute-start = (bf16[128,256]{1,0:T(8,128)(2,1)}, bf16[128,256]{1,0:T(8,128)(2,1)S(1)}, u32[]{:S(2)}, u32[]{:S(2)}) collective-permute-start(bf16[128,256]{1,0:T(8,128)(2,1)} %param.5), channel_id=1, source_target_pairs={{0,8},{2,10},{4,12},{6,14},{8,0},{10,2},{12,4},{14,6},{16,24},{18,... | collective-permute-start | bytes 196616 | tf_op jit(solution)/shard_map/ppermute | solution.py:10
  6.4 1.7 %collective-permute-start.3 = (bf16[128,256]{1,0:T(8,128)(2,1)}, bf16[128,256]{1,0:T(8,128)(2,1)S(1)}, u32[]{:S(2)}, u32[]{:S(2)}) collective-permute-start(bf16[128,256]{1,0:T(8,128)(2,1)} %param.7), channel_id=1, source_target_pairs={{0,1},{1,0},{2,3},{3,2},{4,5},{5,4},{6,7},{7,6},{8,9},{9,8},{10,11... | collective-permute-start | bytes 196616 | tf_op jit(solution)/shard_map/ppermute | solution.py:10
  8.1 0.7 %fusion.16 = s32[24]{0:T(128)S(1)} fusion(s32[1,1,24]{2,1,0:T(1,128)} %param.9, s32[]{:T(128)S(6)} %axis_index.23), kind=kLoop, calls=%fused_computation.69 | loop fusion | flops 1656 | bytes 196 | tf_op jit(solution)/shard_map/select_n | solution.py:44
  9.0 1.7 %scatter_fusion = bf16[32,128,128]{2,1,0:T(8,128)(2,1)S(1)} fusion(bf16[32,128,128]{2,1,0:T(8,128)(2,1)S(1)} %broadcast_in_dim.4, s32[24]{0:T(128)S(1)} %fusion.16, bf16[24,128,128]{2,1,0:T(8,128)(2,1)S(1)} %bitcast.147), kind=kCustom, calls=%fused_computation | custom fusion | bytes 2359392 | tf_op jit(solution)/shard_map/scatter | solution.py:44
  11.0 0.6 %collective-permute-done.1 = bf16[128,256]{1,0:T(8,128)(2,1)S(1)} collective-permute-done((bf16[128,256]{1,0:T(8,128)(2,1)}, bf16[128,256]{1,0:T(8,128)(2,1)S(1)}, u32[]{:S(2)}, u32[]{:S(2)}) %collective-permute-start.1) | collective-permute-done | bytes 65568 | tf_op jit(solution)/shard_map/ppermute | solution.py:10
  11.8 1.7 %collective-permute-start.5 = (bf16[512,256]{1,0:T(8,128)(2,1)S(1)}, bf16[512,256]{1,0:T(8,128)(2,1)S(1)}, u32[]{:S(2)}, u32[]{:S(2)}) collective-permute-start(bf16[512,256]{1,0:T(8,128)(2,1)S(1)} %pad_maximum_fusion), channel_id=1, source_target_pairs={{0,4},{2,6},{4,0},{6,2},{8,12},{10,14},{12,8},{14,10},{16,20},{18,... | collective-permute-start | bytes 786440 | tf_op jit(solution)/shard_map/ppermute | solution.py:10
  13.7 5.8 %collective-permute-done.5 = bf16[512,256]{1,0:T(8,128)(2,1)S(1)} collective-permute-done((bf16[512,256]{1,0:T(8,128)(2,1)S(1)}, bf16[512,256]{1,0:T(8,128)(2,1)S(1)}, u32[]{:S(2)}, u32[]{:S(2)}) %collective-permute-start.5) | collective-permute-done | bytes 262176 | tf_op jit(solution)/shard_map/ppermute | solution.py:10
  20.0 1.1 %collective-permute-done.6 = bf16[512,256]{1,0:T(8,128)(2,1)S(1)} collective-permute-done((bf16[512,256]{1,0:T(8,128)(2,1)S(1)}, bf16[512,256]{1,0:T(8,128)(2,1)S(1)}, u32[]{:S(2)}, u32[]{:S(2)}) %collective-permute-start.6) | collective-permute-done | bytes 262176 | tf_op jit(solution)/shard_map/ppermute | solution.py:10
  21.3 1.8 %collective-permute-start.7 = (bf16[2,128,256]{2,1,0:T(8,128)(2,1)S(1)}, bf16[2,128,256]{2,1,0:T(8,128)(2,1)S(1)}, u32[]{:S(2)}, u32[]{:S(2)}) collective-permute-start(bf16[2,128,256]{2,1,0:T(8,128)(2,1)S(1)} %fusion.5), channel_id=1, source_target_pairs={{0,1},{1,0},{2,3},{3,2},{4,5},{5,4},{6,7},{7,6},{8,9},{9,8},{10,11... | collective-permute-start | bytes 393224 | tf_op jit(solution)/shard_map/ppermute | solution.py:10
  23.1 3.8 %collective-permute-done.7 = bf16[2,128,256]{2,1,0:T(8,128)(2,1)S(1)} collective-permute-done((bf16[2,128,256]{2,1,0:T(8,128)(2,1)S(1)}, bf16[2,128,256]{2,1,0:T(8,128)(2,1)S(1)}, u32[]{:S(2)}, u32[]{:S(2)}) %collective-permute-start.7) | collective-permute-done | bytes 131104 | tf_op jit(solution)/shard_map/ppermute | solution.py:10
  28.1 1.3 %collective-permute-done.9 = bf16[4,128,256]{2,1,0:T(8,128)(2,1)S(1)} collective-permute-done((bf16[4,128,256]{2,1,0:T(8,128)(2,1)S(1)}, bf16[4,128,256]{2,1,0:T(8,128)(2,1)S(1)}, u32[]{:S(2)}, u32[]{:S(2)}) %collective-permute-start.9) | collective-permute-done | bytes 262176 | tf_op jit(solution)/shard_map/ppermute | solution.py:10
  30.6 1.7 %collective-permute-start.10 = (bf16[4,128,256]{2,1,0:T(8,128)(2,1)S(1)}, bf16[4,128,256]{2,1,0:T(8,128)(2,1)S(1)}, u32[]{:S(2)}, u32[]{:S(2)}) collective-permute-start(bf16[4,128,256]{2,1,0:T(8,128)(2,1)S(1)} %add_convert_fusion), channel_id=1, source_target_pairs={{0,4},{2,6},{4,0},{6,2},{8,12},{10,14},{12,8},{14,10},{16,20},{18,... | collective-permute-start | bytes 786440 | tf_op jit(solution)/shard_map/ppermute | solution.py:10
  33.1 3.6 %collective-permute-done.12 = bf16[128,256]{1,0:T(8,128)(2,1)S(1)} collective-permute-done((bf16[128,256]{1,0:T(8,128)(2,1)S(1)}, bf16[128,256]{1,0:T(8,128)(2,1)S(1)}, u32[]{:S(2)}, u32[]{:S(2)}) %collective-permute-start.12) | collective-permute-done | bytes 65568 | tf_op jit(solution)/shard_map/ppermute | solution.py:10
  36.7 1.4 %collective-permute-start.13 = (bf16[128,256]{1,0:T(8,128)(2,1)S(1)}, bf16[128,256]{1,0:T(8,128)(2,1)S(1)}, u32[]{:S(2)}, u32[]{:S(2)}) collective-permute-start(bf16[128,256]{1,0:T(8,128)(2,1)S(1)} %add_convert_fusion.3), channel_id=1, source_target_pairs={{0,16},{2,18},{4,20},{6,22},{8,24},{10,26},{12,28},{14,30},{16,0},... | collective-permute-start | bytes 196616 | tf_op jit(solution)/shard_map/ppermute | solution.py:10
  38.0 0.9 %collective-permute-done.10 = bf16[4,128,256]{2,1,0:T(8,128)(2,1)S(1)} collective-permute-done((bf16[4,128,256]{2,1,0:T(8,128)(2,1)S(1)}, bf16[4,128,256]{2,1,0:T(8,128)(2,1)S(1)}, u32[]{:S(2)}, u32[]{:S(2)}) %collective-permute-start.10) | collective-permute-done | bytes 262176 | tf_op jit(solution)/shard_map/ppermute | solution.py:10
  39.1 3.4 %collective-permute-done.13 = bf16[128,256]{1,0:T(8,128)(2,1)S(1)} collective-permute-done((bf16[128,256]{1,0:T(8,128)(2,1)S(1)}, bf16[128,256]{1,0:T(8,128)(2,1)S(1)}, u32[]{:S(2)}, u32[]{:S(2)}) %collective-permute-start.13) | collective-permute-done | bytes 65568 | tf_op jit(solution)/shard_map/ppermute | solution.py:10
  43.1 0.6 %multiply_convert_fusion.1 = bf16[128,256]{1,0:T(8,128)(2,1)} fusion(f32[256,256]{1,0:T(8,128)S(1)} %get-tuple-element.33, s32[]{:T(128)S(6)} %select_n.123, f32[256,256]{1,0:T(8,128)S(1)} %fusion.18), kind=kLoop, calls=%fused_computation.38 | loop fusion | flops 65536 | bytes 327684 | tf_op jit(solution)/shard_map/convert_element_type | solution.py:120
  43.7 2.4 %collective-permute-start.18 = (bf16[128,256]{1,0:T(8,128)(2,1)S(1)}, bf16[128,256]{1,0:T(8,128)(2,1)S(1)}, u32[]{:S(2)}, u32[]{:S(2)}) collective-permute-start(bf16[128,256]{1,0:T(8,128)(2,1)S(1)} %get-tuple-element.24), channel_id=1, source_target_pairs={{0,24},{2,26},{4,28},{6,30},{8,16},{10,18},{12,20},{14,22},{16,8},... | collective-permute-start | bytes 196616 | tf_op jit(solution)/shard_map/ppermute | solution.py:10
  46.1 2.0 %collective-permute-start.16 = (bf16[128,256]{1,0:T(8,128)(2,1)S(1)}, bf16[128,256]{1,0:T(8,128)(2,1)S(1)}, u32[]{:S(2)}, u32[]{:S(2)}) collective-permute-start(bf16[128,256]{1,0:T(8,128)(2,1)S(1)} %get-tuple-element.22), channel_id=1, source_target_pairs={{0,8},{2,10},{4,12},{6,14},{8,0},{10,2},{12,4},{14,6},{16,24},{18,... | collective-permute-start | bytes 196616 | tf_op jit(solution)/shard_map/ppermute | solution.py:10
  48.2 1.6 %collective-permute-done.18 = bf16[128,256]{1,0:T(8,128)(2,1)S(1)} collective-permute-done((bf16[128,256]{1,0:T(8,128)(2,1)S(1)}, bf16[128,256]{1,0:T(8,128)(2,1)S(1)}, u32[]{:S(2)}, u32[]{:S(2)}) %collective-permute-start.18) | collective-permute-done | bytes 65568 | tf_op jit(solution)/shard_map/ppermute | solution.py:10
  49.8 1.5 %collective-permute-done.17 = bf16[128,256]{1,0:T(8,128)(2,1)S(1)} collective-permute-done((bf16[128,256]{1,0:T(8,128)(2,1)S(1)}, bf16[128,256]{1,0:T(8,128)(2,1)S(1)}, u32[]{:S(2)}, u32[]{:S(2)}) %collective-permute-start.17) | collective-permute-done | bytes 65568 | tf_op jit(solution)/shard_map/ppermute | solution.py:10
  51.2 0.7 %fusion.8 = bf16[128,256]{1,0:T(8,128)(2,1)} fusion(f32[4,128,256]{2,1,0:T(8,128)S(1)} %get-tuple-element.26, bf16[128,256]{1,0:T(8,128)(2,1)S(1)} %collective-permute-done.18, bf16[128,256]{1,0:T(8,128)(2,1)S(1)} %collective-permute-done.17, bf16[128,256]{1,0:T(8,128)(2,1)S(1)} %collective-permute-done.16), kind=kLoop, calls=%fused_computation.30 | loop fusion | flops 229376 | bytes 393216 | tf_op jit(solution)/shard_map/convert_element_type | solution.py:121
  51.9 0.7 %maximum_multiply_fusion = f32[256,256]{1,0:T(8,128)} fusion(f32[128,256]{1,0:T(8,128)S(1)} %get-tuple-element.28, f32[128,256]{1,0:T(8,128)S(1)} %get-tuple-element.27), kind=kLoop, calls=%fused_computation.23 | loop fusion | flops 131072 | bytes 524288 | tf_op jit(solution)/shard_map/mul | solution.py:115
  (52 shorter events, 5.5 us)
Async XLA Ops:
  0.6 26.3 %copy-start = (bf16[256,256]{1,0:T(8,128)(2,1)S(1)}, bf16[256,256]{1,0:T(8,128)(2,1)}, u32[]{:S(2)}) copy-start(bf16[256,256]{1,0:T(8,128)(2,1)} %param.6) | copy-start | bytes 393220
  0.6 8.4 %copy-start.1 = (bf16[1,1,24,128,128]{4,3,2,1,0:T(8,128)(2,1)S(1)}, bf16[1,1,24,128,128]{4,3,2,1,0:T(8,128)(2,1)}, u32[]{:S(2)}) copy-start(bf16[1,1,24,128,128]{4,3,2,1,0:T(8,128)(2,1)} %param.8) | copy-start | bytes 2359300
  0.7 10.3 %collective-permute-start.2 = (bf16[128,256]{1,0:T(8,128)(2,1)}, bf16[128,256]{1,0:T(8,128)(2,1)S(1)}, u32[]{:S(2)}, u32[]{:S(2)}) collective-permute-start(bf16[128,256]{1,0:T(8,128)(2,1)} %param.5), channel_id=1, source_target_pairs={{0,24},{2,26},{4,28},{6,30},{8,16},{10,18},{12,20},{14,22},{16,8},... | collective-permute-start | bytes 196616 | tf_op jit(solution)/shard_map/ppermute | solution.py:10
  5.8 5.8 %collective-permute-start.1 = (bf16[128,256]{1,0:T(8,128)(2,1)}, bf16[128,256]{1,0:T(8,128)(2,1)S(1)}, u32[]{:S(2)}, u32[]{:S(2)}) collective-permute-start(bf16[128,256]{1,0:T(8,128)(2,1)} %param.5), channel_id=1, source_target_pairs={{0,16},{2,18},{4,20},{6,22},{8,24},{10,26},{12,28},{14,30},{16,0},... | collective-permute-start | bytes 196616 | tf_op jit(solution)/shard_map/ppermute | solution.py:10
  5.8 5.8 %collective-permute-start = (bf16[128,256]{1,0:T(8,128)(2,1)}, bf16[128,256]{1,0:T(8,128)(2,1)S(1)}, u32[]{:S(2)}, u32[]{:S(2)}) collective-permute-start(bf16[128,256]{1,0:T(8,128)(2,1)} %param.5), channel_id=1, source_target_pairs={{0,8},{2,10},{4,12},{6,14},{8,0},{10,2},{12,4},{14,6},{16,24},{18,... | collective-permute-start | bytes 196616 | tf_op jit(solution)/shard_map/ppermute | solution.py:10
  6.4 4.5 %collective-permute-start.3 = (bf16[128,256]{1,0:T(8,128)(2,1)}, bf16[128,256]{1,0:T(8,128)(2,1)S(1)}, u32[]{:S(2)}, u32[]{:S(2)}) collective-permute-start(bf16[128,256]{1,0:T(8,128)(2,1)} %param.7), channel_id=1, source_target_pairs={{0,1},{1,0},{2,3},{3,2},{4,5},{5,4},{6,7},{7,6},{8,9},{9,8},{10,11... | collective-permute-start | bytes 196616 | tf_op jit(solution)/shard_map/ppermute | solution.py:10
  9.0 1.9 %copy-start.2 = (bf16[128,256]{1,0:T(8,128)(2,1)S(1)}, bf16[128,256]{1,0:T(8,128)(2,1)}, u32[]{:S(2)}) copy-start(bf16[128,256]{1,0:T(8,128)(2,1)} %param.7) | copy-start | bytes 196612
  10.9 0.8 %copy-start.3 = (bf16[128,256]{1,0:T(8,128)(2,1)S(1)}, bf16[128,256]{1,0:T(8,128)(2,1)}, u32[]{:S(2)}) copy-start(bf16[128,256]{1,0:T(8,128)(2,1)} %param.5) | copy-start | bytes 196612
  11.8 7.8 %collective-permute-start.5 = (bf16[512,256]{1,0:T(8,128)(2,1)S(1)}, bf16[512,256]{1,0:T(8,128)(2,1)S(1)}, u32[]{:S(2)}, u32[]{:S(2)}) collective-permute-start(bf16[512,256]{1,0:T(8,128)(2,1)S(1)} %pad_maximum_fusion), channel_id=1, source_target_pairs={{0,4},{2,6},{4,0},{6,2},{8,12},{10,14},{12,8},{14,10},{16,20},{18,... | collective-permute-start | bytes 786440 | tf_op jit(solution)/shard_map/ppermute | solution.py:10
  13.5 6.3 %collective-permute-start.4 = (bf16[512,256]{1,0:T(8,128)(2,1)S(1)}, bf16[512,256]{1,0:T(8,128)(2,1)S(1)}, u32[]{:S(2)}, u32[]{:S(2)}) collective-permute-start(bf16[512,256]{1,0:T(8,128)(2,1)S(1)} %pad_maximum_fusion), channel_id=1, source_target_pairs={{0,2},{2,0},{4,6},{6,4},{8,10},{10,8},{12,14},{14,12},{16,18},{18,... | collective-permute-start | bytes 786440 | tf_op jit(solution)/shard_map/ppermute | solution.py:10
  19.6 1.5 %collective-permute-start.6 = (bf16[512,256]{1,0:T(8,128)(2,1)S(1)}, bf16[512,256]{1,0:T(8,128)(2,1)S(1)}, u32[]{:S(2)}, u32[]{:S(2)}) collective-permute-start(bf16[512,256]{1,0:T(8,128)(2,1)S(1)} %collective-permute-done.5), channel_id=1, source_target_pairs={{0,2},{2,0},{4,6},{6,4},{8,10},{10,8},{12,14},{14,12},{16,18},{18,... | collective-permute-start | bytes 786440 | tf_op jit(solution)/shard_map/ppermute | solution.py:10
  21.3 5.6 %collective-permute-start.7 = (bf16[2,128,256]{2,1,0:T(8,128)(2,1)S(1)}, bf16[2,128,256]{2,1,0:T(8,128)(2,1)S(1)}, u32[]{:S(2)}, u32[]{:S(2)}) collective-permute-start(bf16[2,128,256]{2,1,0:T(8,128)(2,1)S(1)} %fusion.5), channel_id=1, source_target_pairs={{0,1},{1,0},{2,3},{3,2},{4,5},{5,4},{6,7},{7,6},{8,9},{9,8},{10,11... | collective-permute-start | bytes 393224 | tf_op jit(solution)/shard_map/ppermute | solution.py:10
  27.8 1.6 %collective-permute-start.9 = (bf16[4,128,256]{2,1,0:T(8,128)(2,1)S(1)}, bf16[4,128,256]{2,1,0:T(8,128)(2,1)S(1)}, u32[]{:S(2)}, u32[]{:S(2)}) collective-permute-start(bf16[4,128,256]{2,1,0:T(8,128)(2,1)S(1)} %fusion.1), channel_id=1, source_target_pairs={{0,2},{2,0},{4,6},{6,4},{8,10},{10,8},{12,14},{14,12},{16,18},{18,... | collective-permute-start | bytes 786440 | tf_op jit(solution)/shard_map/ppermute | solution.py:10
  29.7 2.6 %collective-permute-start.11 = (f32[128,256]{1,0:T(8,128)S(1)}, f32[128,256]{1,0:T(8,128)S(1)}, u32[]{:S(2)}, u32[]{:S(2)}) collective-permute-start(f32[128,256]{1,0:T(8,128)S(1)} %dynamic-slice_bitcast_fusion), channel_id=1, source_target_pairs={{0,2},{2,0},{4,6},{6,4},{8,10},{10,8},{12,14},{14,12},{16,18},{18,... | collective-permute-start | bytes 393224 | tf_op jit(solution)/shard_map/ppermute | solution.py:10
  30.2 7.9 %collective-permute-start.8 = (bf16[4,128,256]{2,1,0:T(8,128)(2,1)S(1)}, bf16[4,128,256]{2,1,0:T(8,128)(2,1)S(1)}, u32[]{:S(2)}, u32[]{:S(2)}) collective-permute-start(bf16[4,128,256]{2,1,0:T(8,128)(2,1)S(1)} %fusion), channel_id=1, source_target_pairs={{0,2},{2,0},{4,6},{6,4},{8,10},{10,8},{12,14},{14,12},{16,18},{18,... | collective-permute-start | bytes 786440 | tf_op jit(solution)/shard_map/ppermute | solution.py:10
  30.6 8.3 %collective-permute-start.10 = (bf16[4,128,256]{2,1,0:T(8,128)(2,1)S(1)}, bf16[4,128,256]{2,1,0:T(8,128)(2,1)S(1)}, u32[]{:S(2)}, u32[]{:S(2)}) collective-permute-start(bf16[4,128,256]{2,1,0:T(8,128)(2,1)S(1)} %add_convert_fusion), channel_id=1, source_target_pairs={{0,4},{2,6},{4,0},{6,2},{8,12},{10,14},{12,8},{14,10},{16,20},{18,... | collective-permute-start | bytes 786440 | tf_op jit(solution)/shard_map/ppermute | solution.py:10
  32.3 4.3 %collective-permute-start.12 = (bf16[128,256]{1,0:T(8,128)(2,1)S(1)}, bf16[128,256]{1,0:T(8,128)(2,1)S(1)}, u32[]{:S(2)}, u32[]{:S(2)}) collective-permute-start(bf16[128,256]{1,0:T(8,128)(2,1)S(1)} %fusion.9), channel_id=1, source_target_pairs={{0,8},{2,10},{4,12},{6,14},{8,0},{10,2},{12,4},{14,6},{16,24},{18,... | collective-permute-start | bytes 196616 | tf_op jit(solution)/shard_map/ppermute | solution.py:10
  36.7 5.8 %collective-permute-start.13 = (bf16[128,256]{1,0:T(8,128)(2,1)S(1)}, bf16[128,256]{1,0:T(8,128)(2,1)S(1)}, u32[]{:S(2)}, u32[]{:S(2)}) collective-permute-start(bf16[128,256]{1,0:T(8,128)(2,1)S(1)} %add_convert_fusion.3), channel_id=1, source_target_pairs={{0,16},{2,18},{4,20},{6,22},{8,24},{10,26},{12,28},{14,30},{16,0},... | collective-permute-start | bytes 196616 | tf_op jit(solution)/shard_map/ppermute | solution.py:10
  42.5 5.6 %collective-permute-start.14 = (bf16[128,256]{1,0:T(8,128)(2,1)S(1)}, bf16[128,256]{1,0:T(8,128)(2,1)S(1)}, u32[]{:S(2)}, u32[]{:S(2)}) collective-permute-start(bf16[128,256]{1,0:T(8,128)(2,1)S(1)} %add_convert_fusion.2), channel_id=1, source_target_pairs={{0,4},{2,6},{4,0},{6,2},{8,12},{10,14},{12,8},{14,10},{16,20},{18,... | collective-permute-start | bytes 196616 | tf_op jit(solution)/shard_map/ppermute | solution.py:10
  43.7 6.1 %collective-permute-start.18 = (bf16[128,256]{1,0:T(8,128)(2,1)S(1)}, bf16[128,256]{1,0:T(8,128)(2,1)S(1)}, u32[]{:S(2)}, u32[]{:S(2)}) collective-permute-start(bf16[128,256]{1,0:T(8,128)(2,1)S(1)} %get-tuple-element.24), channel_id=1, source_target_pairs={{0,24},{2,26},{4,28},{6,30},{8,16},{10,18},{12,20},{14,22},{16,8},... | collective-permute-start | bytes 196616 | tf_op jit(solution)/shard_map/ppermute | solution.py:10
  46.1 5.2 %collective-permute-start.17 = (bf16[128,256]{1,0:T(8,128)(2,1)S(1)}, bf16[128,256]{1,0:T(8,128)(2,1)S(1)}, u32[]{:S(2)}, u32[]{:S(2)}) collective-permute-start(bf16[128,256]{1,0:T(8,128)(2,1)S(1)} %get-tuple-element.23), channel_id=1, source_target_pairs={{0,16},{2,18},{4,20},{6,22},{8,24},{10,26},{12,28},{14,30},{16,0},... | collective-permute-start | bytes 196616 | tf_op jit(solution)/shard_map/ppermute | solution.py:10
  46.1 5.2 %collective-permute-start.16 = (bf16[128,256]{1,0:T(8,128)(2,1)S(1)}, bf16[128,256]{1,0:T(8,128)(2,1)S(1)}, u32[]{:S(2)}, u32[]{:S(2)}) collective-permute-start(bf16[128,256]{1,0:T(8,128)(2,1)S(1)} %get-tuple-element.22), channel_id=1, source_target_pairs={{0,8},{2,10},{4,12},{6,14},{8,0},{10,2},{12,4},{14,6},{16,24},{18,... | collective-permute-start | bytes 196616 | tf_op jit(solution)/shard_map/ppermute | solution.py:10
  48.1 3.8 %collective-permute-start.15 = (f32[128,256]{1,0:T(8,128)S(1)}, f32[128,256]{1,0:T(8,128)S(1)}, u32[]{:S(2)}, u32[]{:S(2)}) collective-permute-start(f32[128,256]{1,0:T(8,128)S(1)} %convert_add_fusion.1), channel_id=1, source_target_pairs={{0,2},{2,0},{4,6},{6,4},{8,10},{10,8},{12,14},{14,12},{16,18},{18,... | collective-permute-start | bytes 393224 | tf_op jit(solution)/shard_map/ppermute | solution.py:10

commit v3 on v2

--- a/solution.py
+++ b/solution.py
@@ -3,6 +3,8 @@
 import jax
 import jax.numpy as jnp
 from jax import lax
+from jax.experimental import pallas as pl
+from jax.experimental.pallas import tpu as pltpu
 from jax.sharding import PartitionSpec as P
 
 
@@ -14,10 +16,61 @@
     return [1 << k for k in range(count.bit_length() - 1)]
 
 
+def total(terms, dtype, flops, later_than=()):
+    count = len(terms)
+
+    def body(*refs):
+        value = refs[0][...].astype(jnp.float32)
+        for ref in refs[1:count]:
+            value = value + ref[...].astype(jnp.float32)
+        refs[-1][...] = value.astype(dtype)
+
+    shape = jax.ShapeDtypeStruct(terms[0].shape, dtype)
+    in_specs = [pl.BlockSpec(memory_space=pltpu.VMEM)] * count
+    in_specs += [pl.BlockSpec(memory_space=pl.ANY)] * len(later_than)
+    return pl.pallas_call(
+        body,
+        out_shape=shape,
+        in_specs=in_specs,
+        out_specs=pl.BlockSpec(memory_space=pltpu.VMEM),
+        compiler_params=pltpu.CompilerParams(vmem_limit_bytes=4 << 20),
+        cost_estimate=pl.CostEstimate(flops=flops, bytes_accessed=4 * shape.size, transcendentals=0),
+    )(*terms, *later_than)
+
+
 def tree_sum(terms):
     while len(terms) > 1:
         terms = [a + b for a, b in zip(terms[::2], terms[1::2])]
     return terms[0]
+
+
+def finish(terms, half, other, core, scale):
+    count = len(terms)
+    rows, width = half.shape
+
+    def body(core_ref, *refs):
+        half_ref, other_ref, grad_ref, weight_ref = refs[count:]
+        value = refs[0][...]
+        for ref in refs[1:count]:
+            value = value + ref[...].astype(jnp.float32)
+        grad_ref[...] = value.astype(jnp.bfloat16)
+        first = pl.multiple_of(core_ref[0] * rows, rows)
+        second = pl.multiple_of(rows - core_ref[0] * rows, rows)
+        weight_ref[pl.ds(first, rows), :] = half_ref[...] * scale
+        weight_ref[pl.ds(second, rows), :] = other_ref[...] * scale
+
+    vmem = pl.BlockSpec(memory_space=pltpu.VMEM)
+    return pl.pallas_call(
+        body,
+        out_shape=(
+            jax.ShapeDtypeStruct(terms[0].shape, jnp.bfloat16),
+            jax.ShapeDtypeStruct((2 * rows, width), jnp.float32),
+        ),
+        in_specs=[pl.BlockSpec(memory_space=pltpu.SMEM)] + [vmem] * (count + 2),
+        out_specs=(vmem, vmem),
+        compiler_params=pltpu.CompilerParams(vmem_limit_bytes=4 << 20),
+        cost_estimate=pl.CostEstimate(flops=10**6, bytes_accessed=10**6, transcendentals=0),
+    )(core.reshape(1), *terms, half, other)
 
 
 def rounded(x):
@@ -79,46 +132,41 @@
     grad_pre = (
         cotangent.astype(f32) * sigmoid_pre * (1.0 + pre * (1.0 - sigmoid_pre))
     ).astype(bf16)
+    term = jnp.dot(aggregated.T, grad_pre, preferred_element_type=f32)
+    grad_pre, term = lax.optimization_barrier((grad_pre, term))
     grad_agg = jnp.dot(grad_pre, weight.T, preferred_element_type=f32).astype(bf16)
     row_panel = grad_agg.reshape(col_count, side, width)
 
     sent_xc = backward(3, row_panel).astype(bf16)
-    sent_xc, aggregated = lax.optimization_barrier((sent_xc, aggregated))
     got_xc = swap(sent_xc, "row", 1)
-    term = jnp.dot(aggregated.T, grad_pre, preferred_element_type=f32)
     got_c = swap(backward(2, row_panel).astype(bf16), "row", 1)
 
     sent_x = (backward(1, row_panel) + got_xc.astype(f32)).astype(bf16)
-    sent_x, term = lax.optimization_barrier((sent_x, term))
     got_x = swap(sent_x, "row", 2)
     mine = backward(0, row_panel) + got_c.astype(f32)
 
     pair = term.reshape(2, term.shape[0] // 2, -1)
-    half = lax.dynamic_index_in_dim(pair, core, 0, False) + swap(
-        lax.dynamic_index_in_dim(pair, 1 - core, 0, False), "row", 1
-    )
-    for bit in bits(depth):
-        sent = rounded(half)
-        half = sent.astype(f32) + swap(sent, "row", 4 * bit).astype(f32)
+    kept = lax.dynamic_index_in_dim(pair, core, 0, False)
+    got = swap(lax.dynamic_index_in_dim(pair, 1 - core, 0, False), "row", 1)
+    half = total([kept, got], bf16, 3000000000, [sent_x])
 
     mine = mine + got_x.astype(f32)
     sent_z = [mine[k].astype(bf16) for k in range(1, depth)]
-    *sent_z, sent = lax.optimization_barrier((*sent_z, half.astype(bf16)))
-    got_z = [swap(sent_z[k - 1], "row", 4 * k).astype(f32) for k in range(1, depth)]
-    grad_in = tree_sum([mine[0]] + got_z)
-
-    half = sent.astype(f32) + swap(sent, "row", 2).astype(f32)
-    other = swap(half, "row", 1)
-    low = jnp.where(core == 0, half, other)
-    high = jnp.where(core == 0, other, half)
+    for bit in bits(depth):
+        last = [sent_z[-1]] if 2 * bit == depth else []
+        half = total([half, swap(half, "row", 4 * bit)], bf16, 3000000000 if last else 100000000, last)
+    got_z = [swap(sent_z[k - 1], "row", 4 * k) for k in range(1, depth)]
+    half = total([half, swap(half, "row", 2)], f32, 10**8)
     total_nodes = own_rows * row_count * col_count
-    grad_weight = jnp.concatenate([low, high]) * (1.0 / math.sqrt(total_nodes))
+    scale = 1.0 / math.sqrt(total_nodes)
+    grad_sum = total([mine[0]] + got_z, f32, 3 * 10**9)
+    grad_in, grad_weight = finish([grad_sum], half, swap(half, "row", 1), core, scale)
 
     start = col * own_rows
     own_pre = lax.dynamic_slice_in_dim(pre, start, own_rows)
     own_sigmoid = lax.dynamic_slice_in_dim(sigmoid_pre, start, own_rows)
     activated = (own_pre * own_sigmoid).astype(bf16)
-    return (activated, grad_weight, grad_in.astype(bf16))
+    return (activated, grad_weight, grad_in)
 
 
 def solution(mesh):

time: 52.8 us -> 49.8 us (0.943)
  waiting for transfers between devices: 23.8 us -> 19.1 us
  starting transfers between devices: 20.2 us -> 22.5 us
  other arithmetic: 3.08 us -> 1.61 us
  Pallas kernels: 0 us -> 0.85 us
    ppermute x19, waiting for transfers between devices: 23.8 us -> 19.1 us  [swap(): lax.ppermute(x, axis, [(i, i ^ bit) for i in range(lax.axis_size(axis))])]
    ppermute x19, starting transfers between devices: 20.2 us -> 22.5 us  [swap(): lax.ppermute(x, axis, [(i, i ^ bit) for i in range(lax.axis_size(axis))])]
    pallas_call x0 -> x6, Pallas kernels: none -> 0.85 us  [the longest x1 0.75 us: finish(): pl.pallas_call(body, out_shape=(jax.ShapeDtypeStruct(terms[0].shape, jnp....]
    mul x1 -> x0, other arithmetic: 0.72 us -> none  [local(): grad_weight = jnp.concatenate([low, high]) * (1.0 / math.sqrt(total_nodes))]
    convert_element_type x4 -> x0, other arithmetic: 0.71 us -> none  [the longest x1 0.66 us: local(): return (activated, grad_weight, grad_in.astype(bf16))]
  transfers between devices with their start and end apart: 19 -> 19, of which waited for: 11 -> 10; matrix products, arithmetic and copies ran while one was open for 10% -> 10% of each run, Pallas kernels for 0% -> 0%
where the time goes in v3:
time: 49.8 us; the launch traced here: 49.6 us
  starting transfers between devices  22.5 us (45%)
  waiting for transfers between devices  19.1 us (38%)
  matrix products  2.63 us (5%)
  local copies, waits for them, and re-layouts  2.01 us (4%)
  other arithmetic  1.61 us (3%)
  between operations  0.92 us (2%)
  Pallas kernels  0.85 us (2%)
    ppermute x19, starting transfers between devices, swap(): lax.ppermute(x, axis, [(i, i ^ bit) for i in range(lax.axis_size(axis))])  22.5 us
    ppermute x19, waiting for transfers between devices, swap(): lax.ppermute(x, axis, [(i, i ^ bit) for i in range(lax.axis_size(axis))])  19.1 us
    scatter x1, local copies, waits for them, and re-layouts, local(): jnp.zeros((col_count * row_count, side, side), bf16).at[position]  1.7 us
    dot_general x4, matrix products, backward(): jnp.einsum('bpij,bif->pjf', dense[:, quarter], row_panel, preferred_eleme...  1.1 us
  transfers between devices with their start and end apart: 19, of which 10 were waited for; matrix products, arithmetic and copies ran while one was open for 10% of the time, Pallas kernels for 0%

profile of v3, /device:TPU:0, one launch (start us, length us, event | category | flops | bytes accessed | tf_op | source)
XLA Modules:
  0.0 49.6 jit_solution(16027605189364893270)
XLA Ops:
  0.7 4.1 %collective-permute-start.1 = (bf16[128,256]{1,0:T(8,128)(2,1)}, bf16[128,256]{1,0:T(8,128)(2,1)S(1)}, u32[]{:S(2)}, u32[]{:S(2)}) collective-permute-start(bf16[128,256]{1,0:T(8,128)(2,1)} %param.5), channel_id=1, source_target_pairs={{0,16},{2,18},{4,20},{6,22},{8,24},{10,26},{12,28},{14,30},{16,0},... | collective-permute-start | bytes 196616 | tf_op jit(solution)/shard_map/ppermute | solution.py:12
  4.8 1.6 %collective-permute-start = (bf16[128,256]{1,0:T(8,128)(2,1)}, bf16[128,256]{1,0:T(8,128)(2,1)S(1)}, u32[]{:S(2)}, u32[]{:S(2)}) collective-permute-start(bf16[128,256]{1,0:T(8,128)(2,1)} %param.5), channel_id=1, source_target_pairs={{0,8},{2,10},{4,12},{6,14},{8,0},{10,2},{12,4},{14,6},{16,24},{18,... | collective-permute-start | bytes 196616 | tf_op jit(solution)/shard_map/ppermute | solution.py:12
  6.3 1.7 %collective-permute-start.3 = (bf16[128,256]{1,0:T(8,128)(2,1)}, bf16[128,256]{1,0:T(8,128)(2,1)S(1)}, u32[]{:S(2)}, u32[]{:S(2)}) collective-permute-start(bf16[128,256]{1,0:T(8,128)(2,1)} %param.7), channel_id=1, source_target_pairs={{0,1},{1,0},{2,3},{3,2},{4,5},{5,4},{6,7},{7,6},{8,9},{9,8},{10,11... | collective-permute-start | bytes 196616 | tf_op jit(solution)/shard_map/ppermute | solution.py:12
  8.1 0.7 %fusion.12 = s32[24]{0:T(128)S(1)} fusion(s32[1,1,24]{2,1,0:T(1,128)} %param.9, s32[]{:T(128)S(6)} %axis_index.23), kind=kLoop, calls=%fused_computation.59 | loop fusion | flops 1656 | bytes 196 | tf_op jit(solution)/shard_map/select_n | solution.py:97
  9.0 1.7 %scatter_fusion = bf16[32,128,128]{2,1,0:T(8,128)(2,1)S(1)} fusion(bf16[32,128,128]{2,1,0:T(8,128)(2,1)S(1)} %broadcast_in_dim.4, s32[24]{0:T(128)S(1)} %fusion.12, bf16[24,128,128]{2,1,0:T(8,128)(2,1)S(1)} %bitcast.140), kind=kCustom, calls=%fused_computation | custom fusion | bytes 2359392 | tf_op jit(solution)/shard_map/scatter | solution.py:97
  10.9 1.7 %collective-permute-done.2 = bf16[128,256]{1,0:T(8,128)(2,1)S(1)} collective-permute-done((bf16[128,256]{1,0:T(8,128)(2,1)}, bf16[128,256]{1,0:T(8,128)(2,1)S(1)}, u32[]{:S(2)}, u32[]{:S(2)}) %collective-permute-start.2) | collective-permute-done | bytes 65568 | tf_op jit(solution)/shard_map/ppermute | solution.py:12
  12.6 1.6 %collective-permute-start.5 = (bf16[512,256]{1,0:T(8,128)(2,1)S(1)}, bf16[512,256]{1,0:T(8,128)(2,1)S(1)}, u32[]{:S(2)}, u32[]{:S(2)}) collective-permute-start(bf16[512,256]{1,0:T(8,128)(2,1)S(1)} %pad_maximum_fusion), channel_id=1, source_target_pairs={{0,4},{2,6},{4,0},{6,2},{8,12},{10,14},{12,8},{14,10},{16,20},{18,... | collective-permute-start | bytes 786440 | tf_op jit(solution)/shard_map/ppermute | solution.py:12
  14.4 4.7 %collective-permute-done.5 = bf16[512,256]{1,0:T(8,128)(2,1)S(1)} collective-permute-done((bf16[512,256]{1,0:T(8,128)(2,1)S(1)}, bf16[512,256]{1,0:T(8,128)(2,1)S(1)}, u32[]{:S(2)}, u32[]{:S(2)}) %collective-permute-start.5) | collective-permute-done | bytes 262176 | tf_op jit(solution)/shard_map/ppermute | solution.py:12
  19.6 1.1 %collective-permute-done.6 = bf16[512,256]{1,0:T(8,128)(2,1)S(1)} collective-permute-done((bf16[512,256]{1,0:T(8,128)(2,1)S(1)}, bf16[512,256]{1,0:T(8,128)(2,1)S(1)}, u32[]{:S(2)}, u32[]{:S(2)}) %collective-permute-start.6) | collective-permute-done | bytes 262176 | tf_op jit(solution)/shard_map/ppermute | solution.py:12
  20.9 1.6 %collective-permute-start.7 = (bf16[2,128,256]{2,1,0:T(8,128)(2,1)S(1)}, bf16[2,128,256]{2,1,0:T(8,128)(2,1)S(1)}, u32[]{:S(2)}, u32[]{:S(2)}) collective-permute-start(bf16[2,128,256]{2,1,0:T(8,128)(2,1)S(1)} %fusion.5), channel_id=1, source_target_pairs={{0,1},{1,0},{2,3},{3,2},{4,5},{5,4},{6,7},{7,6},{8,9},{9,8},{10,11... | collective-permute-start | bytes 393224 | tf_op jit(solution)/shard_map/ppermute | solution.py:12
  22.5 4.0 %collective-permute-done.7 = bf16[2,128,256]{2,1,0:T(8,128)(2,1)S(1)} collective-permute-done((bf16[2,128,256]{2,1,0:T(8,128)(2,1)S(1)}, bf16[2,128,256]{2,1,0:T(8,128)(2,1)S(1)}, u32[]{:S(2)}, u32[]{:S(2)}) %collective-permute-start.7) | collective-permute-done | bytes 131104 | tf_op jit(solution)/shard_map/ppermute | solution.py:12
  27.7 0.6 %collective-permute-start.9 = (bf16[4,128,256]{2,1,0:T(8,128)(2,1)S(1)}, bf16[4,128,256]{2,1,0:T(8,128)(2,1)S(1)}, u32[]{:S(2)}, u32[]{:S(2)}) collective-permute-start(bf16[4,128,256]{2,1,0:T(8,128)(2,1)S(1)} %fusion.1), channel_id=1, source_target_pairs={{0,2},{2,0},{4,6},{6,4},{8,10},{10,8},{12,14},{14,12},{16,18},{18,... | collective-permute-start | bytes 786440 | tf_op jit(solution)/shard_map/ppermute | solution.py:12
  29.7 1.6 %collective-permute-start.10 = (bf16[4,128,256]{2,1,0:T(8,128)(2,1)S(1)}, bf16[4,128,256]{2,1,0:T(8,128)(2,1)S(1)}, u32[]{:S(2)}, u32[]{:S(2)}) collective-permute-start(bf16[4,128,256]{2,1,0:T(8,128)(2,1)S(1)} %add_convert_fusion.refs_2_), channel_id=1, source_target_pairs={{0,4},{2,6},{4,0},{6,2},{8,12},{10,14},{12,8},{14,10},{16,20},{18,... | collective-permute-start | bytes 786440 | tf_op jit(solution)/shard_map/ppermute | solution.py:12
  31.3 0.8 %collective-permute-start.15 = (bf16[128,256]{1,0:T(8,128)(2,1)S(1)}, bf16[128,256]{1,0:T(8,128)(2,1)S(1)}, u32[]{:S(2)}, u32[]{:S(2)}) collective-permute-start(bf16[128,256]{1,0:T(8,128)(2,1)S(1)} %shard_map.77.refs_0_), channel_id=1, source_target_pairs={{0,8},{2,10},{4,12},{6,14},{8,0},{10,2},{12,4},{14,6},{16,24},{18,... | collective-permute-start | bytes 196616 | tf_op jit(solution)/shard_map/ppermute | solution.py:12
  32.2 0.6 %multiply_convert_fusion.1 = bf16[128,256]{1,0:T(8,128)(2,1)} fusion(f32[256,256]{1,0:T(8,128)S(1)} %get-tuple-element.25, s32[]{:T(128)S(6)} %select_n.111, f32[256,256]{1,0:T(8,128)S(1)} %fusion.14), kind=kLoop, calls=%fused_computation.30 | loop fusion | flops 65536 | bytes 327684 | tf_op jit(solution)/shard_map/convert_element_type | solution.py:168
  32.8 2.8 %collective-permute-done.15.refs_1_ = bf16[128,256]{1,0:T(8,128)(2,1)S(1)} collective-permute-done((bf16[128,256]{1,0:T(8,128)(2,1)S(1)}, bf16[128,256]{1,0:T(8,128)(2,1)S(1)}, u32[]{:S(2)}, u32[]{:S(2)}) %collective-permute-start.15) | collective-permute-done | bytes 65568 | tf_op jit(solution)/shard_map/ppermute | solution.py:12
  35.7 2.8 %collective-permute-start.16 = (bf16[128,256]{1,0:T(8,128)(2,1)S(1)}, bf16[128,256]{1,0:T(8,128)(2,1)S(1)}, u32[]{:S(2)}, u32[]{:S(2)}) collective-permute-start(bf16[128,256]{1,0:T(8,128)(2,1)S(1)} %shard_map.78.refs_0_), channel_id=1, source_target_pairs={{0,16},{2,18},{4,20},{6,22},{8,24},{10,26},{12,28},{14,30},{16,0},... | collective-permute-start | bytes 196616 | tf_op jit(solution)/shard_map/ppermute | solution.py:12
  38.6 2.7 %collective-permute-start.12 = (bf16[128,256]{1,0:T(8,128)(2,1)S(1)}, bf16[128,256]{1,0:T(8,128)(2,1)S(1)}, u32[]{:S(2)}, u32[]{:S(2)}) collective-permute-start(bf16[128,256]{1,0:T(8,128)(2,1)S(1)} %get-tuple-element.22), channel_id=1, source_target_pairs={{0,16},{2,18},{4,20},{6,22},{8,24},{10,26},{12,28},{14,30},{16,0},... | collective-permute-start | bytes 196616 | tf_op jit(solution)/shard_map/ppermute | solution.py:12
  41.3 0.9 %collective-permute-start.11 = (bf16[128,256]{1,0:T(8,128)(2,1)S(1)}, bf16[128,256]{1,0:T(8,128)(2,1)S(1)}, u32[]{:S(2)}, u32[]{:S(2)}) collective-permute-start(bf16[128,256]{1,0:T(8,128)(2,1)S(1)} %get-tuple-element.23), channel_id=1, source_target_pairs={{0,8},{2,10},{4,12},{6,14},{8,0},{10,2},{12,4},{14,6},{16,24},{18,... | collective-permute-start | bytes 196616 | tf_op jit(solution)/shard_map/ppermute | solution.py:12
  42.2 0.8 %collective-permute-start.13 = (bf16[128,256]{1,0:T(8,128)(2,1)S(1)}, bf16[128,256]{1,0:T(8,128)(2,1)S(1)}, u32[]{:S(2)}, u32[]{:S(2)}) collective-permute-start(bf16[128,256]{1,0:T(8,128)(2,1)S(1)} %get-tuple-element.21.refs_2_), channel_id=1, source_target_pairs={{0,24},{2,26},{4,28},{6,30},{8,16},{10,18},{12,20},{14,22},{16,8},... | collective-permute-start | bytes 196616 | tf_op jit(solution)/shard_map/ppermute | solution.py:12
  43.1 1.5 %collective-permute-start.17 = (bf16[128,256]{1,0:T(8,128)(2,1)S(1)}, bf16[128,256]{1,0:T(8,128)(2,1)S(1)}, u32[]{:S(2)}, u32[]{:S(2)}) collective-permute-start(bf16[128,256]{1,0:T(8,128)(2,1)S(1)} %shard_map.79.refs_0_), channel_id=1, source_target_pairs={{0,4},{2,6},{4,0},{6,2},{8,12},{10,14},{12,8},{14,10},{16,20},{18,... | collective-permute-start | bytes 196616 | tf_op jit(solution)/shard_map/ppermute | solution.py:12
  44.6 2.9 %collective-permute-done.17.refs_1_ = bf16[128,256]{1,0:T(8,128)(2,1)S(1)} collective-permute-done((bf16[128,256]{1,0:T(8,128)(2,1)S(1)}, bf16[128,256]{1,0:T(8,128)(2,1)S(1)}, u32[]{:S(2)}, u32[]{:S(2)}) %collective-permute-start.17) | collective-permute-done | bytes 65568 | tf_op jit(solution)/shard_map/ppermute | solution.py:12
  47.5 0.8 %collective-permute-done.13.refs_3_ = bf16[128,256]{1,0:T(8,128)(2,1)S(1)} collective-permute-done((bf16[128,256]{1,0:T(8,128)(2,1)S(1)}, bf16[128,256]{1,0:T(8,128)(2,1)S(1)}, u32[]{:S(2)}, u32[]{:S(2)}) %collective-permute-start.13) | collective-permute-done | bytes 65568 | tf_op jit(solution)/shard_map/ppermute | solution.py:12
  48.9 0.7 %shard_map.81 = (bf16[128,256]{1,0:T(8,128)(2,1)}, f32[256,256]{1,0:T(8,128)}) custom-call(s32[1]{0:T(128)} %bitcast.25.core_ref, f32[128,256]{1,0:T(8,128)S(1)} %shard_map.76.refs_0_, f32[128,256]{1,0:T(8,128)S(1)} %shard_map.80.refs_1_, f32[128,256]{1,0:T(8,128)S(1)} %collective-permute-done.18.refs_2_), custom_call_target="tpu_custom_call" | custom-call | flops 1000000 | bytes 1000000 | tf_op jit(solution)/shard_map/pallas_call | solution.py:63
  (52 shorter events, 4.7 us)
Async XLA Ops:
  0.6 25.9 %copy-start = (bf16[256,256]{1,0:T(8,128)(2,1)S(1)}, bf16[256,256]{1,0:T(8,128)(2,1)}, u32[]{:S(2)}) copy-start(bf16[256,256]{1,0:T(8,128)(2,1)} %param.6) | copy-start | bytes 393220
  0.6 8.4 %copy-start.1 = (bf16[1,1,24,128,128]{4,3,2,1,0:T(8,128)(2,1)S(1)}, bf16[1,1,24,128,128]{4,3,2,1,0:T(8,128)(2,1)}, u32[]{:S(2)}) copy-start(bf16[1,1,24,128,128]{4,3,2,1,0:T(8,128)(2,1)} %param.8) | copy-start | bytes 2359300
  0.7 10.2 %collective-permute-start.1 = (bf16[128,256]{1,0:T(8,128)(2,1)}, bf16[128,256]{1,0:T(8,128)(2,1)S(1)}, u32[]{:S(2)}, u32[]{:S(2)}) collective-permute-start(bf16[128,256]{1,0:T(8,128)(2,1)} %param.5), channel_id=1, source_target_pairs={{0,16},{2,18},{4,20},{6,22},{8,24},{10,26},{12,28},{14,30},{16,0},... | collective-permute-start | bytes 196616 | tf_op jit(solution)/shard_map/ppermute | solution.py:12
  4.8 6.1 %collective-permute-start = (bf16[128,256]{1,0:T(8,128)(2,1)}, bf16[128,256]{1,0:T(8,128)(2,1)S(1)}, u32[]{:S(2)}, u32[]{:S(2)}) collective-permute-start(bf16[128,256]{1,0:T(8,128)(2,1)} %param.5), channel_id=1, source_target_pairs={{0,8},{2,10},{4,12},{6,14},{8,0},{10,2},{12,4},{14,6},{16,24},{18,... | collective-permute-start | bytes 196616 | tf_op jit(solution)/shard_map/ppermute | solution.py:12
  6.3 6.3 %collective-permute-start.2 = (bf16[128,256]{1,0:T(8,128)(2,1)}, bf16[128,256]{1,0:T(8,128)(2,1)S(1)}, u32[]{:S(2)}, u32[]{:S(2)}) collective-permute-start(bf16[128,256]{1,0:T(8,128)(2,1)} %param.5), channel_id=1, source_target_pairs={{0,24},{2,26},{4,28},{6,30},{8,16},{10,18},{12,20},{14,22},{16,8},... | collective-permute-start | bytes 196616 | tf_op jit(solution)/shard_map/ppermute | solution.py:12
  6.3 4.5 %collective-permute-start.3 = (bf16[128,256]{1,0:T(8,128)(2,1)}, bf16[128,256]{1,0:T(8,128)(2,1)S(1)}, u32[]{:S(2)}, u32[]{:S(2)}) collective-permute-start(bf16[128,256]{1,0:T(8,128)(2,1)} %param.7), channel_id=1, source_target_pairs={{0,1},{1,0},{2,3},{3,2},{4,5},{5,4},{6,7},{7,6},{8,9},{9,8},{10,11... | collective-permute-start | bytes 196616 | tf_op jit(solution)/shard_map/ppermute | solution.py:12
  9.0 1.8 %copy-start.2 = (bf16[128,256]{1,0:T(8,128)(2,1)S(1)}, bf16[128,256]{1,0:T(8,128)(2,1)}, u32[]{:S(2)}) copy-start(bf16[128,256]{1,0:T(8,128)(2,1)} %param.7) | copy-start | bytes 196612
  10.8 1.8 %copy-start.3 = (bf16[128,256]{1,0:T(8,128)(2,1)S(1)}, bf16[128,256]{1,0:T(8,128)(2,1)}, u32[]{:S(2)}) copy-start(bf16[128,256]{1,0:T(8,128)(2,1)} %param.5) | copy-start | bytes 196612
  12.6 6.5 %collective-permute-start.5 = (bf16[512,256]{1,0:T(8,128)(2,1)S(1)}, bf16[512,256]{1,0:T(8,128)(2,1)S(1)}, u32[]{:S(2)}, u32[]{:S(2)}) collective-permute-start(bf16[512,256]{1,0:T(8,128)(2,1)S(1)} %pad_maximum_fusion), channel_id=1, source_target_pairs={{0,4},{2,6},{4,0},{6,2},{8,12},{10,14},{12,8},{14,10},{16,20},{18,... | collective-permute-start | bytes 786440 | tf_op jit(solution)/shard_map/ppermute | solution.py:12
  14.2 5.2 %collective-permute-start.4 = (bf16[512,256]{1,0:T(8,128)(2,1)S(1)}, bf16[512,256]{1,0:T(8,128)(2,1)S(1)}, u32[]{:S(2)}, u32[]{:S(2)}) collective-permute-start(bf16[512,256]{1,0:T(8,128)(2,1)S(1)} %pad_maximum_fusion), channel_id=1, source_target_pairs={{0,2},{2,0},{4,6},{6,4},{8,10},{10,8},{12,14},{14,12},{16,18},{18,... | collective-permute-start | bytes 786440 | tf_op jit(solution)/shard_map/ppermute | solution.py:12
  19.1 1.5 %collective-permute-start.6 = (bf16[512,256]{1,0:T(8,128)(2,1)S(1)}, bf16[512,256]{1,0:T(8,128)(2,1)S(1)}, u32[]{:S(2)}, u32[]{:S(2)}) collective-permute-start(bf16[512,256]{1,0:T(8,128)(2,1)S(1)} %collective-permute-done.5), channel_id=1, source_target_pairs={{0,2},{2,0},{4,6},{6,4},{8,10},{10,8},{12,14},{14,12},{16,18},{18,... | collective-permute-start | bytes 786440 | tf_op jit(solution)/shard_map/ppermute | solution.py:12
  20.9 5.6 %collective-permute-start.7 = (bf16[2,128,256]{2,1,0:T(8,128)(2,1)S(1)}, bf16[2,128,256]{2,1,0:T(8,128)(2,1)S(1)}, u32[]{:S(2)}, u32[]{:S(2)}) collective-permute-start(bf16[2,128,256]{2,1,0:T(8,128)(2,1)S(1)} %fusion.5), channel_id=1, source_target_pairs={{0,1},{1,0},{2,3},{3,2},{4,5},{5,4},{6,7},{7,6},{8,9},{9,8},{10,11... | collective-permute-start | bytes 393224 | tf_op jit(solution)/shard_map/ppermute | solution.py:12
  27.4 3.9 %collective-permute-start.14 = (f32[128,256]{1,0:T(8,128)S(1)}, f32[128,256]{1,0:T(8,128)S(1)}, u32[]{:S(2)}, u32[]{:S(2)}) collective-permute-start(f32[128,256]{1,0:T(8,128)S(1)} %get-tuple-element.19), channel_id=1, source_target_pairs={{0,2},{2,0},{4,6},{6,4},{8,10},{10,8},{12,14},{14,12},{16,18},{18,... | collective-permute-start | bytes 393224 | tf_op jit(solution)/shard_map/ppermute | solution.py:12
  27.7 1.7 %collective-permute-start.9 = (bf16[4,128,256]{2,1,0:T(8,128)(2,1)S(1)}, bf16[4,128,256]{2,1,0:T(8,128)(2,1)S(1)}, u32[]{:S(2)}, u32[]{:S(2)}) collective-permute-start(bf16[4,128,256]{2,1,0:T(8,128)(2,1)S(1)} %fusion.1), channel_id=1, source_target_pairs={{0,2},{2,0},{4,6},{6,4},{8,10},{10,8},{12,14},{14,12},{16,18},{18,... | collective-permute-start | bytes 786440 | tf_op jit(solution)/shard_map/ppermute | solution.py:12
  28.6 9.9 %collective-permute-start.8 = (bf16[4,128,256]{2,1,0:T(8,128)(2,1)S(1)}, bf16[4,128,256]{2,1,0:T(8,128)(2,1)S(1)}, u32[]{:S(2)}, u32[]{:S(2)}) collective-permute-start(bf16[4,128,256]{2,1,0:T(8,128)(2,1)S(1)} %fusion), channel_id=1, source_target_pairs={{0,2},{2,0},{4,6},{6,4},{8,10},{10,8},{12,14},{14,12},{16,18},{18,... | collective-permute-start | bytes 786440 | tf_op jit(solution)/shard_map/ppermute | solution.py:12
  29.7 8.8 %collective-permute-start.10 = (bf16[4,128,256]{2,1,0:T(8,128)(2,1)S(1)}, bf16[4,128,256]{2,1,0:T(8,128)(2,1)S(1)}, u32[]{:S(2)}, u32[]{:S(2)}) collective-permute-start(bf16[4,128,256]{2,1,0:T(8,128)(2,1)S(1)} %add_convert_fusion.refs_2_), channel_id=1, source_target_pairs={{0,4},{2,6},{4,0},{6,2},{8,12},{10,14},{12,8},{14,10},{16,20},{18,... | collective-permute-start | bytes 786440 | tf_op jit(solution)/shard_map/ppermute | solution.py:12
  31.3 4.3 %collective-permute-start.15 = (bf16[128,256]{1,0:T(8,128)(2,1)S(1)}, bf16[128,256]{1,0:T(8,128)(2,1)S(1)}, u32[]{:S(2)}, u32[]{:S(2)}) collective-permute-start(bf16[128,256]{1,0:T(8,128)(2,1)S(1)} %shard_map.77.refs_0_), channel_id=1, source_target_pairs={{0,8},{2,10},{4,12},{6,14},{8,0},{10,2},{12,4},{14,6},{16,24},{18,... | collective-permute-start | bytes 196616 | tf_op jit(solution)/shard_map/ppermute | solution.py:12
  35.7 7.4 %collective-permute-start.16 = (bf16[128,256]{1,0:T(8,128)(2,1)S(1)}, bf16[128,256]{1,0:T(8,128)(2,1)S(1)}, u32[]{:S(2)}, u32[]{:S(2)}) collective-permute-start(bf16[128,256]{1,0:T(8,128)(2,1)S(1)} %shard_map.78.refs_0_), channel_id=1, source_target_pairs={{0,16},{2,18},{4,20},{6,22},{8,24},{10,26},{12,28},{14,30},{16,0},... | collective-permute-start | bytes 196616 | tf_op jit(solution)/shard_map/ppermute | solution.py:12
  38.6 8.9 %collective-permute-start.12 = (bf16[128,256]{1,0:T(8,128)(2,1)S(1)}, bf16[128,256]{1,0:T(8,128)(2,1)S(1)}, u32[]{:S(2)}, u32[]{:S(2)}) collective-permute-start(bf16[128,256]{1,0:T(8,128)(2,1)S(1)} %get-tuple-element.22), channel_id=1, source_target_pairs={{0,16},{2,18},{4,20},{6,22},{8,24},{10,26},{12,28},{14,30},{16,0},... | collective-permute-start | bytes 196616 | tf_op jit(solution)/shard_map/ppermute | solution.py:12
  41.3 6.2 %collective-permute-start.11 = (bf16[128,256]{1,0:T(8,128)(2,1)S(1)}, bf16[128,256]{1,0:T(8,128)(2,1)S(1)}, u32[]{:S(2)}, u32[]{:S(2)}) collective-permute-start(bf16[128,256]{1,0:T(8,128)(2,1)S(1)} %get-tuple-element.23), channel_id=1, source_target_pairs={{0,8},{2,10},{4,12},{6,14},{8,0},{10,2},{12,4},{14,6},{16,24},{18,... | collective-permute-start | bytes 196616 | tf_op jit(solution)/shard_map/ppermute | solution.py:12
  42.2 6.1 %collective-permute-start.13 = (bf16[128,256]{1,0:T(8,128)(2,1)S(1)}, bf16[128,256]{1,0:T(8,128)(2,1)S(1)}, u32[]{:S(2)}, u32[]{:S(2)}) collective-permute-start(bf16[128,256]{1,0:T(8,128)(2,1)S(1)} %get-tuple-element.21.refs_2_), channel_id=1, source_target_pairs={{0,24},{2,26},{4,28},{6,30},{8,16},{10,18},{12,20},{14,22},{16,8},... | collective-permute-start | bytes 196616 | tf_op jit(solution)/shard_map/ppermute | solution.py:12
  43.1 4.3 %collective-permute-start.17 = (bf16[128,256]{1,0:T(8,128)(2,1)S(1)}, bf16[128,256]{1,0:T(8,128)(2,1)S(1)}, u32[]{:S(2)}, u32[]{:S(2)}) collective-permute-start(bf16[128,256]{1,0:T(8,128)(2,1)S(1)} %shard_map.79.refs_0_), channel_id=1, source_target_pairs={{0,4},{2,6},{4,0},{6,2},{8,12},{10,14},{12,8},{14,10},{16,20},{18,... | collective-permute-start | bytes 196616 | tf_op jit(solution)/shard_map/ppermute | solution.py:12
  47.4 1.4 %collective-permute-start.18 = (f32[128,256]{1,0:T(8,128)S(1)}, f32[128,256]{1,0:T(8,128)S(1)}, u32[]{:S(2)}, u32[]{:S(2)}) collective-permute-start(f32[128,256]{1,0:T(8,128)S(1)} %shard_map.80.refs_1_), channel_id=1, source_target_pairs={{0,2},{2,0},{4,6},{6,4},{8,10},{10,8},{12,14},{14,12},{16,18},{18,... | collective-permute-start | bytes 393224 | tf_op jit(solution)/shard_map/ppermute | solution.py:12

commit v4 on v3

--- a/solution.py
+++ b/solution.py
@@ -71,6 +71,35 @@
         compiler_params=pltpu.CompilerParams(vmem_limit_bytes=4 << 20),
         cost_estimate=pl.CostEstimate(flops=10**6, bytes_accessed=10**6, transcendentals=0),
     )(core.reshape(1), *terms, half, other)
+
+
+def dense_tile(tiles, slots, row, col, row_count, col_count, flops, later_than):
+    blocks, side, _ = tiles.shape
+    depth = row_count // 4
+
+    def body(slots_ref, row_ref, tiles_ref, *refs):
+        out_ref = refs[-1]
+        out_ref[...] = jnp.zeros_like(out_ref)
+
+        @pl.loop(0, blocks)
+        def _(k):
+            slot = slots_ref[k]
+            relative = (slot & (row_count - 1)) ^ row_ref[0]
+            place = (relative & 1) * (row_count // 2) + (relative >> 1 & 1) * depth
+            place = place + (relative >> 2) + (slot - (slot & (row_count - 1)))
+            out_ref[place] = tiles_ref[k]
+
+    shape = jax.ShapeDtypeStruct((col_count * row_count, side, side), tiles.dtype)
+    smem = pl.BlockSpec(memory_space=pltpu.SMEM)
+    vmem = pl.BlockSpec(memory_space=pltpu.VMEM)
+    return pl.pallas_call(
+        body,
+        out_shape=shape,
+        in_specs=[smem, smem, vmem] + [pl.BlockSpec(memory_space=pl.ANY)] * len(later_than),
+        out_specs=vmem,
+        compiler_params=pltpu.CompilerParams(vmem_limit_bytes=(2 * (blocks + row_count * col_count) * side * side * 2) + (1 << 20)),
+        cost_estimate=pl.CostEstimate(flops=flops, bytes_accessed=10**6, transcendentals=0),
+    )(slots, row.reshape(1), tiles, *later_than)
 
 
 def rounded(x):
@@ -91,18 +120,23 @@
     f32 = jnp.float32
     bf16 = jnp.bfloat16
 
-    relative = (tile_slots % row_count) ^ row
-    position = (relative % 2) * (row_count // 2) + (relative // 2 % 2) * depth + relative // 4
-    position = tile_slots // row_count * row_count + position
-    dense = jnp.zeros((col_count * row_count, side, side), bf16).at[position].set(tile_blocks)
+    def direct(bit, low, high):
+        return [swap(features, "row", 4 * k + bit) if k or bit else features for k in range(low, high)]
+
+    straight = 1
+    far = jnp.concatenate(direct(0, straight, depth))
+    near = direct(0, 0, straight)
+    near_x = jnp.concatenate(direct(2, 0, straight))
+    panel = jnp.concatenate(near + [far])
+    far_x = swap(far, "row", 2)
+
     cotangent = grad_out
     for bit in bits(col_count):
         got = swap(cotangent, "col", bit)
         low = jnp.where(col & bit == 0, cotangent, got)
         high = jnp.where(col & bit == 0, got, cotangent)
         cotangent = jnp.concatenate([low, high])
-    panel = jnp.concatenate([features] + [swap(features, "row", 4 * k) for k in range(1, depth)])
-    panel, dense, cotangent = lax.optimization_barrier((panel, dense, cotangent))
+    dense = dense_tile(tile_blocks, tile_slots, row, col, row_count, col_count, 3000000000, [far])
     dense = dense.reshape(col_count, 4, depth, side, side)
 
     def forward(quarter, block):
@@ -118,11 +152,13 @@
             "bpij,bif->pjf", dense[:, quarter], row_panel, preferred_element_type=f32
         )
 
-    panel_x = swap(panel, "row", 2)
     panel_c = swap(panel, "row", 1)
+    near_xc = swap(near_x, "row", 1)
     partial = forward(0, panel) + forward(2, panel_c)
-    panel_xc = swap(panel_x, "row", 1)
-    partial = partial + forward(1, panel_x) + forward(3, panel_xc)
+    far_x, cotangent, partial = lax.optimization_barrier((far_x, cotangent, partial))
+    far_xc = swap(far_x, "row", 1)
+    partial = partial + forward(1, jnp.concatenate([near_x, far_x]))
+    partial = partial + forward(3, jnp.concatenate([near_xc, far_xc]))
     for bit in bits(col_count):
         sent = rounded(partial)
         partial = sent.astype(f32) + swap(sent, "col", bit).astype(f32)

time: 49.8 us -> 48.7 us (0.978)
  waiting for transfers between devices: 19.1 us -> 17.3 us
  Pallas kernels: 0.85 us -> 1.79 us
    ppermute x19 -> x21, waiting for transfers between devices: 19.1 us -> 17.3 us  [swap(): lax.ppermute(x, axis, [(i, i ^ bit) for i in range(lax.axis_size(axis))])]
    scatter x1 -> x0, local copies, waits for them, and re-layouts: 1.7 us -> none  [local(): jnp.zeros((col_count * row_count, side, side), bf16).at[position]]
    unnamed x8 -> x9, local copies, waits for them, and re-layouts: 0.03 us -> 1.53 us
    pallas_call x0 -> x1, Pallas kernels: none -> 0.94 us  [dense_tile(): pl.pallas_call(body, out_shape=shape, in_specs=[smem, smem, vmem] + [pl.B...]
    select_n x1, other arithmetic: 0.01 us -> 0.85 us  [local(): low = jnp.where(col & bit == 0, cotangent, got)]
    select_n x1 -> x0, other arithmetic: 0.69 us -> none  [local(): jnp.zeros((col_count * row_count, side, side), bf16).at[position]]
    ppermute x19 -> x21, starting transfers between devices: 22.5 us -> 22.4 us  [swap(): lax.ppermute(x, axis, [(i, i ^ bit) for i in range(lax.axis_size(axis))])]
  transfers between devices with their start and end apart: 19 -> 21, of which waited for: 10 -> 9; matrix products, arithmetic and copies ran while one was open for 10% -> 9% of each run, Pallas kernels for 0% -> 2%
where the time goes in v4:
time: 48.7 us; the launch traced here: 48.4 us
  starting transfers between devices  22.4 us (46%)
  waiting for transfers between devices  17.3 us (36%)
  matrix products  2.63 us (5%)
  Pallas kernels  1.79 us (4%)
  other arithmetic  1.78 us (4%)
  local copies, waits for them, and re-layouts  1.59 us (3%)
  between operations  0.93 us (2%)
    ppermute x21, starting transfers between devices, swap(): lax.ppermute(x, axis, [(i, i ^ bit) for i in range(lax.axis_size(axis))])  22.4 us
    ppermute x21, waiting for transfers between devices, swap(): lax.ppermute(x, axis, [(i, i ^ bit) for i in range(lax.axis_size(axis))])  17.3 us
    unnamed x9, local copies, waits for them, and re-layouts  1.53 us
    dot_general x4, matrix products, backward(): jnp.einsum('bpij,bif->pjf', dense[:, quarter], row_panel, preferred_eleme...  1.1 us
  transfers between devices with their start and end apart: 21, of which 9 were waited for; matrix products, arithmetic and copies ran while one was open for 9% of the time, Pallas kernels for 2%

profile of v4, /device:TPU:0, one launch (start us, length us, event | category | flops | bytes accessed | tf_op | source)
XLA Modules:
  0.0 48.4 jit_solution(2658244981298177043)
XLA Ops:
  0.7 5.1 %collective-permute-start.2 = (bf16[128,256]{1,0:T(8,128)(2,1)}, bf16[128,256]{1,0:T(8,128)(2,1)S(1)}, u32[]{:S(2)}, u32[]{:S(2)}) collective-permute-start(bf16[128,256]{1,0:T(8,128)(2,1)} %param.5), channel_id=1, source_target_pairs={{0,24},{2,26},{4,28},{6,30},{8,16},{10,18},{12,20},{14,22},{16,8},... | collective-permute-start | bytes 196616 | tf_op jit(solution)/shard_map/ppermute | solution.py:12
  6.4 1.6 %collective-permute-start.6 = (bf16[128,256]{1,0:T(8,128)(2,1)}, bf16[128,256]{1,0:T(8,128)(2,1)S(1)}, u32[]{:S(2)}, u32[]{:S(2)}) collective-permute-start(bf16[128,256]{1,0:T(8,128)(2,1)} %param.5), channel_id=1, source_target_pairs={{0,4},{2,6},{4,0},{6,2},{8,12},{10,14},{12,8},{14,10},{16,20},{18,... | collective-permute-start | bytes 196616 | tf_op jit(solution)/shard_map/ppermute | solution.py:12
  8.0 1.5 %collective-permute-start.4 = (bf16[128,256]{1,0:T(8,128)(2,1)}, bf16[128,256]{1,0:T(8,128)(2,1)S(1)}, u32[]{:S(2)}, u32[]{:S(2)}) collective-permute-start(bf16[128,256]{1,0:T(8,128)(2,1)} %param.7), channel_id=1, source_target_pairs={{0,1},{1,0},{2,3},{3,2},{4,5},{5,4},{6,7},{7,6},{8,9},{9,8},{10,11... | collective-permute-start | bytes 196616 | tf_op jit(solution)/shard_map/ppermute | solution.py:12
  9.6 0.8 %constant_dynamic-update-slice_fusion.6 = bf16[512,256]{1,0:T(8,128)(2,1)S(1)} fusion(bf16[128,256]{1,0:T(8,128)(2,1)} %param.5), kind=kLoop, calls=%fused_computation.41 | loop fusion | bytes 131072
  10.4 1.2 %collective-permute-done.1 = bf16[128,256]{1,0:T(8,128)(2,1)S(1)} collective-permute-done((bf16[128,256]{1,0:T(8,128)(2,1)}, bf16[128,256]{1,0:T(8,128)(2,1)S(1)}, u32[]{:S(2)}, u32[]{:S(2)}) %collective-permute-start.1) | collective-permute-done | bytes 65568 | tf_op jit(solution)/shard_map/ppermute | solution.py:12
  11.6 1.6 %collective-permute-start.3 = (bf16[384,256]{1,0:T(8,128)(2,1)S(1)}, bf16[384,256]{1,0:T(8,128)(2,1)S(1)}, u32[]{:S(2)}, u32[]{:S(2)}) collective-permute-start(bf16[384,256]{1,0:T(8,128)(2,1)S(1)} %get-tuple-element.29.refs_0_), channel_id=1, source_target_pairs={{0,4},{2,6},{4,0},{6,2},{8,12},{10,14},{12,8},{14,10},{16,20},{18,... | collective-permute-start | bytes 589832 | tf_op jit(solution)/shard_map/ppermute | solution.py:12
  13.2 0.9 %broadcast_select_fusion.1 = (bf16[128,256]{1,0:T(8,128)(2,1)S(1)}, bf16[128,256]{1,0:T(8,128)(2,1)S(1)}) fusion(bf16[128,256]{1,0:T(8,128)(2,1)} %param.7, bf16[128,256]{1,0:T(8,128)(2,1)S(1)} %collective-permute-done.4, pred[]{:T(512)S(6)} %eq.4), kind=kLoop, calls=%fused_computation.34 | loop fusion | flops 65536 | bytes 262145 | tf_op jit(solution)/shard_map/jit(_where)/select_n | solution.py:136
  14.7 0.7 %copy-done.2 = s32[1,1,24]{2,1,0:T(1,128)S(1)} copy-done((s32[1,1,24]{2,1,0:T(1,128)S(1)}, s32[1,1,24]{2,1,0:T(1,128)}, u32[]{:S(2)}) %copy-start.2) | copy-done | bytes 120
  15.3 0.9 %shard_map.76 = bf16[32,128,128]{2,1,0:T(8,128)(2,1)S(1)} custom-call(s32[24]{0:T(128)S(1)} %bitcast.117, s32[1]{0:T(128)} %bitcast.1.row_ref, bf16[24,128,128]{2,1,0:T(8,128)(2,1)S(1)} %bitcast.116, bf16[384,256]{1,0:T(8,128)(2,1)S(1)} %get-tuple-element.29.refs_0_), custom_call_target="tpu_custom_call" | custom-call | flops 3000000000 | bytes 1000000 | tf_op jit(solution)/shard_map/pallas_call | solution.py:95
  16.7 1.4 %collective-permute-done.3 = bf16[384,256]{1,0:T(8,128)(2,1)S(1)} collective-permute-done((bf16[384,256]{1,0:T(8,128)(2,1)S(1)}, bf16[384,256]{1,0:T(8,128)(2,1)S(1)}, u32[]{:S(2)}, u32[]{:S(2)}) %collective-permute-start.3) | collective-permute-done | bytes 196640 | tf_op jit(solution)/shard_map/ppermute | solution.py:12
  18.4 1.2 %collective-permute-done.8 = bf16[384,256]{1,0:T(8,128)(2,1)S(1)} collective-permute-done((bf16[384,256]{1,0:T(8,128)(2,1)S(1)}, bf16[384,256]{1,0:T(8,128)(2,1)S(1)}, u32[]{:S(2)}, u32[]{:S(2)}) %collective-permute-start.8) | collective-permute-done | bytes 196640 | tf_op jit(solution)/shard_map/ppermute | solution.py:12
  19.9 1.8 %collective-permute-start.9 = (bf16[2,128,256]{2,1,0:T(8,128)(2,1)S(1)}, bf16[2,128,256]{2,1,0:T(8,128)(2,1)S(1)}, u32[]{:S(2)}, u32[]{:S(2)}) collective-permute-start(bf16[2,128,256]{2,1,0:T(8,128)(2,1)S(1)} %fusion.4), channel_id=1, source_target_pairs={{0,1},{1,0},{2,3},{3,2},{4,5},{5,4},{6,7},{7,6},{8,9},{9,8},{10,11... | collective-permute-start | bytes 393224 | tf_op jit(solution)/shard_map/ppermute | solution.py:12
  21.6 3.8 %collective-permute-done.9 = bf16[2,128,256]{2,1,0:T(8,128)(2,1)S(1)} collective-permute-done((bf16[2,128,256]{2,1,0:T(8,128)(2,1)S(1)}, bf16[2,128,256]{2,1,0:T(8,128)(2,1)S(1)}, u32[]{:S(2)}, u32[]{:S(2)}) %collective-permute-start.9) | collective-permute-done | bytes 131104 | tf_op jit(solution)/shard_map/ppermute | solution.py:12
  28.7 1.8 %collective-permute-start.12 = (bf16[4,128,256]{2,1,0:T(8,128)(2,1)S(1)}, bf16[4,128,256]{2,1,0:T(8,128)(2,1)S(1)}, u32[]{:S(2)}, u32[]{:S(2)}) collective-permute-start(bf16[4,128,256]{2,1,0:T(8,128)(2,1)S(1)} %add_convert_fusion.refs_2_), channel_id=1, source_target_pairs={{0,4},{2,6},{4,0},{6,2},{8,12},{10,14},{12,8},{14,10},{16,20},{18,... | collective-permute-start | bytes 786440 | tf_op jit(solution)/shard_map/ppermute | solution.py:12
  31.3 3.5 %collective-permute-done.17.refs_1_ = bf16[128,256]{1,0:T(8,128)(2,1)S(1)} collective-permute-done((bf16[128,256]{1,0:T(8,128)(2,1)S(1)}, bf16[128,256]{1,0:T(8,128)(2,1)S(1)}, u32[]{:S(2)}, u32[]{:S(2)}) %collective-permute-start.17) | collective-permute-done | bytes 65568 | tf_op jit(solution)/shard_map/ppermute | solution.py:12
  34.8 0.7 %collective-permute-start.18 = (bf16[128,256]{1,0:T(8,128)(2,1)S(1)}, bf16[128,256]{1,0:T(8,128)(2,1)S(1)}, u32[]{:S(2)}, u32[]{:S(2)}) collective-permute-start(bf16[128,256]{1,0:T(8,128)(2,1)S(1)} %shard_map.79.refs_0_), channel_id=1, source_target_pairs={{0,16},{2,18},{4,20},{6,22},{8,24},{10,26},{12,28},{14,30},{16,0},... | collective-permute-start | bytes 196616 | tf_op jit(solution)/shard_map/ppermute | solution.py:12
  35.5 1.8 %collective-permute-done.12 = bf16[4,128,256]{2,1,0:T(8,128)(2,1)S(1)} collective-permute-done((bf16[4,128,256]{2,1,0:T(8,128)(2,1)S(1)}, bf16[4,128,256]{2,1,0:T(8,128)(2,1)S(1)}, u32[]{:S(2)}, u32[]{:S(2)}) %collective-permute-start.12) | collective-permute-done | bytes 262176 | tf_op jit(solution)/shard_map/ppermute | solution.py:12
  37.5 0.9 %collective-permute-start.14 = (bf16[128,256]{1,0:T(8,128)(2,1)S(1)}, bf16[128,256]{1,0:T(8,128)(2,1)S(1)}, u32[]{:S(2)}, u32[]{:S(2)}) collective-permute-start(bf16[128,256]{1,0:T(8,128)(2,1)S(1)} %get-tuple-element.22), channel_id=1, source_target_pairs={{0,16},{2,18},{4,20},{6,22},{8,24},{10,26},{12,28},{14,30},{16,0},... | collective-permute-start | bytes 196616 | tf_op jit(solution)/shard_map/ppermute | solution.py:12
  38.3 1.7 %collective-permute-start.13 = (bf16[128,256]{1,0:T(8,128)(2,1)S(1)}, bf16[128,256]{1,0:T(8,128)(2,1)S(1)}, u32[]{:S(2)}, u32[]{:S(2)}) collective-permute-start(bf16[128,256]{1,0:T(8,128)(2,1)S(1)} %get-tuple-element.23), channel_id=1, source_target_pairs={{0,8},{2,10},{4,12},{6,14},{8,0},{10,2},{12,4},{14,6},{16,24},{18,... | collective-permute-start | bytes 196616 | tf_op jit(solution)/shard_map/ppermute | solution.py:12
  40.0 1.9 %collective-permute-start.15 = (bf16[128,256]{1,0:T(8,128)(2,1)S(1)}, bf16[128,256]{1,0:T(8,128)(2,1)S(1)}, u32[]{:S(2)}, u32[]{:S(2)}) collective-permute-start(bf16[128,256]{1,0:T(8,128)(2,1)S(1)} %get-tuple-element.21.refs_2_), channel_id=1, source_target_pairs={{0,24},{2,26},{4,28},{6,30},{8,16},{10,18},{12,20},{14,22},{16,8},... | collective-permute-start | bytes 196616 | tf_op jit(solution)/shard_map/ppermute | solution.py:12
  41.9 1.7 %collective-permute-start.19 = (bf16[128,256]{1,0:T(8,128)(2,1)S(1)}, bf16[128,256]{1,0:T(8,128)(2,1)S(1)}, u32[]{:S(2)}, u32[]{:S(2)}) collective-permute-start(bf16[128,256]{1,0:T(8,128)(2,1)S(1)} %shard_map.80.refs_0_), channel_id=1, source_target_pairs={{0,4},{2,6},{4,0},{6,2},{8,12},{10,14},{12,8},{14,10},{16,20},{18,... | collective-permute-start | bytes 196616 | tf_op jit(solution)/shard_map/ppermute | solution.py:12
  43.7 2.6 %collective-permute-done.19.refs_1_ = bf16[128,256]{1,0:T(8,128)(2,1)S(1)} collective-permute-done((bf16[128,256]{1,0:T(8,128)(2,1)S(1)}, bf16[128,256]{1,0:T(8,128)(2,1)S(1)}, u32[]{:S(2)}, u32[]{:S(2)}) %collective-permute-start.19) | collective-permute-done | bytes 65568 | tf_op jit(solution)/shard_map/ppermute | solution.py:12
  46.4 1.3 %collective-permute-done.20.refs_2_ = f32[128,256]{1,0:T(8,128)S(1)} collective-permute-done((f32[128,256]{1,0:T(8,128)S(1)}, f32[128,256]{1,0:T(8,128)S(1)}, u32[]{:S(2)}, u32[]{:S(2)}) %collective-permute-start.20) | collective-permute-done | bytes 131104 | tf_op jit(solution)/shard_map/ppermute | solution.py:12
  47.7 0.7 %shard_map.82 = (bf16[128,256]{1,0:T(8,128)(2,1)}, f32[256,256]{1,0:T(8,128)}) custom-call(s32[1]{0:T(128)} %bitcast.25.core_ref, f32[128,256]{1,0:T(8,128)S(1)} %shard_map.77.refs_0_, f32[128,256]{1,0:T(8,128)S(1)} %shard_map.81.refs_1_, f32[128,256]{1,0:T(8,128)S(1)} %collective-permute-done.20.refs_2_), custom_call_target="tpu_custom_call" | custom-call | flops 1000000 | bytes 1000000 | tf_op jit(solution)/shard_map/pallas_call | solution.py:63
  (57 shorter events, 6.5 us)
Async XLA Ops:
  0.6 24.9 %copy-start = (bf16[256,256]{1,0:T(8,128)(2,1)S(1)}, bf16[256,256]{1,0:T(8,128)(2,1)}, u32[]{:S(2)}) copy-start(bf16[256,256]{1,0:T(8,128)(2,1)} %param.6) | copy-start | bytes 393220
  0.6 14.0 %copy-start.1 = (bf16[1,1,24,128,128]{4,3,2,1,0:T(8,128)(2,1)S(1)}, bf16[1,1,24,128,128]{4,3,2,1,0:T(8,128)(2,1)}, u32[]{:S(2)}) copy-start(bf16[1,1,24,128,128]{4,3,2,1,0:T(8,128)(2,1)} %param.8) | copy-start | bytes 2359300
  0.7 10.9 %collective-permute-start.2 = (bf16[128,256]{1,0:T(8,128)(2,1)}, bf16[128,256]{1,0:T(8,128)(2,1)S(1)}, u32[]{:S(2)}, u32[]{:S(2)}) collective-permute-start(bf16[128,256]{1,0:T(8,128)(2,1)} %param.5), channel_id=1, source_target_pairs={{0,24},{2,26},{4,28},{6,30},{8,16},{10,18},{12,20},{14,22},{16,8},... | collective-permute-start | bytes 196616 | tf_op jit(solution)/shard_map/ppermute | solution.py:12
  5.8 5.8 %collective-permute-start.1 = (bf16[128,256]{1,0:T(8,128)(2,1)}, bf16[128,256]{1,0:T(8,128)(2,1)S(1)}, u32[]{:S(2)}, u32[]{:S(2)}) collective-permute-start(bf16[128,256]{1,0:T(8,128)(2,1)} %param.5), channel_id=1, source_target_pairs={{0,16},{2,18},{4,20},{6,22},{8,24},{10,26},{12,28},{14,30},{16,0},... | collective-permute-start | bytes 196616 | tf_op jit(solution)/shard_map/ppermute | solution.py:12
  5.8 4.6 %collective-permute-start = (bf16[128,256]{1,0:T(8,128)(2,1)}, bf16[128,256]{1,0:T(8,128)(2,1)S(1)}, u32[]{:S(2)}, u32[]{:S(2)}) collective-permute-start(bf16[128,256]{1,0:T(8,128)(2,1)} %param.5), channel_id=1, source_target_pairs={{0,8},{2,10},{4,12},{6,14},{8,0},{10,2},{12,4},{14,6},{16,24},{18,... | collective-permute-start | bytes 196616 | tf_op jit(solution)/shard_map/ppermute | solution.py:12
  6.4 7.7 %collective-permute-start.6 = (bf16[128,256]{1,0:T(8,128)(2,1)}, bf16[128,256]{1,0:T(8,128)(2,1)S(1)}, u32[]{:S(2)}, u32[]{:S(2)}) collective-permute-start(bf16[128,256]{1,0:T(8,128)(2,1)} %param.5), channel_id=1, source_target_pairs={{0,4},{2,6},{4,0},{6,2},{8,12},{10,14},{12,8},{14,10},{16,20},{18,... | collective-permute-start | bytes 196616 | tf_op jit(solution)/shard_map/ppermute | solution.py:12
  8.0 5.1 %collective-permute-start.4 = (bf16[128,256]{1,0:T(8,128)(2,1)}, bf16[128,256]{1,0:T(8,128)(2,1)S(1)}, u32[]{:S(2)}, u32[]{:S(2)}) collective-permute-start(bf16[128,256]{1,0:T(8,128)(2,1)} %param.7), channel_id=1, source_target_pairs={{0,1},{1,0},{2,3},{3,2},{4,5},{5,4},{6,7},{7,6},{8,9},{9,8},{10,11... | collective-permute-start | bytes 196616 | tf_op jit(solution)/shard_map/ppermute | solution.py:12
  11.6 6.5 %collective-permute-start.3 = (bf16[384,256]{1,0:T(8,128)(2,1)S(1)}, bf16[384,256]{1,0:T(8,128)(2,1)S(1)}, u32[]{:S(2)}, u32[]{:S(2)}) collective-permute-start(bf16[384,256]{1,0:T(8,128)(2,1)S(1)} %get-tuple-element.29.refs_0_), channel_id=1, source_target_pairs={{0,4},{2,6},{4,0},{6,2},{8,12},{10,14},{12,8},{14,10},{16,20},{18,... | collective-permute-start | bytes 589832 | tf_op jit(solution)/shard_map/ppermute | solution.py:12
  13.2 3.1 %collective-permute-start.5 = (bf16[512,256]{1,0:T(8,128)(2,1)S(1)}, bf16[512,256]{1,0:T(8,128)(2,1)S(1)}, u32[]{:S(2)}, u32[]{:S(2)}) collective-permute-start(bf16[512,256]{1,0:T(8,128)(2,1)S(1)} %get-tuple-element.28), channel_id=1, source_target_pairs={{0,2},{2,0},{4,6},{6,4},{8,10},{10,8},{12,14},{14,12},{16,18},{18,... | collective-permute-start | bytes 786440 | tf_op jit(solution)/shard_map/ppermute | solution.py:12
  14.1 4.4 %collective-permute-start.7 = (bf16[128,256]{1,0:T(8,128)(2,1)S(1)}, bf16[128,256]{1,0:T(8,128)(2,1)S(1)}, u32[]{:S(2)}, u32[]{:S(2)}) collective-permute-start(bf16[128,256]{1,0:T(8,128)(2,1)S(1)} %collective-permute-done.6), channel_id=1, source_target_pairs={{0,2},{2,0},{4,6},{6,4},{8,10},{10,8},{12,14},{14,12},{16,18},{18,... | collective-permute-start | bytes 196616 | tf_op jit(solution)/shard_map/ppermute | solution.py:12
  14.6 0.7 %copy-start.2 = (s32[1,1,24]{2,1,0:T(1,128)S(1)}, s32[1,1,24]{2,1,0:T(1,128)}, u32[]{:S(2)}) copy-start(s32[1,1,24]{2,1,0:T(1,128)} %param.9) | copy-start | bytes 292
  18.2 1.4 %collective-permute-start.8 = (bf16[384,256]{1,0:T(8,128)(2,1)S(1)}, bf16[384,256]{1,0:T(8,128)(2,1)S(1)}, u32[]{:S(2)}, u32[]{:S(2)}) collective-permute-start(bf16[384,256]{1,0:T(8,128)(2,1)S(1)} %collective-permute-done.3), channel_id=1, source_target_pairs={{0,2},{2,0},{4,6},{6,4},{8,10},{10,8},{12,14},{14,12},{16,18},{18,... | collective-permute-start | bytes 589832 | tf_op jit(solution)/shard_map/ppermute | solution.py:12
  19.9 5.6 %collective-permute-start.9 = (bf16[2,128,256]{2,1,0:T(8,128)(2,1)S(1)}, bf16[2,128,256]{2,1,0:T(8,128)(2,1)S(1)}, u32[]{:S(2)}, u32[]{:S(2)}) collective-permute-start(bf16[2,128,256]{2,1,0:T(8,128)(2,1)S(1)} %fusion.4), channel_id=1, source_target_pairs={{0,1},{1,0},{2,3},{3,2},{4,5},{5,4},{6,7},{7,6},{8,9},{9,8},{10,11... | collective-permute-start | bytes 393224 | tf_op jit(solution)/shard_map/ppermute | solution.py:12
  26.3 4.1 %collective-permute-start.16 = (f32[128,256]{1,0:T(8,128)S(1)}, f32[128,256]{1,0:T(8,128)S(1)}, u32[]{:S(2)}, u32[]{:S(2)}) collective-permute-start(f32[128,256]{1,0:T(8,128)S(1)} %get-tuple-element.19), channel_id=1, source_target_pairs={{0,2},{2,0},{4,6},{6,4},{8,10},{10,8},{12,14},{14,12},{16,18},{18,... | collective-permute-start | bytes 393224 | tf_op jit(solution)/shard_map/ppermute | solution.py:12
  26.7 1.7 %collective-permute-start.11 = (bf16[4,128,256]{2,1,0:T(8,128)(2,1)S(1)}, bf16[4,128,256]{2,1,0:T(8,128)(2,1)S(1)}, u32[]{:S(2)}, u32[]{:S(2)}) collective-permute-start(bf16[4,128,256]{2,1,0:T(8,128)(2,1)S(1)} %fusion.1), channel_id=1, source_target_pairs={{0,2},{2,0},{4,6},{6,4},{8,10},{10,8},{12,14},{14,12},{16,18},{18,... | collective-permute-start | bytes 786440 | tf_op jit(solution)/shard_map/ppermute | solution.py:12
  27.5 8.0 %collective-permute-start.10 = (bf16[4,128,256]{2,1,0:T(8,128)(2,1)S(1)}, bf16[4,128,256]{2,1,0:T(8,128)(2,1)S(1)}, u32[]{:S(2)}, u32[]{:S(2)}) collective-permute-start(bf16[4,128,256]{2,1,0:T(8,128)(2,1)S(1)} %fusion), channel_id=1, source_target_pairs={{0,2},{2,0},{4,6},{6,4},{8,10},{10,8},{12,14},{14,12},{16,18},{18,... | collective-permute-start | bytes 786440 | tf_op jit(solution)/shard_map/ppermute | solution.py:12
  28.7 8.7 %collective-permute-start.12 = (bf16[4,128,256]{2,1,0:T(8,128)(2,1)S(1)}, bf16[4,128,256]{2,1,0:T(8,128)(2,1)S(1)}, u32[]{:S(2)}, u32[]{:S(2)}) collective-permute-start(bf16[4,128,256]{2,1,0:T(8,128)(2,1)S(1)} %add_convert_fusion.refs_2_), channel_id=1, source_target_pairs={{0,4},{2,6},{4,0},{6,2},{8,12},{10,14},{12,8},{14,10},{16,20},{18,... | collective-permute-start | bytes 786440 | tf_op jit(solution)/shard_map/ppermute | solution.py:12
  30.5 4.3 %collective-permute-start.17 = (bf16[128,256]{1,0:T(8,128)(2,1)S(1)}, bf16[128,256]{1,0:T(8,128)(2,1)S(1)}, u32[]{:S(2)}, u32[]{:S(2)}) collective-permute-start(bf16[128,256]{1,0:T(8,128)(2,1)S(1)} %shard_map.78.refs_0_), channel_id=1, source_target_pairs={{0,8},{2,10},{4,12},{6,14},{8,0},{10,2},{12,4},{14,6},{16,24},{18,... | collective-permute-start | bytes 196616 | tf_op jit(solution)/shard_map/ppermute | solution.py:12
  34.8 7.1 %collective-permute-start.18 = (bf16[128,256]{1,0:T(8,128)(2,1)S(1)}, bf16[128,256]{1,0:T(8,128)(2,1)S(1)}, u32[]{:S(2)}, u32[]{:S(2)}) collective-permute-start(bf16[128,256]{1,0:T(8,128)(2,1)S(1)} %shard_map.79.refs_0_), channel_id=1, source_target_pairs={{0,16},{2,18},{4,20},{6,22},{8,24},{10,26},{12,28},{14,30},{16,0},... | collective-permute-start | bytes 196616 | tf_op jit(solution)/shard_map/ppermute | solution.py:12
  37.5 8.9 %collective-permute-start.14 = (bf16[128,256]{1,0:T(8,128)(2,1)S(1)}, bf16[128,256]{1,0:T(8,128)(2,1)S(1)}, u32[]{:S(2)}, u32[]{:S(2)}) collective-permute-start(bf16[128,256]{1,0:T(8,128)(2,1)S(1)} %get-tuple-element.22), channel_id=1, source_target_pairs={{0,16},{2,18},{4,20},{6,22},{8,24},{10,26},{12,28},{14,30},{16,0},... | collective-permute-start | bytes 196616 | tf_op jit(solution)/shard_map/ppermute | solution.py:12
  38.3 8.0 %collective-permute-start.13 = (bf16[128,256]{1,0:T(8,128)(2,1)S(1)}, bf16[128,256]{1,0:T(8,128)(2,1)S(1)}, u32[]{:S(2)}, u32[]{:S(2)}) collective-permute-start(bf16[128,256]{1,0:T(8,128)(2,1)S(1)} %get-tuple-element.23), channel_id=1, source_target_pairs={{0,8},{2,10},{4,12},{6,14},{8,0},{10,2},{12,4},{14,6},{16,24},{18,... | collective-permute-start | bytes 196616 | tf_op jit(solution)/shard_map/ppermute | solution.py:12
  40.0 6.4 %collective-permute-start.15 = (bf16[128,256]{1,0:T(8,128)(2,1)S(1)}, bf16[128,256]{1,0:T(8,128)(2,1)S(1)}, u32[]{:S(2)}, u32[]{:S(2)}) collective-permute-start(bf16[128,256]{1,0:T(8,128)(2,1)S(1)} %get-tuple-element.21.refs_2_), channel_id=1, source_target_pairs={{0,24},{2,26},{4,28},{6,30},{8,16},{10,18},{12,20},{14,22},{16,8},... | collective-permute-start | bytes 196616 | tf_op jit(solution)/shard_map/ppermute | solution.py:12
  41.9 4.3 %collective-permute-start.19 = (bf16[128,256]{1,0:T(8,128)(2,1)S(1)}, bf16[128,256]{1,0:T(8,128)(2,1)S(1)}, u32[]{:S(2)}, u32[]{:S(2)}) collective-permute-start(bf16[128,256]{1,0:T(8,128)(2,1)S(1)} %shard_map.80.refs_0_), channel_id=1, source_target_pairs={{0,4},{2,6},{4,0},{6,2},{8,12},{10,14},{12,8},{14,10},{16,20},{18,... | collective-permute-start | bytes 196616 | tf_op jit(solution)/shard_map/ppermute | solution.py:12
  46.3 1.4 %collective-permute-start.20 = (f32[128,256]{1,0:T(8,128)S(1)}, f32[128,256]{1,0:T(8,128)S(1)}, u32[]{:S(2)}, u32[]{:S(2)}) collective-permute-start(f32[128,256]{1,0:T(8,128)S(1)} %shard_map.81.refs_1_), channel_id=1, source_target_pairs={{0,2},{2,0},{4,6},{6,4},{8,10},{10,8},{12,14},{14,12},{16,18},{18,... | collective-permute-start | bytes 393224 | tf_op jit(solution)/shard_map/ppermute | solution.py:12

commit v5 on v4

--- a/solution.py
+++ b/solution.py
@@ -191,6 +191,8 @@
     for bit in bits(depth):
         last = [sent_z[-1]] if 2 * bit == depth else []
         half = total([half, swap(half, "row", 4 * bit)], bf16, 3000000000 if last else 100000000, last)
+    for k in (1,2,):
+        sent_z[k - 1] = total([sent_z[k - 1]], bf16, 100000000, [half])
     got_z = [swap(sent_z[k - 1], "row", 4 * k) for k in range(1, depth)]
     half = total([half, swap(half, "row", 2)], f32, 10**8)
     total_nodes = own_rows * row_count * col_count

time: 48.7 us -> 47.8 us (0.982)
  starting transfers between devices: 22.4 us -> 20.9 us
  waiting for transfers between devices: 17.3 us -> 17.9 us
    ppermute x21, starting transfers between devices: 22.4 us -> 20.9 us  [swap(): lax.ppermute(x, axis, [(i, i ^ bit) for i in range(lax.axis_size(axis))])]
    ppermute x21, waiting for transfers between devices: 17.3 us -> 17.9 us  [swap(): lax.ppermute(x, axis, [(i, i ^ bit) for i in range(lax.axis_size(axis))])]
  transfers between devices with their start and end apart: 21 -> 21, of which waited for: 9 -> 11; matrix products, arithmetic and copies ran while one was open for 9% -> 9% of each run, Pallas kernels for 2% -> 2%
where the time goes in v5:
time: 47.8 us; the launch traced here: 47.5 us
  starting transfers between devices  20.9 us (44%)
  waiting for transfers between devices  17.9 us (37%)
  matrix products  2.63 us (6%)
  Pallas kernels  1.8 us (4%)
  other arithmetic  1.78 us (4%)
  local copies, waits for them, and re-layouts  1.59 us (3%)
  between operations  0.93 us (2%)
    ppermute x21, starting transfers between devices, swap(): lax.ppermute(x, axis, [(i, i ^ bit) for i in range(lax.axis_size(axis))])  20.9 us
    ppermute x21, waiting for transfers between devices, swap(): lax.ppermute(x, axis, [(i, i ^ bit) for i in range(lax.axis_size(axis))])  17.9 us
    unnamed x9, local copies, waits for them, and re-layouts  1.53 us
    dot_general x4, matrix products, backward(): jnp.einsum('bpij,bif->pjf', dense[:, quarter], row_panel, preferred_eleme...  1.1 us
  transfers between devices with their start and end apart: 21, of which 11 were waited for; matrix products, arithmetic and copies ran while one was open for 9% of the time, Pallas kernels for 2%

profile of v5, /device:TPU:0, one launch (start us, length us, event | category | flops | bytes accessed | tf_op | source)
XLA Modules:
  0.0 47.5 jit_solution(12785082099554349922)
XLA Ops:
  0.7 5.1 %collective-permute-start.2 = (bf16[128,256]{1,0:T(8,128)(2,1)}, bf16[128,256]{1,0:T(8,128)(2,1)S(1)}, u32[]{:S(2)}, u32[]{:S(2)}) collective-permute-start(bf16[128,256]{1,0:T(8,128)(2,1)} %param.5), channel_id=1, source_target_pairs={{0,24},{2,26},{4,28},{6,30},{8,16},{10,18},{12,20},{14,22},{16,8},... | collective-permute-start | bytes 196616 | tf_op jit(solution)/shard_map/ppermute | solution.py:12
  6.4 1.6 %collective-permute-start.6 = (bf16[128,256]{1,0:T(8,128)(2,1)}, bf16[128,256]{1,0:T(8,128)(2,1)S(1)}, u32[]{:S(2)}, u32[]{:S(2)}) collective-permute-start(bf16[128,256]{1,0:T(8,128)(2,1)} %param.5), channel_id=1, source_target_pairs={{0,4},{2,6},{4,0},{6,2},{8,12},{10,14},{12,8},{14,10},{16,20},{18,... | collective-permute-start | bytes 196616 | tf_op jit(solution)/shard_map/ppermute | solution.py:12
  8.0 1.5 %collective-permute-start.4 = (bf16[128,256]{1,0:T(8,128)(2,1)}, bf16[128,256]{1,0:T(8,128)(2,1)S(1)}, u32[]{:S(2)}, u32[]{:S(2)}) collective-permute-start(bf16[128,256]{1,0:T(8,128)(2,1)} %param.7), channel_id=1, source_target_pairs={{0,1},{1,0},{2,3},{3,2},{4,5},{5,4},{6,7},{7,6},{8,9},{9,8},{10,11... | collective-permute-start | bytes 196616 | tf_op jit(solution)/shard_map/ppermute | solution.py:12
  9.6 0.8 %constant_dynamic-update-slice_fusion.6 = bf16[512,256]{1,0:T(8,128)(2,1)S(1)} fusion(bf16[128,256]{1,0:T(8,128)(2,1)} %param.5), kind=kLoop, calls=%fused_computation.41 | loop fusion | bytes 131072
  10.4 1.2 %collective-permute-done.1 = bf16[128,256]{1,0:T(8,128)(2,1)S(1)} collective-permute-done((bf16[128,256]{1,0:T(8,128)(2,1)}, bf16[128,256]{1,0:T(8,128)(2,1)S(1)}, u32[]{:S(2)}, u32[]{:S(2)}) %collective-permute-start.1) | collective-permute-done | bytes 65568 | tf_op jit(solution)/shard_map/ppermute | solution.py:12
  11.6 1.6 %collective-permute-start.3 = (bf16[384,256]{1,0:T(8,128)(2,1)S(1)}, bf16[384,256]{1,0:T(8,128)(2,1)S(1)}, u32[]{:S(2)}, u32[]{:S(2)}) collective-permute-start(bf16[384,256]{1,0:T(8,128)(2,1)S(1)} %get-tuple-element.29.refs_0_), channel_id=1, source_target_pairs={{0,4},{2,6},{4,0},{6,2},{8,12},{10,14},{12,8},{14,10},{16,20},{18,... | collective-permute-start | bytes 589832 | tf_op jit(solution)/shard_map/ppermute | solution.py:12
  13.2 0.9 %broadcast_select_fusion.1 = (bf16[128,256]{1,0:T(8,128)(2,1)S(1)}, bf16[128,256]{1,0:T(8,128)(2,1)S(1)}) fusion(bf16[128,256]{1,0:T(8,128)(2,1)} %param.7, bf16[128,256]{1,0:T(8,128)(2,1)S(1)} %collective-permute-done.4, pred[]{:T(512)S(6)} %eq.4), kind=kLoop, calls=%fused_computation.34 | loop fusion | flops 65536 | bytes 262145 | tf_op jit(solution)/shard_map/jit(_where)/select_n | solution.py:136
  14.7 0.7 %copy-done.2 = s32[1,1,24]{2,1,0:T(1,128)S(1)} copy-done((s32[1,1,24]{2,1,0:T(1,128)S(1)}, s32[1,1,24]{2,1,0:T(1,128)}, u32[]{:S(2)}) %copy-start.2) | copy-done | bytes 120
  15.3 0.9 %shard_map.76 = bf16[32,128,128]{2,1,0:T(8,128)(2,1)S(1)} custom-call(s32[24]{0:T(128)S(1)} %bitcast.117, s32[1]{0:T(128)} %bitcast.1.row_ref, bf16[24,128,128]{2,1,0:T(8,128)(2,1)S(1)} %bitcast.116, bf16[384,256]{1,0:T(8,128)(2,1)S(1)} %get-tuple-element.29.refs_0_), custom_call_target="tpu_custom_call" | custom-call | flops 3000000000 | bytes 1000000 | tf_op jit(solution)/shard_map/pallas_call | solution.py:95
  16.7 1.4 %collective-permute-done.3 = bf16[384,256]{1,0:T(8,128)(2,1)S(1)} collective-permute-done((bf16[384,256]{1,0:T(8,128)(2,1)S(1)}, bf16[384,256]{1,0:T(8,128)(2,1)S(1)}, u32[]{:S(2)}, u32[]{:S(2)}) %collective-permute-start.3) | collective-permute-done | bytes 196640 | tf_op jit(solution)/shard_map/ppermute | solution.py:12
  18.4 1.2 %collective-permute-done.8 = bf16[384,256]{1,0:T(8,128)(2,1)S(1)} collective-permute-done((bf16[384,256]{1,0:T(8,128)(2,1)S(1)}, bf16[384,256]{1,0:T(8,128)(2,1)S(1)}, u32[]{:S(2)}, u32[]{:S(2)}) %collective-permute-start.8) | collective-permute-done | bytes 196640 | tf_op jit(solution)/shard_map/ppermute | solution.py:12
  19.9 1.8 %collective-permute-start.9 = (bf16[2,128,256]{2,1,0:T(8,128)(2,1)S(1)}, bf16[2,128,256]{2,1,0:T(8,128)(2,1)S(1)}, u32[]{:S(2)}, u32[]{:S(2)}) collective-permute-start(bf16[2,128,256]{2,1,0:T(8,128)(2,1)S(1)} %fusion.4), channel_id=1, source_target_pairs={{0,1},{1,0},{2,3},{3,2},{4,5},{5,4},{6,7},{7,6},{8,9},{9,8},{10,11... | collective-permute-start | bytes 393224 | tf_op jit(solution)/shard_map/ppermute | solution.py:12
  21.6 3.8 %collective-permute-done.9 = bf16[2,128,256]{2,1,0:T(8,128)(2,1)S(1)} collective-permute-done((bf16[2,128,256]{2,1,0:T(8,128)(2,1)S(1)}, bf16[2,128,256]{2,1,0:T(8,128)(2,1)S(1)}, u32[]{:S(2)}, u32[]{:S(2)}) %collective-permute-start.9) | collective-permute-done | bytes 131104 | tf_op jit(solution)/shard_map/ppermute | solution.py:12
  28.7 1.8 %collective-permute-start.12 = (bf16[4,128,256]{2,1,0:T(8,128)(2,1)S(1)}, bf16[4,128,256]{2,1,0:T(8,128)(2,1)S(1)}, u32[]{:S(2)}, u32[]{:S(2)}) collective-permute-start(bf16[4,128,256]{2,1,0:T(8,128)(2,1)S(1)} %add_convert_fusion.refs_2_), channel_id=1, source_target_pairs={{0,4},{2,6},{4,0},{6,2},{8,12},{10,14},{12,8},{14,10},{16,20},{18,... | collective-permute-start | bytes 786440 | tf_op jit(solution)/shard_map/ppermute | solution.py:12
  30.7 0.6 %multiply_convert_fusion.1 = bf16[128,256]{1,0:T(8,128)(2,1)} fusion(f32[256,256]{1,0:T(8,128)S(1)} %get-tuple-element.25, s32[]{:T(128)S(6)} %select_n.26, f32[256,256]{1,0:T(8,128)S(1)} %fusion.6), kind=kLoop, calls=%fused_computation.29 | loop fusion | flops 65536 | bytes 327684 | tf_op jit(solution)/shard_map/convert_element_type | solution.py:206
  31.3 3.5 %collective-permute-done.14.refs_1_ = bf16[128,256]{1,0:T(8,128)(2,1)S(1)} collective-permute-done((bf16[128,256]{1,0:T(8,128)(2,1)S(1)}, bf16[128,256]{1,0:T(8,128)(2,1)S(1)}, u32[]{:S(2)}, u32[]{:S(2)}) %collective-permute-start.14) | collective-permute-done | bytes 65568 | tf_op jit(solution)/shard_map/ppermute | solution.py:12
  34.8 0.7 %collective-permute-start.15 = (bf16[128,256]{1,0:T(8,128)(2,1)S(1)}, bf16[128,256]{1,0:T(8,128)(2,1)S(1)}, u32[]{:S(2)}, u32[]{:S(2)}) collective-permute-start(bf16[128,256]{1,0:T(8,128)(2,1)S(1)} %shard_map.78.refs_0_), channel_id=1, source_target_pairs={{0,16},{2,18},{4,20},{6,22},{8,24},{10,26},{12,28},{14,30},{16,0},... | collective-permute-start | bytes 196616 | tf_op jit(solution)/shard_map/ppermute | solution.py:12
  35.5 1.8 %collective-permute-done.12 = bf16[4,128,256]{2,1,0:T(8,128)(2,1)S(1)} collective-permute-done((bf16[4,128,256]{2,1,0:T(8,128)(2,1)S(1)}, bf16[4,128,256]{2,1,0:T(8,128)(2,1)S(1)}, u32[]{:S(2)}, u32[]{:S(2)}) %collective-permute-start.12) | collective-permute-done | bytes 262176 | tf_op jit(solution)/shard_map/ppermute | solution.py:12
  37.5 2.0 %collective-permute-start.18 = (bf16[128,256]{1,0:T(8,128)(2,1)S(1)}, bf16[128,256]{1,0:T(8,128)(2,1)S(1)}, u32[]{:S(2)}, u32[]{:S(2)}) collective-permute-start(bf16[128,256]{1,0:T(8,128)(2,1)S(1)} %get-tuple-element.20.refs_2_), channel_id=1, source_target_pairs={{0,24},{2,26},{4,28},{6,30},{8,16},{10,18},{12,20},{14,22},{16,8},... | collective-permute-start | bytes 196616 | tf_op jit(solution)/shard_map/ppermute | solution.py:12
  39.4 1.6 %collective-permute-done.15.refs_1_ = bf16[128,256]{1,0:T(8,128)(2,1)S(1)} collective-permute-done((bf16[128,256]{1,0:T(8,128)(2,1)S(1)}, bf16[128,256]{1,0:T(8,128)(2,1)S(1)}, u32[]{:S(2)}, u32[]{:S(2)}) %collective-permute-start.15) | collective-permute-done | bytes 65568 | tf_op jit(solution)/shard_map/ppermute | solution.py:12
  41.2 2.5 %collective-permute-start.17 = (bf16[128,256]{1,0:T(8,128)(2,1)S(1)}, bf16[128,256]{1,0:T(8,128)(2,1)S(1)}, u32[]{:S(2)}, u32[]{:S(2)}) collective-permute-start(bf16[128,256]{1,0:T(8,128)(2,1)S(1)} %shard_map.81), channel_id=1, source_target_pairs={{0,16},{2,18},{4,20},{6,22},{8,24},{10,26},{12,28},{14,30},{16,0},... | collective-permute-start | bytes 196616 | tf_op jit(solution)/shard_map/ppermute | solution.py:12
  43.8 1.6 %collective-permute-done.19.refs_1_ = bf16[128,256]{1,0:T(8,128)(2,1)S(1)} collective-permute-done((bf16[128,256]{1,0:T(8,128)(2,1)S(1)}, bf16[128,256]{1,0:T(8,128)(2,1)S(1)}, u32[]{:S(2)}, u32[]{:S(2)}) %collective-permute-start.19) | collective-permute-done | bytes 65568 | tf_op jit(solution)/shard_map/ppermute | solution.py:12
  45.5 1.2 %collective-permute-done.17.refs_2_ = bf16[128,256]{1,0:T(8,128)(2,1)S(1)} collective-permute-done((bf16[128,256]{1,0:T(8,128)(2,1)S(1)}, bf16[128,256]{1,0:T(8,128)(2,1)S(1)}, u32[]{:S(2)}, u32[]{:S(2)}) %collective-permute-start.17) | collective-permute-done | bytes 65568 | tf_op jit(solution)/shard_map/ppermute | solution.py:12
  46.8 0.7 %shard_map.84 = (bf16[128,256]{1,0:T(8,128)(2,1)}, f32[256,256]{1,0:T(8,128)}) custom-call(s32[1]{0:T(128)} %bitcast.25.core_ref, f32[128,256]{1,0:T(8,128)S(1)} %shard_map.82.refs_0_, f32[128,256]{1,0:T(8,128)S(1)} %shard_map.83.refs_1_, f32[128,256]{1,0:T(8,128)S(1)} %collective-permute-done.20.refs_2_), custom_call_target="tpu_custom_call" | custom-call | flops 1000000 | bytes 1000000 | tf_op jit(solution)/shard_map/pallas_call | solution.py:63
  (59 shorter events, 6.1 us)
Async XLA Ops:
  0.6 24.9 %copy-start = (bf16[256,256]{1,0:T(8,128)(2,1)S(1)}, bf16[256,256]{1,0:T(8,128)(2,1)}, u32[]{:S(2)}) copy-start(bf16[256,256]{1,0:T(8,128)(2,1)} %param.6) | copy-start | bytes 393220
  0.6 14.0 %copy-start.1 = (bf16[1,1,24,128,128]{4,3,2,1,0:T(8,128)(2,1)S(1)}, bf16[1,1,24,128,128]{4,3,2,1,0:T(8,128)(2,1)}, u32[]{:S(2)}) copy-start(bf16[1,1,24,128,128]{4,3,2,1,0:T(8,128)(2,1)} %param.8) | copy-start | bytes 2359300
  0.7 10.9 %collective-permute-start.2 = (bf16[128,256]{1,0:T(8,128)(2,1)}, bf16[128,256]{1,0:T(8,128)(2,1)S(1)}, u32[]{:S(2)}, u32[]{:S(2)}) collective-permute-start(bf16[128,256]{1,0:T(8,128)(2,1)} %param.5), channel_id=1, source_target_pairs={{0,24},{2,26},{4,28},{6,30},{8,16},{10,18},{12,20},{14,22},{16,8},... | collective-permute-start | bytes 196616 | tf_op jit(solution)/shard_map/ppermute | solution.py:12
  5.8 5.8 %collective-permute-start.1 = (bf16[128,256]{1,0:T(8,128)(2,1)}, bf16[128,256]{1,0:T(8,128)(2,1)S(1)}, u32[]{:S(2)}, u32[]{:S(2)}) collective-permute-start(bf16[128,256]{1,0:T(8,128)(2,1)} %param.5), channel_id=1, source_target_pairs={{0,16},{2,18},{4,20},{6,22},{8,24},{10,26},{12,28},{14,30},{16,0},... | collective-permute-start | bytes 196616 | tf_op jit(solution)/shard_map/ppermute | solution.py:12
  5.8 4.6 %collective-permute-start = (bf16[128,256]{1,0:T(8,128)(2,1)}, bf16[128,256]{1,0:T(8,128)(2,1)S(1)}, u32[]{:S(2)}, u32[]{:S(2)}) collective-permute-start(bf16[128,256]{1,0:T(8,128)(2,1)} %param.5), channel_id=1, source_target_pairs={{0,8},{2,10},{4,12},{6,14},{8,0},{10,2},{12,4},{14,6},{16,24},{18,... | collective-permute-start | bytes 196616 | tf_op jit(solution)/shard_map/ppermute | solution.py:12
  6.4 7.7 %collective-permute-start.6 = (bf16[128,256]{1,0:T(8,128)(2,1)}, bf16[128,256]{1,0:T(8,128)(2,1)S(1)}, u32[]{:S(2)}, u32[]{:S(2)}) collective-permute-start(bf16[128,256]{1,0:T(8,128)(2,1)} %param.5), channel_id=1, source_target_pairs={{0,4},{2,6},{4,0},{6,2},{8,12},{10,14},{12,8},{14,10},{16,20},{18,... | collective-permute-start | bytes 196616 | tf_op jit(solution)/shard_map/ppermute | solution.py:12
  8.0 5.1 %collective-permute-start.4 = (bf16[128,256]{1,0:T(8,128)(2,1)}, bf16[128,256]{1,0:T(8,128)(2,1)S(1)}, u32[]{:S(2)}, u32[]{:S(2)}) collective-permute-start(bf16[128,256]{1,0:T(8,128)(2,1)} %param.7), channel_id=1, source_target_pairs={{0,1},{1,0},{2,3},{3,2},{4,5},{5,4},{6,7},{7,6},{8,9},{9,8},{10,11... | collective-permute-start | bytes 196616 | tf_op jit(solution)/shard_map/ppermute | solution.py:12
  11.6 6.5 %collective-permute-start.3 = (bf16[384,256]{1,0:T(8,128)(2,1)S(1)}, bf16[384,256]{1,0:T(8,128)(2,1)S(1)}, u32[]{:S(2)}, u32[]{:S(2)}) collective-permute-start(bf16[384,256]{1,0:T(8,128)(2,1)S(1)} %get-tuple-element.29.refs_0_), channel_id=1, source_target_pairs={{0,4},{2,6},{4,0},{6,2},{8,12},{10,14},{12,8},{14,10},{16,20},{18,... | collective-permute-start | bytes 589832 | tf_op jit(solution)/shard_map/ppermute | solution.py:12
  13.2 3.1 %collective-permute-start.5 = (bf16[512,256]{1,0:T(8,128)(2,1)S(1)}, bf16[512,256]{1,0:T(8,128)(2,1)S(1)}, u32[]{:S(2)}, u32[]{:S(2)}) collective-permute-start(bf16[512,256]{1,0:T(8,128)(2,1)S(1)} %get-tuple-element.28), channel_id=1, source_target_pairs={{0,2},{2,0},{4,6},{6,4},{8,10},{10,8},{12,14},{14,12},{16,18},{18,... | collective-permute-start | bytes 786440 | tf_op jit(solution)/shard_map/ppermute | solution.py:12
  14.1 4.4 %collective-permute-start.7 = (bf16[128,256]{1,0:T(8,128)(2,1)S(1)}, bf16[128,256]{1,0:T(8,128)(2,1)S(1)}, u32[]{:S(2)}, u32[]{:S(2)}) collective-permute-start(bf16[128,256]{1,0:T(8,128)(2,1)S(1)} %collective-permute-done.6), channel_id=1, source_target_pairs={{0,2},{2,0},{4,6},{6,4},{8,10},{10,8},{12,14},{14,12},{16,18},{18,... | collective-permute-start | bytes 196616 | tf_op jit(solution)/shard_map/ppermute | solution.py:12
  14.6 0.7 %copy-start.2 = (s32[1,1,24]{2,1,0:T(1,128)S(1)}, s32[1,1,24]{2,1,0:T(1,128)}, u32[]{:S(2)}) copy-start(s32[1,1,24]{2,1,0:T(1,128)} %param.9) | copy-start | bytes 292
  18.2 1.4 %collective-permute-start.8 = (bf16[384,256]{1,0:T(8,128)(2,1)S(1)}, bf16[384,256]{1,0:T(8,128)(2,1)S(1)}, u32[]{:S(2)}, u32[]{:S(2)}) collective-permute-start(bf16[384,256]{1,0:T(8,128)(2,1)S(1)} %collective-permute-done.3), channel_id=1, source_target_pairs={{0,2},{2,0},{4,6},{6,4},{8,10},{10,8},{12,14},{14,12},{16,18},{18,... | collective-permute-start | bytes 589832 | tf_op jit(solution)/shard_map/ppermute | solution.py:12
  19.9 5.6 %collective-permute-start.9 = (bf16[2,128,256]{2,1,0:T(8,128)(2,1)S(1)}, bf16[2,128,256]{2,1,0:T(8,128)(2,1)S(1)}, u32[]{:S(2)}, u32[]{:S(2)}) collective-permute-start(bf16[2,128,256]{2,1,0:T(8,128)(2,1)S(1)} %fusion.4), channel_id=1, source_target_pairs={{0,1},{1,0},{2,3},{3,2},{4,5},{5,4},{6,7},{7,6},{8,9},{9,8},{10,11... | collective-permute-start | bytes 393224 | tf_op jit(solution)/shard_map/ppermute | solution.py:12
  26.3 4.1 %collective-permute-start.13 = (f32[128,256]{1,0:T(8,128)S(1)}, f32[128,256]{1,0:T(8,128)S(1)}, u32[]{:S(2)}, u32[]{:S(2)}) collective-permute-start(f32[128,256]{1,0:T(8,128)S(1)} %get-tuple-element.22), channel_id=1, source_target_pairs={{0,2},{2,0},{4,6},{6,4},{8,10},{10,8},{12,14},{14,12},{16,18},{18,... | collective-permute-start | bytes 393224 | tf_op jit(solution)/shard_map/ppermute | solution.py:12
  26.7 1.7 %collective-permute-start.11 = (bf16[4,128,256]{2,1,0:T(8,128)(2,1)S(1)}, bf16[4,128,256]{2,1,0:T(8,128)(2,1)S(1)}, u32[]{:S(2)}, u32[]{:S(2)}) collective-permute-start(bf16[4,128,256]{2,1,0:T(8,128)(2,1)S(1)} %fusion.1), channel_id=1, source_target_pairs={{0,2},{2,0},{4,6},{6,4},{8,10},{10,8},{12,14},{14,12},{16,18},{18,... | collective-permute-start | bytes 786440 | tf_op jit(solution)/shard_map/ppermute | solution.py:12
  27.5 8.0 %collective-permute-start.10 = (bf16[4,128,256]{2,1,0:T(8,128)(2,1)S(1)}, bf16[4,128,256]{2,1,0:T(8,128)(2,1)S(1)}, u32[]{:S(2)}, u32[]{:S(2)}) collective-permute-start(bf16[4,128,256]{2,1,0:T(8,128)(2,1)S(1)} %fusion), channel_id=1, source_target_pairs={{0,2},{2,0},{4,6},{6,4},{8,10},{10,8},{12,14},{14,12},{16,18},{18,... | collective-permute-start | bytes 786440 | tf_op jit(solution)/shard_map/ppermute | solution.py:12
  28.7 8.7 %collective-permute-start.12 = (bf16[4,128,256]{2,1,0:T(8,128)(2,1)S(1)}, bf16[4,128,256]{2,1,0:T(8,128)(2,1)S(1)}, u32[]{:S(2)}, u32[]{:S(2)}) collective-permute-start(bf16[4,128,256]{2,1,0:T(8,128)(2,1)S(1)} %add_convert_fusion.refs_2_), channel_id=1, source_target_pairs={{0,4},{2,6},{4,0},{6,2},{8,12},{10,14},{12,8},{14,10},{16,20},{18,... | collective-permute-start | bytes 786440 | tf_op jit(solution)/shard_map/ppermute | solution.py:12
  30.5 4.3 %collective-permute-start.14 = (bf16[128,256]{1,0:T(8,128)(2,1)S(1)}, bf16[128,256]{1,0:T(8,128)(2,1)S(1)}, u32[]{:S(2)}, u32[]{:S(2)}) collective-permute-start(bf16[128,256]{1,0:T(8,128)(2,1)S(1)} %shard_map.77.refs_0_), channel_id=1, source_target_pairs={{0,8},{2,10},{4,12},{6,14},{8,0},{10,2},{12,4},{14,6},{16,24},{18,... | collective-permute-start | bytes 196616 | tf_op jit(solution)/shard_map/ppermute | solution.py:12
  34.8 6.2 %collective-permute-start.15 = (bf16[128,256]{1,0:T(8,128)(2,1)S(1)}, bf16[128,256]{1,0:T(8,128)(2,1)S(1)}, u32[]{:S(2)}, u32[]{:S(2)}) collective-permute-start(bf16[128,256]{1,0:T(8,128)(2,1)S(1)} %shard_map.78.refs_0_), channel_id=1, source_target_pairs={{0,16},{2,18},{4,20},{6,22},{8,24},{10,26},{12,28},{14,30},{16,0},... | collective-permute-start | bytes 196616 | tf_op jit(solution)/shard_map/ppermute | solution.py:12
  37.5 9.2 %collective-permute-start.18 = (bf16[128,256]{1,0:T(8,128)(2,1)S(1)}, bf16[128,256]{1,0:T(8,128)(2,1)S(1)}, u32[]{:S(2)}, u32[]{:S(2)}) collective-permute-start(bf16[128,256]{1,0:T(8,128)(2,1)S(1)} %get-tuple-element.20.refs_2_), channel_id=1, source_target_pairs={{0,24},{2,26},{4,28},{6,30},{8,16},{10,18},{12,20},{14,22},{16,8},... | collective-permute-start | bytes 196616 | tf_op jit(solution)/shard_map/ppermute | solution.py:12
  41.0 4.3 %collective-permute-start.19 = (bf16[128,256]{1,0:T(8,128)(2,1)S(1)}, bf16[128,256]{1,0:T(8,128)(2,1)S(1)}, u32[]{:S(2)}, u32[]{:S(2)}) collective-permute-start(bf16[128,256]{1,0:T(8,128)(2,1)S(1)} %shard_map.79.refs_1_.refs_0_), channel_id=1, source_target_pairs={{0,4},{2,6},{4,0},{6,2},{8,12},{10,14},{12,8},{14,10},{16,20},{18,... | collective-permute-start | bytes 196616 | tf_op jit(solution)/shard_map/ppermute | solution.py:12
  41.1 4.4 %collective-permute-start.16 = (bf16[128,256]{1,0:T(8,128)(2,1)S(1)}, bf16[128,256]{1,0:T(8,128)(2,1)S(1)}, u32[]{:S(2)}, u32[]{:S(2)}) collective-permute-start(bf16[128,256]{1,0:T(8,128)(2,1)S(1)} %shard_map.80), channel_id=1, source_target_pairs={{0,8},{2,10},{4,12},{6,14},{8,0},{10,2},{12,4},{14,6},{16,24},{18,... | collective-permute-start | bytes 196616 | tf_op jit(solution)/shard_map/ppermute | solution.py:12
  41.2 5.4 %collective-permute-start.17 = (bf16[128,256]{1,0:T(8,128)(2,1)S(1)}, bf16[128,256]{1,0:T(8,128)(2,1)S(1)}, u32[]{:S(2)}, u32[]{:S(2)}) collective-permute-start(bf16[128,256]{1,0:T(8,128)(2,1)S(1)} %shard_map.81), channel_id=1, source_target_pairs={{0,16},{2,18},{4,20},{6,22},{8,24},{10,26},{12,28},{14,30},{16,0},... | collective-permute-start | bytes 196616 | tf_op jit(solution)/shard_map/ppermute | solution.py:12
  45.4 1.4 %collective-permute-start.20 = (f32[128,256]{1,0:T(8,128)S(1)}, f32[128,256]{1,0:T(8,128)S(1)}, u32[]{:S(2)}, u32[]{:S(2)}) collective-permute-start(f32[128,256]{1,0:T(8,128)S(1)} %shard_map.83.refs_1_), channel_id=1, source_target_pairs={{0,2},{2,0},{4,6},{6,4},{8,10},{10,8},{12,14},{14,12},{16,18},{18,... | collective-permute-start | bytes 393224 | tf_op jit(solution)/shard_map/ppermute | solution.py:12

commit v6 on v5

--- a/solution.py
+++ b/solution.py
@@ -20,10 +20,10 @@
     count = len(terms)
 
     def body(*refs):
-        value = refs[0][...].astype(jnp.float32)
-        for ref in refs[1:count]:
-            value = value + ref[...].astype(jnp.float32)
-        refs[-1][...] = value.astype(dtype)
+        values = [ref[...].astype(jnp.float32) for ref in refs[:count]]
+        while len(values) > 1:
+            values = [a + b for a, b in zip(values[::2], values[1::2])]
+        refs[-1][...] = values[0].astype(dtype)
 
     shape = jax.ShapeDtypeStruct(terms[0].shape, dtype)
     in_specs = [pl.BlockSpec(memory_space=pltpu.VMEM)] * count
@@ -78,25 +78,33 @@
     depth = row_count // 4
 
     def body(slots_ref, row_ref, tiles_ref, *refs):
-        out_ref = refs[-1]
-        out_ref[...] = jnp.zeros_like(out_ref)
+        own_ref, other_ref = refs[-2:]
+        own_ref[...] = jnp.zeros_like(own_ref)
+        other_ref[...] = jnp.zeros_like(other_ref)
 
         @pl.loop(0, blocks)
         def _(k):
             slot = slots_ref[k]
             relative = (slot & (row_count - 1)) ^ row_ref[0]
-            place = (relative & 1) * (row_count // 2) + (relative >> 1 & 1) * depth
-            place = place + (relative >> 2) + (slot - (slot & (row_count - 1)))
-            out_ref[place] = tiles_ref[k]
-
-    shape = jax.ShapeDtypeStruct((col_count * row_count, side, side), tiles.dtype)
+            place = (relative >> 1 & 1) * depth + (relative >> 2)
+            place = place + (slot - (slot & (row_count - 1))) // 2
+
+            @pl.when(relative & 1 == 0)
+            def _():
+                own_ref[place] = tiles_ref[k]
+
+            @pl.when(relative & 1 == 1)
+            def _():
+                other_ref[place] = tiles_ref[k]
+
+    shape = jax.ShapeDtypeStruct((col_count * row_count // 2, side, side), tiles.dtype)
     smem = pl.BlockSpec(memory_space=pltpu.SMEM)
     vmem = pl.BlockSpec(memory_space=pltpu.VMEM)
     return pl.pallas_call(
         body,
-        out_shape=shape,
+        out_shape=(shape, shape),
         in_specs=[smem, smem, vmem] + [pl.BlockSpec(memory_space=pl.ANY)] * len(later_than),
-        out_specs=vmem,
+        out_specs=(vmem, vmem),
         compiler_params=pltpu.CompilerParams(vmem_limit_bytes=(2 * (blocks + row_count * col_count) * side * side * 2) + (1 << 20)),
         cost_estimate=pl.CostEstimate(flops=flops, bytes_accessed=10**6, transcendentals=0),
     )(slots, row.reshape(1), tiles, *later_than)
@@ -121,7 +129,7 @@
     bf16 = jnp.bfloat16
 
     def direct(bit, low, high):
-        return [swap(features, "row", 4 * k + bit) if k or bit else features for k in range(low, high)]
+        return [swap(features, "row", 4 * k + bit) if k or bit else features for k in reversed(range(low, high))][::-1]
 
     straight = 1
     far = jnp.concatenate(direct(0, straight, depth))
@@ -136,62 +144,66 @@
         low = jnp.where(col & bit == 0, cotangent, got)
         high = jnp.where(col & bit == 0, got, cotangent)
         cotangent = jnp.concatenate([low, high])
-    dense = dense_tile(tile_blocks, tile_slots, row, col, row_count, col_count, 3000000000, [far])
-    dense = dense.reshape(col_count, 4, depth, side, side)
+    own_tile, other_tile = dense_tile(tile_blocks, tile_slots, row, col, row_count, col_count, 3000000000, [far])
+    own_tile = own_tile.reshape(col_count, 2, depth, side, side)
+    other_tile = other_tile.reshape(col_count, 2, depth, side, side)
 
     def forward(quarter, block):
         return jnp.einsum(
             "bpij,pjf->bif",
-            dense[:, quarter],
+            (own_tile if quarter < 2 else other_tile)[:, quarter % 2],
             block.reshape(depth, side, width),
             preferred_element_type=f32,
         )
 
-    def backward(quarter, row_panel):
-        return jnp.einsum(
-            "bpij,bif->pjf", dense[:, quarter], row_panel, preferred_element_type=f32
-        )
-
     panel_c = swap(panel, "row", 1)
-    near_xc = swap(near_x, "row", 1)
     partial = forward(0, panel) + forward(2, panel_c)
     far_x, cotangent, partial = lax.optimization_barrier((far_x, cotangent, partial))
-    far_xc = swap(far_x, "row", 1)
-    partial = partial + forward(1, jnp.concatenate([near_x, far_x]))
-    partial = partial + forward(3, jnp.concatenate([near_xc, far_xc]))
+    panel_x = jnp.concatenate([near_x, far_x])
+    partial = partial + forward(1, panel_x) + forward(3, swap(panel_x, "row", 1))
     for bit in bits(col_count):
-        sent = rounded(partial)
-        partial = sent.astype(f32) + swap(sent, "col", bit).astype(f32)
+        sent, other_tile = lax.optimization_barrier((partial.astype(bf16), other_tile))
+        got = swap(sent, "col", bit)
+        partial = sent.astype(f32) + got.astype(f32)
+    partner = swap(other_tile, "row", 1)
     aggregated = partial.astype(bf16).reshape(-1, width)
     pre = jnp.dot(aggregated, weight, preferred_element_type=f32)
     sigmoid_pre = jax.nn.sigmoid(pre)
     grad_pre = (
         cotangent.astype(f32) * sigmoid_pre * (1.0 + pre * (1.0 - sigmoid_pre))
     ).astype(bf16)
-    term = jnp.dot(aggregated.T, grad_pre, preferred_element_type=f32)
-    grad_pre, term = lax.optimization_barrier((grad_pre, term))
-    grad_agg = jnp.dot(grad_pre, weight.T, preferred_element_type=f32).astype(bf16)
-    row_panel = grad_agg.reshape(col_count, side, width)
-
-    sent_xc = backward(3, row_panel).astype(bf16)
-    got_xc = swap(sent_xc, "row", 1)
-    got_c = swap(backward(2, row_panel).astype(bf16), "row", 1)
-
-    sent_x = (backward(1, row_panel) + got_xc.astype(f32)).astype(bf16)
+    partner_grad_pre = swap(grad_pre, "row", 1)
+    partner_aggregated = swap(aggregated, "row", 1)
+
+    def panel_of(rows):
+        grad_agg = jnp.dot(rows, weight.T, preferred_element_type=f32).astype(bf16)
+        return grad_agg.reshape(col_count, side, width)
+
+    row_panel = panel_of(grad_pre)
+    partner_panel = panel_of(partner_grad_pre)
+
+    def backward(quarter):
+        spec = "bpij,bif->pjf"
+        own = jnp.einsum(spec, own_tile[:, quarter], row_panel, preferred_element_type=f32)
+        return own + jnp.einsum(spec, partner[:, quarter], partner_panel, preferred_element_type=f32)
+
+    sent_x = backward(1).astype(bf16)
+    sent_x, pre = lax.optimization_barrier((sent_x, pre))
     got_x = swap(sent_x, "row", 2)
-    mine = backward(0, row_panel) + got_c.astype(f32)
-
-    pair = term.reshape(2, term.shape[0] // 2, -1)
-    kept = lax.dynamic_index_in_dim(pair, core, 0, False)
-    got = swap(lax.dynamic_index_in_dim(pair, 1 - core, 0, False), "row", 1)
-    half = total([kept, got], bf16, 3000000000, [sent_x])
+    mine = backward(0)
+
+    columns = [
+        lax.dynamic_slice_in_dim(rows, core * (width // 2), width // 2, 1)
+        for rows in (aggregated, partner_aggregated)
+    ]
+    half = jnp.dot(columns[0].T, grad_pre, preferred_element_type=f32)
+    half = half + jnp.dot(columns[1].T, partner_grad_pre, preferred_element_type=f32)
+    half = total([half], bf16, 3000000000, [sent_x])
 
     mine = mine + got_x.astype(f32)
     sent_z = [mine[k].astype(bf16) for k in range(1, depth)]
-    for bit in bits(depth):
-        last = [sent_z[-1]] if 2 * bit == depth else []
-        half = total([half, swap(half, "row", 4 * bit)], bf16, 3000000000 if last else 100000000, last)
-    for k in (1,2,):
+    half = total([half] + [swap(half, "row", 4 * k) for k in range(1, depth)], bf16, 3 * 10**9, [sent_z[-1]])
+    for k in (1,):
         sent_z[k - 1] = total([sent_z[k - 1]], bf16, 100000000, [half])
     got_z = [swap(sent_z[k - 1], "row", 4 * k) for k in range(1, depth)]
     half = total([half, swap(half, "row", 2)], f32, 10**8)

time: 47.8 us -> 47.5 us (level)
  waiting for transfers between devices: 17.9 us -> 12.3 us
  starting transfers between devices: 20.9 us -> 25.5 us
    ppermute x21, waiting for transfers between devices: 17.9 us -> 12.3 us  [swap(): lax.ppermute(x, axis, [(i, i ^ bit) for i in range(lax.axis_size(axis))])]
    ppermute x21, starting transfers between devices: 20.9 us -> 25.5 us  [swap(): lax.ppermute(x, axis, [(i, i ^ bit) for i in range(lax.axis_size(axis))])]
    dot_general x10 -> x12, matrix products: 2.45 us -> 2.76 us  [the longest x4 0.91 us: forward(): jnp.einsum('bpij,pjf->bif', (own_tile if quarter < 2 else other_tile)[:,...]
    unnamed x9 -> x10, local copies, waits for them, and re-layouts: 1.53 us -> 1.52 us
  transfers between devices with their start and end apart: 21 -> 21, of which waited for: 11 -> 9; matrix products, arithmetic and copies ran while one was open for 9% -> 11% of each run, Pallas kernels for 2% -> 3%
where the time goes in v6:
time: 47.5 us; the launch traced here: 47.3 us
  starting transfers between devices  25.5 us (54%)
  waiting for transfers between devices  12.3 us (26%)
  matrix products  2.95 us (6%)
  Pallas kernels  2.15 us (5%)
  local copies, waits for them, and re-layouts  1.85 us (4%)
  other arithmetic  1.66 us (3%)
  between operations  0.94 us (2%)
    ppermute x21, starting transfers between devices, swap(): lax.ppermute(x, axis, [(i, i ^ bit) for i in range(lax.axis_size(axis))])  25.5 us
    ppermute x21, waiting for transfers between devices, swap(): lax.ppermute(x, axis, [(i, i ^ bit) for i in range(lax.axis_size(axis))])  12.3 us
    unnamed x10, local copies, waits for them, and re-layouts  1.52 us
    pallas_call x1, Pallas kernels, dense_tile(): pl.pallas_call(body, out_shape=(shape, shape), in_specs=[smem, smem, vmem...  1.3 us
  transfers between devices with their start and end apart: 21, of which 9 were waited for; matrix products, arithmetic and copies ran while one was open for 11% of the time, Pallas kernels for 3%

profile of v6, /device:TPU:0, one launch (start us, length us, event | category | flops | bytes accessed | tf_op | source)
XLA Modules:
  0.0 47.3 jit_solution(8861450738464805254)
XLA Ops:
  0.7 5.1 %collective-permute-start.2 = (bf16[128,256]{1,0:T(8,128)(2,1)}, bf16[128,256]{1,0:T(8,128)(2,1)S(1)}, u32[]{:S(2)}, u32[]{:S(2)}) collective-permute-start(bf16[128,256]{1,0:T(8,128)(2,1)} %param.5), channel_id=1, source_target_pairs={{0,24},{2,26},{4,28},{6,30},{8,16},{10,18},{12,20},{14,22},{16,8},... | collective-permute-start | bytes 196616 | tf_op jit(solution)/shard_map/ppermute | solution.py:12
  5.8 0.6 %collective-permute-start = (bf16[128,256]{1,0:T(8,128)(2,1)}, bf16[128,256]{1,0:T(8,128)(2,1)S(1)}, u32[]{:S(2)}, u32[]{:S(2)}) collective-permute-start(bf16[128,256]{1,0:T(8,128)(2,1)} %param.5), channel_id=1, source_target_pairs={{0,8},{2,10},{4,12},{6,14},{8,0},{10,2},{12,4},{14,6},{16,24},{18,... | collective-permute-start | bytes 196616 | tf_op jit(solution)/shard_map/ppermute | solution.py:12
  6.4 1.6 %collective-permute-start.6 = (bf16[128,256]{1,0:T(8,128)(2,1)}, bf16[128,256]{1,0:T(8,128)(2,1)S(1)}, u32[]{:S(2)}, u32[]{:S(2)}) collective-permute-start(bf16[128,256]{1,0:T(8,128)(2,1)} %param.5), channel_id=1, source_target_pairs={{0,4},{2,6},{4,0},{6,2},{8,12},{10,14},{12,8},{14,10},{16,20},{18,... | collective-permute-start | bytes 196616 | tf_op jit(solution)/shard_map/ppermute | solution.py:12
  8.0 1.5 %collective-permute-start.4 = (bf16[128,256]{1,0:T(8,128)(2,1)}, bf16[128,256]{1,0:T(8,128)(2,1)S(1)}, u32[]{:S(2)}, u32[]{:S(2)}) collective-permute-start(bf16[128,256]{1,0:T(8,128)(2,1)} %param.7), channel_id=1, source_target_pairs={{0,1},{1,0},{2,3},{3,2},{4,5},{5,4},{6,7},{7,6},{8,9},{9,8},{10,11... | collective-permute-start | bytes 196616 | tf_op jit(solution)/shard_map/ppermute | solution.py:12
  9.6 0.8 %constant_dynamic-update-slice_fusion.6 = bf16[512,256]{1,0:T(8,128)(2,1)S(1)} fusion(bf16[128,256]{1,0:T(8,128)(2,1)} %param.5), kind=kLoop, calls=%fused_computation.43 | loop fusion | bytes 131072
  10.4 1.2 %collective-permute-done.1 = bf16[128,256]{1,0:T(8,128)(2,1)S(1)} collective-permute-done((bf16[128,256]{1,0:T(8,128)(2,1)}, bf16[128,256]{1,0:T(8,128)(2,1)S(1)}, u32[]{:S(2)}, u32[]{:S(2)}) %collective-permute-start.1) | collective-permute-done | bytes 65568 | tf_op jit(solution)/shard_map/ppermute | solution.py:12
  11.6 1.6 %collective-permute-start.3 = (bf16[384,256]{1,0:T(8,128)(2,1)S(1)}, bf16[384,256]{1,0:T(8,128)(2,1)S(1)}, u32[]{:S(2)}, u32[]{:S(2)}) collective-permute-start(bf16[384,256]{1,0:T(8,128)(2,1)S(1)} %get-tuple-element.33.refs_0_), channel_id=1, source_target_pairs={{0,4},{2,6},{4,0},{6,2},{8,12},{10,14},{12,8},{14,10},{16,20},{18,... | collective-permute-start | bytes 589832 | tf_op jit(solution)/shard_map/ppermute | solution.py:12
  13.2 0.9 %broadcast_select_fusion.1 = (bf16[128,256]{1,0:T(8,128)(2,1)S(1)}, bf16[128,256]{1,0:T(8,128)(2,1)S(1)}) fusion(bf16[128,256]{1,0:T(8,128)(2,1)} %param.7, bf16[128,256]{1,0:T(8,128)(2,1)S(1)} %collective-permute-done.4, pred[]{:T(512)S(6)} %eq.4), kind=kLoop, calls=%fused_computation.36 | loop fusion | flops 65536 | bytes 262145 | tf_op jit(solution)/shard_map/jit(_where)/select_n | solution.py:144
  14.7 1.3 %shard_map.76 = (bf16[16,128,128]{2,1,0:T(8,128)(2,1)S(1)}, bf16[16,128,128]{2,1,0:T(8,128)(2,1)S(1)}) custom-call(s32[24]{0:T(128)S(1)} %bitcast.123, s32[1]{0:T(128)} %bitcast.1.row_ref, bf16[24,128,128]{2,1,0:T(8,128)(2,1)S(1)} %bitcast.122, bf16[384,256]{1,0:T(8,128)(2,1)S(1)} %get-tuple-element.33.refs_0_), custom_call_target="tpu_custom_call" | custom-call | flops 3000000000 | bytes 1000000 | tf_op jit(solution)/shard_map/pallas_call | solution.py:103
  16.5 1.6 %collective-permute-done.3 = bf16[384,256]{1,0:T(8,128)(2,1)S(1)} collective-permute-done((bf16[384,256]{1,0:T(8,128)(2,1)S(1)}, bf16[384,256]{1,0:T(8,128)(2,1)S(1)}, u32[]{:S(2)}, u32[]{:S(2)}) %collective-permute-start.3) | collective-permute-done | bytes 196640 | tf_op jit(solution)/shard_map/ppermute | solution.py:12
  18.5 1.3 %collective-permute-done.7 = bf16[512,256]{1,0:T(8,128)(2,1)S(1)} collective-permute-done((bf16[512,256]{1,0:T(8,128)(2,1)S(1)}, bf16[512,256]{1,0:T(8,128)(2,1)S(1)}, u32[]{:S(2)}, u32[]{:S(2)}) %collective-permute-start.7) | collective-permute-done | bytes 262176 | tf_op jit(solution)/shard_map/ppermute | solution.py:12
  20.0 1.8 %collective-permute-start.8 = (bf16[2,128,256]{2,1,0:T(8,128)(2,1)S(1)}, bf16[2,128,256]{2,1,0:T(8,128)(2,1)S(1)}, u32[]{:S(2)}, u32[]{:S(2)}) collective-permute-start(bf16[2,128,256]{2,1,0:T(8,128)(2,1)S(1)} %add_convert_fusion.1), channel_id=1, source_target_pairs={{0,1},{1,0},{2,3},{3,2},{4,5},{5,4},{6,7},{7,6},{8,9},{9,8},{10,11... | collective-permute-start | bytes 393224 | tf_op jit(solution)/shard_map/ppermute | solution.py:12
  22.1 3.5 %collective-permute-done.8 = bf16[2,128,256]{2,1,0:T(8,128)(2,1)S(1)} collective-permute-done((bf16[2,128,256]{2,1,0:T(8,128)(2,1)S(1)}, bf16[2,128,256]{2,1,0:T(8,128)(2,1)S(1)}, u32[]{:S(2)}, u32[]{:S(2)}) %collective-permute-start.8) | collective-permute-done | bytes 131104 | tf_op jit(solution)/shard_map/ppermute | solution.py:12
  28.5 1.7 %collective-permute-start.11 = (bf16[4,128,256]{2,1,0:T(8,128)(2,1)S(1)}, bf16[4,128,256]{2,1,0:T(8,128)(2,1)S(1)}, u32[]{:S(2)}, u32[]{:S(2)}) collective-permute-start(bf16[4,128,256]{2,1,0:T(8,128)(2,1)S(1)} %fusion.3.refs_1_), channel_id=1, source_target_pairs={{0,4},{2,6},{4,0},{6,2},{8,12},{10,14},{12,8},{14,10},{16,20},{18,... | collective-permute-start | bytes 786440 | tf_op jit(solution)/shard_map/ppermute | solution.py:12
  30.3 1.8 %collective-permute-start.15 = (bf16[128,256]{1,0:T(8,128)(2,1)S(1)}, bf16[128,256]{1,0:T(8,128)(2,1)S(1)}, u32[]{:S(2)}, u32[]{:S(2)}) collective-permute-start(bf16[128,256]{1,0:T(8,128)(2,1)S(1)} %shard_map.77.refs_0_), channel_id=1, source_target_pairs={{0,24},{2,26},{4,28},{6,30},{8,16},{10,18},{12,20},{14,22},{16,8},... | collective-permute-start | bytes 196616 | tf_op jit(solution)/shard_map/ppermute | solution.py:12
  32.1 2.6 %collective-permute-start.13 = (bf16[128,256]{1,0:T(8,128)(2,1)S(1)}, bf16[128,256]{1,0:T(8,128)(2,1)S(1)}, u32[]{:S(2)}, u32[]{:S(2)}) collective-permute-start(bf16[128,256]{1,0:T(8,128)(2,1)S(1)} %shard_map.77.refs_0_), channel_id=1, source_target_pairs={{0,8},{2,10},{4,12},{6,14},{8,0},{10,2},{12,4},{14,6},{16,24},{18,... | collective-permute-start | bytes 196616 | tf_op jit(solution)/shard_map/ppermute | solution.py:12
  34.7 0.6 %multiply_convert_fusion.1 = bf16[128,256]{1,0:T(8,128)(2,1)} fusion(f32[256,256]{1,0:T(8,128)S(1)} %get-tuple-element.29, s32[]{:T(128)S(6)} %select_n.23, f32[256,256]{1,0:T(8,128)S(1)} %fusion.11), kind=kLoop, calls=%fused_computation.28 | loop fusion | flops 65536 | bytes 327684 | tf_op jit(solution)/shard_map/convert_element_type | solution.py:218
  35.4 1.8 %collective-permute-done.11 = bf16[4,128,256]{2,1,0:T(8,128)(2,1)S(1)} collective-permute-done((bf16[4,128,256]{2,1,0:T(8,128)(2,1)S(1)}, bf16[4,128,256]{2,1,0:T(8,128)(2,1)S(1)}, u32[]{:S(2)}, u32[]{:S(2)}) %collective-permute-start.11) | collective-permute-done | bytes 262176 | tf_op jit(solution)/shard_map/ppermute | solution.py:12
  37.4 2.0 %collective-permute-start.18 = (bf16[128,256]{1,0:T(8,128)(2,1)S(1)}, bf16[128,256]{1,0:T(8,128)(2,1)S(1)}, u32[]{:S(2)}, u32[]{:S(2)}) collective-permute-start(bf16[128,256]{1,0:T(8,128)(2,1)S(1)} %get-tuple-element.26.refs_4_), channel_id=1, source_target_pairs={{0,24},{2,26},{4,28},{6,30},{8,16},{10,18},{12,20},{14,22},{16,8},... | collective-permute-start | bytes 196616 | tf_op jit(solution)/shard_map/ppermute | solution.py:12
  39.5 1.6 %collective-permute-start.19 = (bf16[128,256]{1,0:T(8,128)(2,1)S(1)}, bf16[128,256]{1,0:T(8,128)(2,1)S(1)}, u32[]{:S(2)}, u32[]{:S(2)}) collective-permute-start(bf16[128,256]{1,0:T(8,128)(2,1)S(1)} %shard_map.78.refs_1_.refs_0_), channel_id=1, source_target_pairs={{0,4},{2,6},{4,0},{6,2},{8,12},{10,14},{12,8},{14,10},{16,20},{18,... | collective-permute-start | bytes 196616 | tf_op jit(solution)/shard_map/ppermute | solution.py:12
  41.0 2.6 %collective-permute-start.17 = (bf16[128,256]{1,0:T(8,128)(2,1)S(1)}, bf16[128,256]{1,0:T(8,128)(2,1)S(1)}, u32[]{:S(2)}, u32[]{:S(2)}) collective-permute-start(bf16[128,256]{1,0:T(8,128)(2,1)S(1)} %get-tuple-element.25), channel_id=1, source_target_pairs={{0,16},{2,18},{4,20},{6,22},{8,24},{10,26},{12,28},{14,30},{16,0},... | collective-permute-start | bytes 196616 | tf_op jit(solution)/shard_map/ppermute | solution.py:12
  43.9 1.5 %collective-permute-done.16.refs_1_ = bf16[128,256]{1,0:T(8,128)(2,1)S(1)} collective-permute-done((bf16[128,256]{1,0:T(8,128)(2,1)S(1)}, bf16[128,256]{1,0:T(8,128)(2,1)S(1)}, u32[]{:S(2)}, u32[]{:S(2)}) %collective-permute-start.16) | collective-permute-done | bytes 65568 | tf_op jit(solution)/shard_map/ppermute | solution.py:12
  45.4 1.1 %collective-permute-done.17.refs_2_ = bf16[128,256]{1,0:T(8,128)(2,1)S(1)} collective-permute-done((bf16[128,256]{1,0:T(8,128)(2,1)S(1)}, bf16[128,256]{1,0:T(8,128)(2,1)S(1)}, u32[]{:S(2)}, u32[]{:S(2)}) %collective-permute-start.17) | collective-permute-done | bytes 65568 | tf_op jit(solution)/shard_map/ppermute | solution.py:12
  46.6 0.8 %shard_map.82 = (bf16[128,256]{1,0:T(8,128)(2,1)}, f32[256,256]{1,0:T(8,128)}) custom-call(s32[1]{0:T(128)} %bitcast.35.core_ref, f32[128,256]{1,0:T(8,128)S(1)} %shard_map.80.refs_0_, f32[128,256]{1,0:T(8,128)S(1)} %shard_map.81.refs_1_, f32[128,256]{1,0:T(8,128)S(1)} %collective-permute-done.20.refs_2_), custom_call_target="tpu_custom_call" | custom-call | flops 1000000 | bytes 1000000 | tf_op jit(solution)/shard_map/pallas_call | solution.py:63
  (58 shorter events, 5.4 us)
Async XLA Ops:
  0.6 25.1 %copy-start = (bf16[256,256]{1,0:T(8,128)(2,1)S(1)}, bf16[256,256]{1,0:T(8,128)(2,1)}, u32[]{:S(2)}) copy-start(bf16[256,256]{1,0:T(8,128)(2,1)} %param.6) | copy-start | bytes 393220
  0.6 13.5 %copy-start.1 = (bf16[1,1,24,128,128]{4,3,2,1,0:T(8,128)(2,1)S(1)}, bf16[1,1,24,128,128]{4,3,2,1,0:T(8,128)(2,1)}, u32[]{:S(2)}) copy-start(bf16[1,1,24,128,128]{4,3,2,1,0:T(8,128)(2,1)} %param.8) | copy-start | bytes 2359300
  0.7 10.9 %collective-permute-start.2 = (bf16[128,256]{1,0:T(8,128)(2,1)}, bf16[128,256]{1,0:T(8,128)(2,1)S(1)}, u32[]{:S(2)}, u32[]{:S(2)}) collective-permute-start(bf16[128,256]{1,0:T(8,128)(2,1)} %param.5), channel_id=1, source_target_pairs={{0,24},{2,26},{4,28},{6,30},{8,16},{10,18},{12,20},{14,22},{16,8},... | collective-permute-start | bytes 196616 | tf_op jit(solution)/shard_map/ppermute | solution.py:12
  5.8 5.8 %collective-permute-start.1 = (bf16[128,256]{1,0:T(8,128)(2,1)}, bf16[128,256]{1,0:T(8,128)(2,1)S(1)}, u32[]{:S(2)}, u32[]{:S(2)}) collective-permute-start(bf16[128,256]{1,0:T(8,128)(2,1)} %param.5), channel_id=1, source_target_pairs={{0,16},{2,18},{4,20},{6,22},{8,24},{10,26},{12,28},{14,30},{16,0},... | collective-permute-start | bytes 196616 | tf_op jit(solution)/shard_map/ppermute | solution.py:12
  5.8 4.6 %collective-permute-start = (bf16[128,256]{1,0:T(8,128)(2,1)}, bf16[128,256]{1,0:T(8,128)(2,1)S(1)}, u32[]{:S(2)}, u32[]{:S(2)}) collective-permute-start(bf16[128,256]{1,0:T(8,128)(2,1)} %param.5), channel_id=1, source_target_pairs={{0,8},{2,10},{4,12},{6,14},{8,0},{10,2},{12,4},{14,6},{16,24},{18,... | collective-permute-start | bytes 196616 | tf_op jit(solution)/shard_map/ppermute | solution.py:12
  6.4 7.7 %collective-permute-start.6 = (bf16[128,256]{1,0:T(8,128)(2,1)}, bf16[128,256]{1,0:T(8,128)(2,1)S(1)}, u32[]{:S(2)}, u32[]{:S(2)}) collective-permute-start(bf16[128,256]{1,0:T(8,128)(2,1)} %param.5), channel_id=1, source_target_pairs={{0,4},{2,6},{4,0},{6,2},{8,12},{10,14},{12,8},{14,10},{16,20},{18,... | collective-permute-start | bytes 196616 | tf_op jit(solution)/shard_map/ppermute | solution.py:12
  8.0 5.1 %collective-permute-start.4 = (bf16[128,256]{1,0:T(8,128)(2,1)}, bf16[128,256]{1,0:T(8,128)(2,1)S(1)}, u32[]{:S(2)}, u32[]{:S(2)}) collective-permute-start(bf16[128,256]{1,0:T(8,128)(2,1)} %param.7), channel_id=1, source_target_pairs={{0,1},{1,0},{2,3},{3,2},{4,5},{5,4},{6,7},{7,6},{8,9},{9,8},{10,11... | collective-permute-start | bytes 196616 | tf_op jit(solution)/shard_map/ppermute | solution.py:12
  11.6 6.5 %collective-permute-start.3 = (bf16[384,256]{1,0:T(8,128)(2,1)S(1)}, bf16[384,256]{1,0:T(8,128)(2,1)S(1)}, u32[]{:S(2)}, u32[]{:S(2)}) collective-permute-start(bf16[384,256]{1,0:T(8,128)(2,1)S(1)} %get-tuple-element.33.refs_0_), channel_id=1, source_target_pairs={{0,4},{2,6},{4,0},{6,2},{8,12},{10,14},{12,8},{14,10},{16,20},{18,... | collective-permute-start | bytes 589832 | tf_op jit(solution)/shard_map/ppermute | solution.py:12
  13.2 2.9 %collective-permute-start.5 = (bf16[512,256]{1,0:T(8,128)(2,1)S(1)}, bf16[512,256]{1,0:T(8,128)(2,1)S(1)}, u32[]{:S(2)}, u32[]{:S(2)}) collective-permute-start(bf16[512,256]{1,0:T(8,128)(2,1)S(1)} %get-tuple-element.32), channel_id=1, source_target_pairs={{0,2},{2,0},{4,6},{6,4},{8,10},{10,8},{12,14},{14,12},{16,18},{18,... | collective-permute-start | bytes 786440 | tf_op jit(solution)/shard_map/ppermute | solution.py:12
  14.1 0.7 %copy-start.2 = (s32[1,1,24]{2,1,0:T(1,128)S(1)}, s32[1,1,24]{2,1,0:T(1,128)}, u32[]{:S(2)}) copy-start(s32[1,1,24]{2,1,0:T(1,128)} %param.9) | copy-start | bytes 292
  18.2 1.6 %collective-permute-start.7 = (bf16[512,256]{1,0:T(8,128)(2,1)S(1)}, bf16[512,256]{1,0:T(8,128)(2,1)S(1)}, u32[]{:S(2)}, u32[]{:S(2)}) collective-permute-start(bf16[512,256]{1,0:T(8,128)(2,1)S(1)} %constant_dynamic-update-slice_fusion.7), channel_id=1, source_target_pairs={{0,2},{2,0},{4,6},{6,4},{8,10},{10,8},{12,14},{14,12},{16,18},{18,... | collective-permute-start | bytes 786440 | tf_op jit(solution)/shard_map/ppermute | solution.py:12
  20.0 5.6 %collective-permute-start.8 = (bf16[2,128,256]{2,1,0:T(8,128)(2,1)S(1)}, bf16[2,128,256]{2,1,0:T(8,128)(2,1)S(1)}, u32[]{:S(2)}, u32[]{:S(2)}) collective-permute-start(bf16[2,128,256]{2,1,0:T(8,128)(2,1)S(1)} %add_convert_fusion.1), channel_id=1, source_target_pairs={{0,1},{1,0},{2,3},{3,2},{4,5},{5,4},{6,7},{7,6},{8,9},{9,8},{10,11... | collective-permute-start | bytes 393224 | tf_op jit(solution)/shard_map/ppermute | solution.py:12
  22.1 6.2 %collective-permute-start.9 = (bf16[2,2,4,128,128]{3,4,0,2,1:T(8,128)(2,1)S(1)}, bf16[2,2,4,128,128]{3,4,0,2,1:T(8,128)(2,1)S(1)}, u32[]{:S(2)}, u32[]{:S(2)}) collective-permute-start(bf16[2,2,4,128,128]{3,4,0,2,1:T(8,128)(2,1)S(1)} %copy.13), channel_id=1, source_target_pairs={{0,2},{2,0},{4,6},{6,4},{8,10},{10,8},{12,14},{14,12},{16,18},{18,... | collective-permute-start | bytes 1572872 | tf_op jit(solution)/shard_map/ppermute | solution.py:12
  25.7 2.4 %collective-permute-start.12 = (bf16[256,256]{1,0:T(8,128)(2,1)S(1)}, bf16[256,256]{1,0:T(8,128)(2,1)S(1)}, u32[]{:S(2)}, u32[]{:S(2)}) collective-permute-start(bf16[256,256]{1,0:T(8,128)(2,1)S(1)} %bitcast.128), channel_id=1, source_target_pairs={{0,2},{2,0},{4,6},{6,4},{8,10},{10,8},{12,14},{14,12},{16,18},{18,... | collective-permute-start | bytes 393224 | tf_op jit(solution)/shard_map/ppermute | solution.py:12
  26.3 1.5 %collective-permute-start.10 = (bf16[256,256]{1,0:T(8,128)(2,1)S(1)}, bf16[256,256]{1,0:T(8,128)(2,1)S(1)}, u32[]{:S(2)}, u32[]{:S(2)}) collective-permute-start(bf16[256,256]{1,0:T(8,128)(2,1)S(1)} %get-tuple-element.28), channel_id=1, source_target_pairs={{0,2},{2,0},{4,6},{6,4},{8,10},{10,8},{12,14},{14,12},{16,18},{18,... | collective-permute-start | bytes 393224 | tf_op jit(solution)/shard_map/ppermute | solution.py:12
  28.5 8.6 %collective-permute-start.11 = (bf16[4,128,256]{2,1,0:T(8,128)(2,1)S(1)}, bf16[4,128,256]{2,1,0:T(8,128)(2,1)S(1)}, u32[]{:S(2)}, u32[]{:S(2)}) collective-permute-start(bf16[4,128,256]{2,1,0:T(8,128)(2,1)S(1)} %fusion.3.refs_1_), channel_id=1, source_target_pairs={{0,4},{2,6},{4,0},{6,2},{8,12},{10,14},{12,8},{14,10},{16,20},{18,... | collective-permute-start | bytes 786440 | tf_op jit(solution)/shard_map/ppermute | solution.py:12
  30.3 9.1 %collective-permute-start.15 = (bf16[128,256]{1,0:T(8,128)(2,1)S(1)}, bf16[128,256]{1,0:T(8,128)(2,1)S(1)}, u32[]{:S(2)}, u32[]{:S(2)}) collective-permute-start(bf16[128,256]{1,0:T(8,128)(2,1)S(1)} %shard_map.77.refs_0_), channel_id=1, source_target_pairs={{0,24},{2,26},{4,28},{6,30},{8,16},{10,18},{12,20},{14,22},{16,8},... | collective-permute-start | bytes 196616 | tf_op jit(solution)/shard_map/ppermute | solution.py:12
  32.1 7.3 %collective-permute-start.14 = (bf16[128,256]{1,0:T(8,128)(2,1)S(1)}, bf16[128,256]{1,0:T(8,128)(2,1)S(1)}, u32[]{:S(2)}, u32[]{:S(2)}) collective-permute-start(bf16[128,256]{1,0:T(8,128)(2,1)S(1)} %shard_map.77.refs_0_), channel_id=1, source_target_pairs={{0,16},{2,18},{4,20},{6,22},{8,24},{10,26},{12,28},{14,30},{16,0},... | collective-permute-start | bytes 196616 | tf_op jit(solution)/shard_map/ppermute | solution.py:12
  32.1 7.3 %collective-permute-start.13 = (bf16[128,256]{1,0:T(8,128)(2,1)S(1)}, bf16[128,256]{1,0:T(8,128)(2,1)S(1)}, u32[]{:S(2)}, u32[]{:S(2)}) collective-permute-start(bf16[128,256]{1,0:T(8,128)(2,1)S(1)} %shard_map.77.refs_0_), channel_id=1, source_target_pairs={{0,8},{2,10},{4,12},{6,14},{8,0},{10,2},{12,4},{14,6},{16,24},{18,... | collective-permute-start | bytes 196616 | tf_op jit(solution)/shard_map/ppermute | solution.py:12
  37.4 9.1 %collective-permute-start.18 = (bf16[128,256]{1,0:T(8,128)(2,1)S(1)}, bf16[128,256]{1,0:T(8,128)(2,1)S(1)}, u32[]{:S(2)}, u32[]{:S(2)}) collective-permute-start(bf16[128,256]{1,0:T(8,128)(2,1)S(1)} %get-tuple-element.26.refs_4_), channel_id=1, source_target_pairs={{0,24},{2,26},{4,28},{6,30},{8,16},{10,18},{12,20},{14,22},{16,8},... | collective-permute-start | bytes 196616 | tf_op jit(solution)/shard_map/ppermute | solution.py:12
  39.5 4.3 %collective-permute-start.19 = (bf16[128,256]{1,0:T(8,128)(2,1)S(1)}, bf16[128,256]{1,0:T(8,128)(2,1)S(1)}, u32[]{:S(2)}, u32[]{:S(2)}) collective-permute-start(bf16[128,256]{1,0:T(8,128)(2,1)S(1)} %shard_map.78.refs_1_.refs_0_), channel_id=1, source_target_pairs={{0,4},{2,6},{4,0},{6,2},{8,12},{10,14},{12,8},{14,10},{16,20},{18,... | collective-permute-start | bytes 196616 | tf_op jit(solution)/shard_map/ppermute | solution.py:12
  41.0 4.4 %collective-permute-start.16 = (bf16[128,256]{1,0:T(8,128)(2,1)S(1)}, bf16[128,256]{1,0:T(8,128)(2,1)S(1)}, u32[]{:S(2)}, u32[]{:S(2)}) collective-permute-start(bf16[128,256]{1,0:T(8,128)(2,1)S(1)} %shard_map.79), channel_id=1, source_target_pairs={{0,8},{2,10},{4,12},{6,14},{8,0},{10,2},{12,4},{14,6},{16,24},{18,... | collective-permute-start | bytes 196616 | tf_op jit(solution)/shard_map/ppermute | solution.py:12
  41.0 5.5 %collective-permute-start.17 = (bf16[128,256]{1,0:T(8,128)(2,1)S(1)}, bf16[128,256]{1,0:T(8,128)(2,1)S(1)}, u32[]{:S(2)}, u32[]{:S(2)}) collective-permute-start(bf16[128,256]{1,0:T(8,128)(2,1)S(1)} %get-tuple-element.25), channel_id=1, source_target_pairs={{0,16},{2,18},{4,20},{6,22},{8,24},{10,26},{12,28},{14,30},{16,0},... | collective-permute-start | bytes 196616 | tf_op jit(solution)/shard_map/ppermute | solution.py:12
  43.8 2.8 %collective-permute-start.20 = (f32[128,256]{1,0:T(8,128)S(1)}, f32[128,256]{1,0:T(8,128)S(1)}, u32[]{:S(2)}, u32[]{:S(2)}) collective-permute-start(f32[128,256]{1,0:T(8,128)S(1)} %shard_map.81.refs_1_), channel_id=1, source_target_pairs={{0,2},{2,0},{4,6},{6,4},{8,10},{10,8},{12,14},{14,12},{16,18},{18,... | collective-permute-start | bytes 393224 | tf_op jit(solution)/shard_map/ppermute | solution.py:12

commit v7 on v6

--- a/solution.py
+++ b/solution.py
@@ -206,6 +206,7 @@
     for k in (1,):
         sent_z[k - 1] = total([sent_z[k - 1]], bf16, 100000000, [half])
     got_z = [swap(sent_z[k - 1], "row", 4 * k) for k in range(1, depth)]
+    half = total([half], bf16, 5 * 10**9)
     half = total([half, swap(half, "row", 2)], f32, 10**8)
     total_nodes = own_rows * row_count * col_count
     scale = 1.0 / math.sqrt(total_nodes)

time: 47.5 us -> 47.3 us (level)
  no operation moved by 1% of the time
where the time goes in v7:
time: 47.3 us; the launch traced here: 47.1 us
  starting transfers between devices  25.4 us (54%)
  waiting for transfers between devices  12.1 us (26%)
  matrix products  2.95 us (6%)
  Pallas kernels  2.16 us (5%)
  local copies, waits for them, and re-layouts  1.85 us (4%)
  other arithmetic  1.66 us (4%)
  between operations  0.96 us (2%)
    ppermute x21, starting transfers between devices, swap(): lax.ppermute(x, axis, [(i, i ^ bit) for i in range(lax.axis_size(axis))])  25.4 us
    ppermute x21, waiting for transfers between devices, swap(): lax.ppermute(x, axis, [(i, i ^ bit) for i in range(lax.axis_size(axis))])  12.1 us
    unnamed x10, local copies, waits for them, and re-layouts  1.52 us
    pallas_call x1, Pallas kernels, dense_tile(): pl.pallas_call(body, out_shape=(shape, shape), in_specs=[smem, smem, vmem...  1.3 us
  transfers between devices with their start and end apart: 21, of which 9 were waited for; matrix products, arithmetic and copies ran while one was open for 11% of the time, Pallas kernels for 3%

profile of v7, /device:TPU:0, one launch (start us, length us, event | category | flops | bytes accessed | tf_op | source)
XLA Modules:
  0.0 47.1 jit_solution(2680212856818302870)
XLA Ops:
  0.7 5.1 %collective-permute-start.2 = (bf16[128,256]{1,0:T(8,128)(2,1)}, bf16[128,256]{1,0:T(8,128)(2,1)S(1)}, u32[]{:S(2)}, u32[]{:S(2)}) collective-permute-start(bf16[128,256]{1,0:T(8,128)(2,1)} %param.5), channel_id=1, source_target_pairs={{0,24},{2,26},{4,28},{6,30},{8,16},{10,18},{12,20},{14,22},{16,8},... | collective-permute-start | bytes 196616 | tf_op jit(solution)/shard_map/ppermute | solution.py:12
  5.8 0.6 %collective-permute-start = (bf16[128,256]{1,0:T(8,128)(2,1)}, bf16[128,256]{1,0:T(8,128)(2,1)S(1)}, u32[]{:S(2)}, u32[]{:S(2)}) collective-permute-start(bf16[128,256]{1,0:T(8,128)(2,1)} %param.5), channel_id=1, source_target_pairs={{0,8},{2,10},{4,12},{6,14},{8,0},{10,2},{12,4},{14,6},{16,24},{18,... | collective-permute-start | bytes 196616 | tf_op jit(solution)/shard_map/ppermute | solution.py:12
  6.4 1.6 %collective-permute-start.6 = (bf16[128,256]{1,0:T(8,128)(2,1)}, bf16[128,256]{1,0:T(8,128)(2,1)S(1)}, u32[]{:S(2)}, u32[]{:S(2)}) collective-permute-start(bf16[128,256]{1,0:T(8,128)(2,1)} %param.5), channel_id=1, source_target_pairs={{0,4},{2,6},{4,0},{6,2},{8,12},{10,14},{12,8},{14,10},{16,20},{18,... | collective-permute-start | bytes 196616 | tf_op jit(solution)/shard_map/ppermute | solution.py:12
  8.0 1.5 %collective-permute-start.4 = (bf16[128,256]{1,0:T(8,128)(2,1)}, bf16[128,256]{1,0:T(8,128)(2,1)S(1)}, u32[]{:S(2)}, u32[]{:S(2)}) collective-permute-start(bf16[128,256]{1,0:T(8,128)(2,1)} %param.7), channel_id=1, source_target_pairs={{0,1},{1,0},{2,3},{3,2},{4,5},{5,4},{6,7},{7,6},{8,9},{9,8},{10,11... | collective-permute-start | bytes 196616 | tf_op jit(solution)/shard_map/ppermute | solution.py:12
  9.6 0.8 %constant_dynamic-update-slice_fusion.6 = bf16[512,256]{1,0:T(8,128)(2,1)S(1)} fusion(bf16[128,256]{1,0:T(8,128)(2,1)} %param.5), kind=kLoop, calls=%fused_computation.43 | loop fusion | bytes 131072
  10.4 1.2 %collective-permute-done.1 = bf16[128,256]{1,0:T(8,128)(2,1)S(1)} collective-permute-done((bf16[128,256]{1,0:T(8,128)(2,1)}, bf16[128,256]{1,0:T(8,128)(2,1)S(1)}, u32[]{:S(2)}, u32[]{:S(2)}) %collective-permute-start.1) | collective-permute-done | bytes 65568 | tf_op jit(solution)/shard_map/ppermute | solution.py:12
  11.6 1.6 %collective-permute-start.3 = (bf16[384,256]{1,0:T(8,128)(2,1)S(1)}, bf16[384,256]{1,0:T(8,128)(2,1)S(1)}, u32[]{:S(2)}, u32[]{:S(2)}) collective-permute-start(bf16[384,256]{1,0:T(8,128)(2,1)S(1)} %get-tuple-element.33.refs_0_), channel_id=1, source_target_pairs={{0,4},{2,6},{4,0},{6,2},{8,12},{10,14},{12,8},{14,10},{16,20},{18,... | collective-permute-start | bytes 589832 | tf_op jit(solution)/shard_map/ppermute | solution.py:12
  13.2 0.9 %broadcast_select_fusion.1 = (bf16[128,256]{1,0:T(8,128)(2,1)S(1)}, bf16[128,256]{1,0:T(8,128)(2,1)S(1)}) fusion(bf16[128,256]{1,0:T(8,128)(2,1)} %param.7, bf16[128,256]{1,0:T(8,128)(2,1)S(1)} %collective-permute-done.4, pred[]{:T(512)S(6)} %eq.4), kind=kLoop, calls=%fused_computation.36 | loop fusion | flops 65536 | bytes 262145 | tf_op jit(solution)/shard_map/jit(_where)/select_n | solution.py:144
  14.7 1.3 %shard_map.76 = (bf16[16,128,128]{2,1,0:T(8,128)(2,1)S(1)}, bf16[16,128,128]{2,1,0:T(8,128)(2,1)S(1)}) custom-call(s32[24]{0:T(128)S(1)} %bitcast.123, s32[1]{0:T(128)} %bitcast.1.row_ref, bf16[24,128,128]{2,1,0:T(8,128)(2,1)S(1)} %bitcast.122, bf16[384,256]{1,0:T(8,128)(2,1)S(1)} %get-tuple-element.33.refs_0_), custom_call_target="tpu_custom_call" | custom-call | flops 3000000000 | bytes 1000000 | tf_op jit(solution)/shard_map/pallas_call | solution.py:103
  16.5 1.6 %collective-permute-done.3 = bf16[384,256]{1,0:T(8,128)(2,1)S(1)} collective-permute-done((bf16[384,256]{1,0:T(8,128)(2,1)S(1)}, bf16[384,256]{1,0:T(8,128)(2,1)S(1)}, u32[]{:S(2)}, u32[]{:S(2)}) %collective-permute-start.3) | collective-permute-done | bytes 196640 | tf_op jit(solution)/shard_map/ppermute | solution.py:12
  18.5 1.3 %collective-permute-done.7 = bf16[512,256]{1,0:T(8,128)(2,1)S(1)} collective-permute-done((bf16[512,256]{1,0:T(8,128)(2,1)S(1)}, bf16[512,256]{1,0:T(8,128)(2,1)S(1)}, u32[]{:S(2)}, u32[]{:S(2)}) %collective-permute-start.7) | collective-permute-done | bytes 262176 | tf_op jit(solution)/shard_map/ppermute | solution.py:12
  20.0 1.8 %collective-permute-start.8 = (bf16[2,128,256]{2,1,0:T(8,128)(2,1)S(1)}, bf16[2,128,256]{2,1,0:T(8,128)(2,1)S(1)}, u32[]{:S(2)}, u32[]{:S(2)}) collective-permute-start(bf16[2,128,256]{2,1,0:T(8,128)(2,1)S(1)} %add_convert_fusion.1), channel_id=1, source_target_pairs={{0,1},{1,0},{2,3},{3,2},{4,5},{5,4},{6,7},{7,6},{8,9},{9,8},{10,11... | collective-permute-start | bytes 393224 | tf_op jit(solution)/shard_map/ppermute | solution.py:12
  22.1 3.5 %collective-permute-done.8 = bf16[2,128,256]{2,1,0:T(8,128)(2,1)S(1)} collective-permute-done((bf16[2,128,256]{2,1,0:T(8,128)(2,1)S(1)}, bf16[2,128,256]{2,1,0:T(8,128)(2,1)S(1)}, u32[]{:S(2)}, u32[]{:S(2)}) %collective-permute-start.8) | collective-permute-done | bytes 131104 | tf_op jit(solution)/shard_map/ppermute | solution.py:12
  28.5 1.7 %collective-permute-start.11 = (bf16[4,128,256]{2,1,0:T(8,128)(2,1)S(1)}, bf16[4,128,256]{2,1,0:T(8,128)(2,1)S(1)}, u32[]{:S(2)}, u32[]{:S(2)}) collective-permute-start(bf16[4,128,256]{2,1,0:T(8,128)(2,1)S(1)} %fusion.3.refs_1_), channel_id=1, source_target_pairs={{0,4},{2,6},{4,0},{6,2},{8,12},{10,14},{12,8},{14,10},{16,20},{18,... | collective-permute-start | bytes 786440 | tf_op jit(solution)/shard_map/ppermute | solution.py:12
  30.3 1.8 %collective-permute-start.15 = (bf16[128,256]{1,0:T(8,128)(2,1)S(1)}, bf16[128,256]{1,0:T(8,128)(2,1)S(1)}, u32[]{:S(2)}, u32[]{:S(2)}) collective-permute-start(bf16[128,256]{1,0:T(8,128)(2,1)S(1)} %shard_map.77.refs_0_), channel_id=1, source_target_pairs={{0,24},{2,26},{4,28},{6,30},{8,16},{10,18},{12,20},{14,22},{16,8},... | collective-permute-start | bytes 196616 | tf_op jit(solution)/shard_map/ppermute | solution.py:12
  32.1 2.6 %collective-permute-start.13 = (bf16[128,256]{1,0:T(8,128)(2,1)S(1)}, bf16[128,256]{1,0:T(8,128)(2,1)S(1)}, u32[]{:S(2)}, u32[]{:S(2)}) collective-permute-start(bf16[128,256]{1,0:T(8,128)(2,1)S(1)} %shard_map.77.refs_0_), channel_id=1, source_target_pairs={{0,8},{2,10},{4,12},{6,14},{8,0},{10,2},{12,4},{14,6},{16,24},{18,... | collective-permute-start | bytes 196616 | tf_op jit(solution)/shard_map/ppermute | solution.py:12
  34.7 0.6 %multiply_convert_fusion.1 = bf16[128,256]{1,0:T(8,128)(2,1)} fusion(f32[256,256]{1,0:T(8,128)S(1)} %get-tuple-element.29, s32[]{:T(128)S(6)} %select_n.23, f32[256,256]{1,0:T(8,128)S(1)} %fusion.11), kind=kLoop, calls=%fused_computation.28 | loop fusion | flops 65536 | bytes 327684 | tf_op jit(solution)/shard_map/convert_element_type | solution.py:219
  35.4 1.8 %collective-permute-done.11 = bf16[4,128,256]{2,1,0:T(8,128)(2,1)S(1)} collective-permute-done((bf16[4,128,256]{2,1,0:T(8,128)(2,1)S(1)}, bf16[4,128,256]{2,1,0:T(8,128)(2,1)S(1)}, u32[]{:S(2)}, u32[]{:S(2)}) %collective-permute-start.11) | collective-permute-done | bytes 262176 | tf_op jit(solution)/shard_map/ppermute | solution.py:12
  37.4 2.0 %collective-permute-start.18 = (bf16[128,256]{1,0:T(8,128)(2,1)S(1)}, bf16[128,256]{1,0:T(8,128)(2,1)S(1)}, u32[]{:S(2)}, u32[]{:S(2)}) collective-permute-start(bf16[128,256]{1,0:T(8,128)(2,1)S(1)} %get-tuple-element.26.refs_4_), channel_id=1, source_target_pairs={{0,24},{2,26},{4,28},{6,30},{8,16},{10,18},{12,20},{14,22},{16,8},... | collective-permute-start | bytes 196616 | tf_op jit(solution)/shard_map/ppermute | solution.py:12
  39.6 1.6 %collective-permute-start.19 = (bf16[128,256]{1,0:T(8,128)(2,1)S(1)}, bf16[128,256]{1,0:T(8,128)(2,1)S(1)}, u32[]{:S(2)}, u32[]{:S(2)}) collective-permute-start(bf16[128,256]{1,0:T(8,128)(2,1)S(1)} %shard_map.81.refs_0_), channel_id=1, source_target_pairs={{0,4},{2,6},{4,0},{6,2},{8,12},{10,14},{12,8},{14,10},{16,20},{18,... | collective-permute-start | bytes 196616 | tf_op jit(solution)/shard_map/ppermute | solution.py:12
  41.1 2.6 %collective-permute-start.17 = (bf16[128,256]{1,0:T(8,128)(2,1)S(1)}, bf16[128,256]{1,0:T(8,128)(2,1)S(1)}, u32[]{:S(2)}, u32[]{:S(2)}) collective-permute-start(bf16[128,256]{1,0:T(8,128)(2,1)S(1)} %get-tuple-element.25), channel_id=1, source_target_pairs={{0,16},{2,18},{4,20},{6,22},{8,24},{10,26},{12,28},{14,30},{16,0},... | collective-permute-start | bytes 196616 | tf_op jit(solution)/shard_map/ppermute | solution.py:12
  44.0 1.0 %collective-permute-done.16.refs_1_ = bf16[128,256]{1,0:T(8,128)(2,1)S(1)} collective-permute-done((bf16[128,256]{1,0:T(8,128)(2,1)S(1)}, bf16[128,256]{1,0:T(8,128)(2,1)S(1)}, u32[]{:S(2)}, u32[]{:S(2)}) %collective-permute-start.16) | collective-permute-done | bytes 65568 | tf_op jit(solution)/shard_map/ppermute | solution.py:12
  45.0 1.3 %collective-permute-done.17.refs_2_ = bf16[128,256]{1,0:T(8,128)(2,1)S(1)} collective-permute-done((bf16[128,256]{1,0:T(8,128)(2,1)S(1)}, bf16[128,256]{1,0:T(8,128)(2,1)S(1)}, u32[]{:S(2)}, u32[]{:S(2)}) %collective-permute-start.17) | collective-permute-done | bytes 65568 | tf_op jit(solution)/shard_map/ppermute | solution.py:12
  46.3 0.8 %shard_map.83 = (bf16[128,256]{1,0:T(8,128)(2,1)}, f32[256,256]{1,0:T(8,128)}) custom-call(s32[1]{0:T(128)} %bitcast.35.core_ref, f32[128,256]{1,0:T(8,128)S(1)} %shard_map.80.refs_0_, f32[128,256]{1,0:T(8,128)S(1)} %shard_map.82.refs_1_, f32[128,256]{1,0:T(8,128)S(1)} %collective-permute-done.20.refs_2_), custom_call_target="tpu_custom_call" | custom-call | flops 1000000 | bytes 1000000 | tf_op jit(solution)/shard_map/pallas_call | solution.py:63
  (59 shorter events, 5.6 us)
Async XLA Ops:
  0.6 25.1 %copy-start = (bf16[256,256]{1,0:T(8,128)(2,1)S(1)}, bf16[256,256]{1,0:T(8,128)(2,1)}, u32[]{:S(2)}) copy-start(bf16[256,256]{1,0:T(8,128)(2,1)} %param.6) | copy-start | bytes 393220
  0.6 13.5 %copy-start.1 = (bf16[1,1,24,128,128]{4,3,2,1,0:T(8,128)(2,1)S(1)}, bf16[1,1,24,128,128]{4,3,2,1,0:T(8,128)(2,1)}, u32[]{:S(2)}) copy-start(bf16[1,1,24,128,128]{4,3,2,1,0:T(8,128)(2,1)} %param.8) | copy-start | bytes 2359300
  0.7 10.9 %collective-permute-start.2 = (bf16[128,256]{1,0:T(8,128)(2,1)}, bf16[128,256]{1,0:T(8,128)(2,1)S(1)}, u32[]{:S(2)}, u32[]{:S(2)}) collective-permute-start(bf16[128,256]{1,0:T(8,128)(2,1)} %param.5), channel_id=1, source_target_pairs={{0,24},{2,26},{4,28},{6,30},{8,16},{10,18},{12,20},{14,22},{16,8},... | collective-permute-start | bytes 196616 | tf_op jit(solution)/shard_map/ppermute | solution.py:12
  5.8 5.8 %collective-permute-start.1 = (bf16[128,256]{1,0:T(8,128)(2,1)}, bf16[128,256]{1,0:T(8,128)(2,1)S(1)}, u32[]{:S(2)}, u32[]{:S(2)}) collective-permute-start(bf16[128,256]{1,0:T(8,128)(2,1)} %param.5), channel_id=1, source_target_pairs={{0,16},{2,18},{4,20},{6,22},{8,24},{10,26},{12,28},{14,30},{16,0},... | collective-permute-start | bytes 196616 | tf_op jit(solution)/shard_map/ppermute | solution.py:12
  5.8 4.6 %collective-permute-start = (bf16[128,256]{1,0:T(8,128)(2,1)}, bf16[128,256]{1,0:T(8,128)(2,1)S(1)}, u32[]{:S(2)}, u32[]{:S(2)}) collective-permute-start(bf16[128,256]{1,0:T(8,128)(2,1)} %param.5), channel_id=1, source_target_pairs={{0,8},{2,10},{4,12},{6,14},{8,0},{10,2},{12,4},{14,6},{16,24},{18,... | collective-permute-start | bytes 196616 | tf_op jit(solution)/shard_map/ppermute | solution.py:12
  6.4 7.7 %collective-permute-start.6 = (bf16[128,256]{1,0:T(8,128)(2,1)}, bf16[128,256]{1,0:T(8,128)(2,1)S(1)}, u32[]{:S(2)}, u32[]{:S(2)}) collective-permute-start(bf16[128,256]{1,0:T(8,128)(2,1)} %param.5), channel_id=1, source_target_pairs={{0,4},{2,6},{4,0},{6,2},{8,12},{10,14},{12,8},{14,10},{16,20},{18,... | collective-permute-start | bytes 196616 | tf_op jit(solution)/shard_map/ppermute | solution.py:12
  8.0 5.1 %collective-permute-start.4 = (bf16[128,256]{1,0:T(8,128)(2,1)}, bf16[128,256]{1,0:T(8,128)(2,1)S(1)}, u32[]{:S(2)}, u32[]{:S(2)}) collective-permute-start(bf16[128,256]{1,0:T(8,128)(2,1)} %param.7), channel_id=1, source_target_pairs={{0,1},{1,0},{2,3},{3,2},{4,5},{5,4},{6,7},{7,6},{8,9},{9,8},{10,11... | collective-permute-start | bytes 196616 | tf_op jit(solution)/shard_map/ppermute | solution.py:12
  11.6 6.5 %collective-permute-start.3 = (bf16[384,256]{1,0:T(8,128)(2,1)S(1)}, bf16[384,256]{1,0:T(8,128)(2,1)S(1)}, u32[]{:S(2)}, u32[]{:S(2)}) collective-permute-start(bf16[384,256]{1,0:T(8,128)(2,1)S(1)} %get-tuple-element.33.refs_0_), channel_id=1, source_target_pairs={{0,4},{2,6},{4,0},{6,2},{8,12},{10,14},{12,8},{14,10},{16,20},{18,... | collective-permute-start | bytes 589832 | tf_op jit(solution)/shard_map/ppermute | solution.py:12
  13.2 2.9 %collective-permute-start.5 = (bf16[512,256]{1,0:T(8,128)(2,1)S(1)}, bf16[512,256]{1,0:T(8,128)(2,1)S(1)}, u32[]{:S(2)}, u32[]{:S(2)}) collective-permute-start(bf16[512,256]{1,0:T(8,128)(2,1)S(1)} %get-tuple-element.32), channel_id=1, source_target_pairs={{0,2},{2,0},{4,6},{6,4},{8,10},{10,8},{12,14},{14,12},{16,18},{18,... | collective-permute-start | bytes 786440 | tf_op jit(solution)/shard_map/ppermute | solution.py:12
  14.1 0.7 %copy-start.2 = (s32[1,1,24]{2,1,0:T(1,128)S(1)}, s32[1,1,24]{2,1,0:T(1,128)}, u32[]{:S(2)}) copy-start(s32[1,1,24]{2,1,0:T(1,128)} %param.9) | copy-start | bytes 292
  18.2 1.6 %collective-permute-start.7 = (bf16[512,256]{1,0:T(8,128)(2,1)S(1)}, bf16[512,256]{1,0:T(8,128)(2,1)S(1)}, u32[]{:S(2)}, u32[]{:S(2)}) collective-permute-start(bf16[512,256]{1,0:T(8,128)(2,1)S(1)} %constant_dynamic-update-slice_fusion.7), channel_id=1, source_target_pairs={{0,2},{2,0},{4,6},{6,4},{8,10},{10,8},{12,14},{14,12},{16,18},{18,... | collective-permute-start | bytes 786440 | tf_op jit(solution)/shard_map/ppermute | solution.py:12
  20.0 5.6 %collective-permute-start.8 = (bf16[2,128,256]{2,1,0:T(8,128)(2,1)S(1)}, bf16[2,128,256]{2,1,0:T(8,128)(2,1)S(1)}, u32[]{:S(2)}, u32[]{:S(2)}) collective-permute-start(bf16[2,128,256]{2,1,0:T(8,128)(2,1)S(1)} %add_convert_fusion.1), channel_id=1, source_target_pairs={{0,1},{1,0},{2,3},{3,2},{4,5},{5,4},{6,7},{7,6},{8,9},{9,8},{10,11... | collective-permute-start | bytes 393224 | tf_op jit(solution)/shard_map/ppermute | solution.py:12
  22.1 6.2 %collective-permute-start.9 = (bf16[2,2,4,128,128]{3,4,0,2,1:T(8,128)(2,1)S(1)}, bf16[2,2,4,128,128]{3,4,0,2,1:T(8,128)(2,1)S(1)}, u32[]{:S(2)}, u32[]{:S(2)}) collective-permute-start(bf16[2,2,4,128,128]{3,4,0,2,1:T(8,128)(2,1)S(1)} %copy.13), channel_id=1, source_target_pairs={{0,2},{2,0},{4,6},{6,4},{8,10},{10,8},{12,14},{14,12},{16,18},{18,... | collective-permute-start | bytes 1572872 | tf_op jit(solution)/shard_map/ppermute | solution.py:12
  25.7 2.4 %collective-permute-start.12 = (bf16[256,256]{1,0:T(8,128)(2,1)S(1)}, bf16[256,256]{1,0:T(8,128)(2,1)S(1)}, u32[]{:S(2)}, u32[]{:S(2)}) collective-permute-start(bf16[256,256]{1,0:T(8,128)(2,1)S(1)} %bitcast.128), channel_id=1, source_target_pairs={{0,2},{2,0},{4,6},{6,4},{8,10},{10,8},{12,14},{14,12},{16,18},{18,... | collective-permute-start | bytes 393224 | tf_op jit(solution)/shard_map/ppermute | solution.py:12
  26.3 1.5 %collective-permute-start.10 = (bf16[256,256]{1,0:T(8,128)(2,1)S(1)}, bf16[256,256]{1,0:T(8,128)(2,1)S(1)}, u32[]{:S(2)}, u32[]{:S(2)}) collective-permute-start(bf16[256,256]{1,0:T(8,128)(2,1)S(1)} %get-tuple-element.28), channel_id=1, source_target_pairs={{0,2},{2,0},{4,6},{6,4},{8,10},{10,8},{12,14},{14,12},{16,18},{18,... | collective-permute-start | bytes 393224 | tf_op jit(solution)/shard_map/ppermute | solution.py:12
  28.5 8.6 %collective-permute-start.11 = (bf16[4,128,256]{2,1,0:T(8,128)(2,1)S(1)}, bf16[4,128,256]{2,1,0:T(8,128)(2,1)S(1)}, u32[]{:S(2)}, u32[]{:S(2)}) collective-permute-start(bf16[4,128,256]{2,1,0:T(8,128)(2,1)S(1)} %fusion.3.refs_1_), channel_id=1, source_target_pairs={{0,4},{2,6},{4,0},{6,2},{8,12},{10,14},{12,8},{14,10},{16,20},{18,... | collective-permute-start | bytes 786440 | tf_op jit(solution)/shard_map/ppermute | solution.py:12
  30.3 9.1 %collective-permute-start.15 = (bf16[128,256]{1,0:T(8,128)(2,1)S(1)}, bf16[128,256]{1,0:T(8,128)(2,1)S(1)}, u32[]{:S(2)}, u32[]{:S(2)}) collective-permute-start(bf16[128,256]{1,0:T(8,128)(2,1)S(1)} %shard_map.77.refs_0_), channel_id=1, source_target_pairs={{0,24},{2,26},{4,28},{6,30},{8,16},{10,18},{12,20},{14,22},{16,8},... | collective-permute-start | bytes 196616 | tf_op jit(solution)/shard_map/ppermute | solution.py:12
  32.1 7.3 %collective-permute-start.14 = (bf16[128,256]{1,0:T(8,128)(2,1)S(1)}, bf16[128,256]{1,0:T(8,128)(2,1)S(1)}, u32[]{:S(2)}, u32[]{:S(2)}) collective-permute-start(bf16[128,256]{1,0:T(8,128)(2,1)S(1)} %shard_map.77.refs_0_), channel_id=1, source_target_pairs={{0,16},{2,18},{4,20},{6,22},{8,24},{10,26},{12,28},{14,30},{16,0},... | collective-permute-start | bytes 196616 | tf_op jit(solution)/shard_map/ppermute | solution.py:12
  32.1 7.3 %collective-permute-start.13 = (bf16[128,256]{1,0:T(8,128)(2,1)S(1)}, bf16[128,256]{1,0:T(8,128)(2,1)S(1)}, u32[]{:S(2)}, u32[]{:S(2)}) collective-permute-start(bf16[128,256]{1,0:T(8,128)(2,1)S(1)} %shard_map.77.refs_0_), channel_id=1, source_target_pairs={{0,8},{2,10},{4,12},{6,14},{8,0},{10,2},{12,4},{14,6},{16,24},{18,... | collective-permute-start | bytes 196616 | tf_op jit(solution)/shard_map/ppermute | solution.py:12
  37.4 8.9 %collective-permute-start.18 = (bf16[128,256]{1,0:T(8,128)(2,1)S(1)}, bf16[128,256]{1,0:T(8,128)(2,1)S(1)}, u32[]{:S(2)}, u32[]{:S(2)}) collective-permute-start(bf16[128,256]{1,0:T(8,128)(2,1)S(1)} %get-tuple-element.26.refs_4_), channel_id=1, source_target_pairs={{0,24},{2,26},{4,28},{6,30},{8,16},{10,18},{12,20},{14,22},{16,8},... | collective-permute-start | bytes 196616 | tf_op jit(solution)/shard_map/ppermute | solution.py:12
  39.5 5.5 %collective-permute-start.16 = (bf16[128,256]{1,0:T(8,128)(2,1)S(1)}, bf16[128,256]{1,0:T(8,128)(2,1)S(1)}, u32[]{:S(2)}, u32[]{:S(2)}) collective-permute-start(bf16[128,256]{1,0:T(8,128)(2,1)S(1)} %shard_map.79), channel_id=1, source_target_pairs={{0,8},{2,10},{4,12},{6,14},{8,0},{10,2},{12,4},{14,6},{16,24},{18,... | collective-permute-start | bytes 196616 | tf_op jit(solution)/shard_map/ppermute | solution.py:12
  39.6 4.3 %collective-permute-start.19 = (bf16[128,256]{1,0:T(8,128)(2,1)S(1)}, bf16[128,256]{1,0:T(8,128)(2,1)S(1)}, u32[]{:S(2)}, u32[]{:S(2)}) collective-permute-start(bf16[128,256]{1,0:T(8,128)(2,1)S(1)} %shard_map.81.refs_0_), channel_id=1, source_target_pairs={{0,4},{2,6},{4,0},{6,2},{8,12},{10,14},{12,8},{14,10},{16,20},{18,... | collective-permute-start | bytes 196616 | tf_op jit(solution)/shard_map/ppermute | solution.py:12
  41.1 5.2 %collective-permute-start.17 = (bf16[128,256]{1,0:T(8,128)(2,1)S(1)}, bf16[128,256]{1,0:T(8,128)(2,1)S(1)}, u32[]{:S(2)}, u32[]{:S(2)}) collective-permute-start(bf16[128,256]{1,0:T(8,128)(2,1)S(1)} %get-tuple-element.25), channel_id=1, source_target_pairs={{0,16},{2,18},{4,20},{6,22},{8,24},{10,26},{12,28},{14,30},{16,0},... | collective-permute-start | bytes 196616 | tf_op jit(solution)/shard_map/ppermute | solution.py:12
  43.9 2.4 %collective-permute-start.20 = (f32[128,256]{1,0:T(8,128)S(1)}, f32[128,256]{1,0:T(8,128)S(1)}, u32[]{:S(2)}, u32[]{:S(2)}) collective-permute-start(f32[128,256]{1,0:T(8,128)S(1)} %shard_map.82.refs_1_), channel_id=1, source_target_pairs={{0,2},{2,0},{4,6},{6,4},{8,10},{10,8},{12,14},{14,12},{16,18},{18,... | collective-permute-start | bytes 393224 | tf_op jit(solution)/shard_map/ppermute | solution.py:12

commit v8 on v7

--- a/solution.py
+++ b/solution.py
@@ -188,7 +188,6 @@
         return own + jnp.einsum(spec, partner[:, quarter], partner_panel, preferred_element_type=f32)
 
     sent_x = backward(1).astype(bf16)
-    sent_x, pre = lax.optimization_barrier((sent_x, pre))
     got_x = swap(sent_x, "row", 2)
     mine = backward(0)
 

time: 47.3 us -> 47.4 us (level)
  transfers between devices with their start and end apart: 21 -> 21, of which waited for: 9 -> 8; matrix products, arithmetic and copies ran while one was open for 11% -> 11% of each run, Pallas kernels for 3% -> 3%
where the time goes in v8:
time: 47.4 us; the launch traced here: 47.2 us
  starting transfers between devices  25.5 us (54%)
  waiting for transfers between devices  12.1 us (26%)
  matrix products  2.94 us (6%)
  Pallas kernels  2.16 us (5%)
  local copies, waits for them, and re-layouts  1.85 us (4%)
  other arithmetic  1.67 us (4%)
  between operations  0.96 us (2%)
    ppermute x21, starting transfers between devices, swap(): lax.ppermute(x, axis, [(i, i ^ bit) for i in range(lax.axis_size(axis))])  25.5 us
    ppermute x21, waiting for transfers between devices, swap(): lax.ppermute(x, axis, [(i, i ^ bit) for i in range(lax.axis_size(axis))])  12.1 us
    unnamed x10, local copies, waits for them, and re-layouts  1.52 us
    pallas_call x1, Pallas kernels, dense_tile(): pl.pallas_call(body, out_shape=(shape, shape), in_specs=[smem, smem, vmem...  1.3 us
  transfers between devices with their start and end apart: 21, of which 8 were waited for; matrix products, arithmetic and copies ran while one was open for 11% of the time, Pallas kernels for 3%

profile of v8, /device:TPU:0, one launch (start us, length us, event | category | flops | bytes accessed | tf_op | source)
XLA Modules:
  0.0 47.2 jit_solution(13653037889663261204)
XLA Ops:
  0.7 5.1 %collective-permute-start.2 = (bf16[128,256]{1,0:T(8,128)(2,1)}, bf16[128,256]{1,0:T(8,128)(2,1)S(1)}, u32[]{:S(2)}, u32[]{:S(2)}) collective-permute-start(bf16[128,256]{1,0:T(8,128)(2,1)} %param.5), channel_id=1, source_target_pairs={{0,24},{2,26},{4,28},{6,30},{8,16},{10,18},{12,20},{14,22},{16,8},... | collective-permute-start | bytes 196616 | tf_op jit(solution)/shard_map/ppermute | solution.py:12
  5.8 0.6 %collective-permute-start = (bf16[128,256]{1,0:T(8,128)(2,1)}, bf16[128,256]{1,0:T(8,128)(2,1)S(1)}, u32[]{:S(2)}, u32[]{:S(2)}) collective-permute-start(bf16[128,256]{1,0:T(8,128)(2,1)} %param.5), channel_id=1, source_target_pairs={{0,8},{2,10},{4,12},{6,14},{8,0},{10,2},{12,4},{14,6},{16,24},{18,... | collective-permute-start | bytes 196616 | tf_op jit(solution)/shard_map/ppermute | solution.py:12
  6.4 1.6 %collective-permute-start.6 = (bf16[128,256]{1,0:T(8,128)(2,1)}, bf16[128,256]{1,0:T(8,128)(2,1)S(1)}, u32[]{:S(2)}, u32[]{:S(2)}) collective-permute-start(bf16[128,256]{1,0:T(8,128)(2,1)} %param.5), channel_id=1, source_target_pairs={{0,4},{2,6},{4,0},{6,2},{8,12},{10,14},{12,8},{14,10},{16,20},{18,... | collective-permute-start | bytes 196616 | tf_op jit(solution)/shard_map/ppermute | solution.py:12
  8.0 1.5 %collective-permute-start.4 = (bf16[128,256]{1,0:T(8,128)(2,1)}, bf16[128,256]{1,0:T(8,128)(2,1)S(1)}, u32[]{:S(2)}, u32[]{:S(2)}) collective-permute-start(bf16[128,256]{1,0:T(8,128)(2,1)} %param.7), channel_id=1, source_target_pairs={{0,1},{1,0},{2,3},{3,2},{4,5},{5,4},{6,7},{7,6},{8,9},{9,8},{10,11... | collective-permute-start | bytes 196616 | tf_op jit(solution)/shard_map/ppermute | solution.py:12
  9.6 0.8 %constant_dynamic-update-slice_fusion.6 = bf16[512,256]{1,0:T(8,128)(2,1)S(1)} fusion(bf16[128,256]{1,0:T(8,128)(2,1)} %param.5), kind=kLoop, calls=%fused_computation.43 | loop fusion | bytes 131072
  10.4 1.2 %collective-permute-done.1 = bf16[128,256]{1,0:T(8,128)(2,1)S(1)} collective-permute-done((bf16[128,256]{1,0:T(8,128)(2,1)}, bf16[128,256]{1,0:T(8,128)(2,1)S(1)}, u32[]{:S(2)}, u32[]{:S(2)}) %collective-permute-start.1) | collective-permute-done | bytes 65568 | tf_op jit(solution)/shard_map/ppermute | solution.py:12
  11.6 1.6 %collective-permute-start.3 = (bf16[384,256]{1,0:T(8,128)(2,1)S(1)}, bf16[384,256]{1,0:T(8,128)(2,1)S(1)}, u32[]{:S(2)}, u32[]{:S(2)}) collective-permute-start(bf16[384,256]{1,0:T(8,128)(2,1)S(1)} %get-tuple-element.29.refs_0_), channel_id=1, source_target_pairs={{0,4},{2,6},{4,0},{6,2},{8,12},{10,14},{12,8},{14,10},{16,20},{18,... | collective-permute-start | bytes 589832 | tf_op jit(solution)/shard_map/ppermute | solution.py:12
  13.2 0.9 %broadcast_select_fusion.1 = (bf16[128,256]{1,0:T(8,128)(2,1)S(1)}, bf16[128,256]{1,0:T(8,128)(2,1)S(1)}) fusion(bf16[128,256]{1,0:T(8,128)(2,1)} %param.7, bf16[128,256]{1,0:T(8,128)(2,1)S(1)} %collective-permute-done.4, pred[]{:T(512)S(6)} %eq.4), kind=kLoop, calls=%fused_computation.36 | loop fusion | flops 65536 | bytes 262145 | tf_op jit(solution)/shard_map/jit(_where)/select_n | solution.py:144
  14.7 1.3 %shard_map.76 = (bf16[16,128,128]{2,1,0:T(8,128)(2,1)S(1)}, bf16[16,128,128]{2,1,0:T(8,128)(2,1)S(1)}) custom-call(s32[24]{0:T(128)S(1)} %bitcast.123, s32[1]{0:T(128)} %bitcast.1.row_ref, bf16[24,128,128]{2,1,0:T(8,128)(2,1)S(1)} %bitcast.122, bf16[384,256]{1,0:T(8,128)(2,1)S(1)} %get-tuple-element.29.refs_0_), custom_call_target="tpu_custom_call" | custom-call | flops 3000000000 | bytes 1000000 | tf_op jit(solution)/shard_map/pallas_call | solution.py:103
  16.5 1.6 %collective-permute-done.3 = bf16[384,256]{1,0:T(8,128)(2,1)S(1)} collective-permute-done((bf16[384,256]{1,0:T(8,128)(2,1)S(1)}, bf16[384,256]{1,0:T(8,128)(2,1)S(1)}, u32[]{:S(2)}, u32[]{:S(2)}) %collective-permute-start.3) | collective-permute-done | bytes 196640 | tf_op jit(solution)/shard_map/ppermute | solution.py:12
  18.5 1.3 %collective-permute-done.7 = bf16[512,256]{1,0:T(8,128)(2,1)S(1)} collective-permute-done((bf16[512,256]{1,0:T(8,128)(2,1)S(1)}, bf16[512,256]{1,0:T(8,128)(2,1)S(1)}, u32[]{:S(2)}, u32[]{:S(2)}) %collective-permute-start.7) | collective-permute-done | bytes 262176 | tf_op jit(solution)/shard_map/ppermute | solution.py:12
  20.0 1.8 %collective-permute-start.8 = (bf16[2,128,256]{2,1,0:T(8,128)(2,1)S(1)}, bf16[2,128,256]{2,1,0:T(8,128)(2,1)S(1)}, u32[]{:S(2)}, u32[]{:S(2)}) collective-permute-start(bf16[2,128,256]{2,1,0:T(8,128)(2,1)S(1)} %add_convert_fusion.1), channel_id=1, source_target_pairs={{0,1},{1,0},{2,3},{3,2},{4,5},{5,4},{6,7},{7,6},{8,9},{9,8},{10,11... | collective-permute-start | bytes 393224 | tf_op jit(solution)/shard_map/ppermute | solution.py:12
  22.1 3.5 %collective-permute-done.8 = bf16[2,128,256]{2,1,0:T(8,128)(2,1)S(1)} collective-permute-done((bf16[2,128,256]{2,1,0:T(8,128)(2,1)S(1)}, bf16[2,128,256]{2,1,0:T(8,128)(2,1)S(1)}, u32[]{:S(2)}, u32[]{:S(2)}) %collective-permute-start.8) | collective-permute-done | bytes 131104 | tf_op jit(solution)/shard_map/ppermute | solution.py:12
  27.6 0.7 %multiply_convert_fusion.1 = bf16[128,256]{1,0:T(8,128)(2,1)} fusion(f32[256,256]{1,0:T(8,128)S(1)} %get-tuple-element.25, s32[]{:T(128)S(6)} %select_n.23, f32[256,256]{1,0:T(8,128)S(1)} %fusion.11), kind=kLoop, calls=%fused_computation.28 | loop fusion | flops 65536 | bytes 327684 | tf_op jit(solution)/shard_map/convert_element_type | solution.py:218
  28.9 1.8 %collective-permute-start.11 = (bf16[4,128,256]{2,1,0:T(8,128)(2,1)S(1)}, bf16[4,128,256]{2,1,0:T(8,128)(2,1)S(1)}, u32[]{:S(2)}, u32[]{:S(2)}) collective-permute-start(bf16[4,128,256]{2,1,0:T(8,128)(2,1)S(1)} %fusion.3.refs_1_), channel_id=1, source_target_pairs={{0,4},{2,6},{4,0},{6,2},{8,12},{10,14},{12,8},{14,10},{16,20},{18,... | collective-permute-start | bytes 786440 | tf_op jit(solution)/shard_map/ppermute | solution.py:12
  30.7 1.8 %collective-permute-start.15 = (bf16[128,256]{1,0:T(8,128)(2,1)S(1)}, bf16[128,256]{1,0:T(8,128)(2,1)S(1)}, u32[]{:S(2)}, u32[]{:S(2)}) collective-permute-start(bf16[128,256]{1,0:T(8,128)(2,1)S(1)} %shard_map.77.refs_0_), channel_id=1, source_target_pairs={{0,24},{2,26},{4,28},{6,30},{8,16},{10,18},{12,20},{14,22},{16,8},... | collective-permute-start | bytes 196616 | tf_op jit(solution)/shard_map/ppermute | solution.py:12
  32.5 2.7 %collective-permute-start.13 = (bf16[128,256]{1,0:T(8,128)(2,1)S(1)}, bf16[128,256]{1,0:T(8,128)(2,1)S(1)}, u32[]{:S(2)}, u32[]{:S(2)}) collective-permute-start(bf16[128,256]{1,0:T(8,128)(2,1)S(1)} %shard_map.77.refs_0_), channel_id=1, source_target_pairs={{0,8},{2,10},{4,12},{6,14},{8,0},{10,2},{12,4},{14,6},{16,24},{18,... | collective-permute-start | bytes 196616 | tf_op jit(solution)/shard_map/ppermute | solution.py:12
  35.2 2.1 %collective-permute-done.11 = bf16[4,128,256]{2,1,0:T(8,128)(2,1)S(1)} collective-permute-done((bf16[4,128,256]{2,1,0:T(8,128)(2,1)S(1)}, bf16[4,128,256]{2,1,0:T(8,128)(2,1)S(1)}, u32[]{:S(2)}, u32[]{:S(2)}) %collective-permute-start.11) | collective-permute-done | bytes 262176 | tf_op jit(solution)/shard_map/ppermute | solution.py:12
  37.5 2.0 %collective-permute-start.18 = (bf16[128,256]{1,0:T(8,128)(2,1)S(1)}, bf16[128,256]{1,0:T(8,128)(2,1)S(1)}, u32[]{:S(2)}, u32[]{:S(2)}) collective-permute-start(bf16[128,256]{1,0:T(8,128)(2,1)S(1)} %get-tuple-element.22.refs_4_), channel_id=1, source_target_pairs={{0,24},{2,26},{4,28},{6,30},{8,16},{10,18},{12,20},{14,22},{16,8},... | collective-permute-start | bytes 196616 | tf_op jit(solution)/shard_map/ppermute | solution.py:12
  39.7 1.5 %collective-permute-start.19 = (bf16[128,256]{1,0:T(8,128)(2,1)S(1)}, bf16[128,256]{1,0:T(8,128)(2,1)S(1)}, u32[]{:S(2)}, u32[]{:S(2)}) collective-permute-start(bf16[128,256]{1,0:T(8,128)(2,1)S(1)} %shard_map.81.refs_0_), channel_id=1, source_target_pairs={{0,4},{2,6},{4,0},{6,2},{8,12},{10,14},{12,8},{14,10},{16,20},{18,... | collective-permute-start | bytes 196616 | tf_op jit(solution)/shard_map/ppermute | solution.py:12
  41.2 2.6 %collective-permute-start.17 = (bf16[128,256]{1,0:T(8,128)(2,1)S(1)}, bf16[128,256]{1,0:T(8,128)(2,1)S(1)}, u32[]{:S(2)}, u32[]{:S(2)}) collective-permute-start(bf16[128,256]{1,0:T(8,128)(2,1)S(1)} %get-tuple-element.21), channel_id=1, source_target_pairs={{0,16},{2,18},{4,20},{6,22},{8,24},{10,26},{12,28},{14,30},{16,0},... | collective-permute-start | bytes 196616 | tf_op jit(solution)/shard_map/ppermute | solution.py:12
  44.1 1.0 %collective-permute-done.16.refs_1_ = bf16[128,256]{1,0:T(8,128)(2,1)S(1)} collective-permute-done((bf16[128,256]{1,0:T(8,128)(2,1)S(1)}, bf16[128,256]{1,0:T(8,128)(2,1)S(1)}, u32[]{:S(2)}, u32[]{:S(2)}) %collective-permute-start.16) | collective-permute-done | bytes 65568 | tf_op jit(solution)/shard_map/ppermute | solution.py:12
  45.0 1.3 %collective-permute-done.17.refs_2_ = bf16[128,256]{1,0:T(8,128)(2,1)S(1)} collective-permute-done((bf16[128,256]{1,0:T(8,128)(2,1)S(1)}, bf16[128,256]{1,0:T(8,128)(2,1)S(1)}, u32[]{:S(2)}, u32[]{:S(2)}) %collective-permute-start.17) | collective-permute-done | bytes 65568 | tf_op jit(solution)/shard_map/ppermute | solution.py:12
  46.4 0.8 %shard_map.83 = (bf16[128,256]{1,0:T(8,128)(2,1)}, f32[256,256]{1,0:T(8,128)}) custom-call(s32[1]{0:T(128)} %bitcast.26.core_ref, f32[128,256]{1,0:T(8,128)S(1)} %shard_map.80.refs_0_, f32[128,256]{1,0:T(8,128)S(1)} %shard_map.82.refs_1_, f32[128,256]{1,0:T(8,128)S(1)} %collective-permute-done.20.refs_2_), custom_call_target="tpu_custom_call" | custom-call | flops 1000000 | bytes 1000000 | tf_op jit(solution)/shard_map/pallas_call | solution.py:63
  (59 shorter events, 5.4 us)
Async XLA Ops:
  0.6 25.1 %copy-start = (bf16[256,256]{1,0:T(8,128)(2,1)S(1)}, bf16[256,256]{1,0:T(8,128)(2,1)}, u32[]{:S(2)}) copy-start(bf16[256,256]{1,0:T(8,128)(2,1)} %param.6) | copy-start | bytes 393220
  0.6 13.5 %copy-start.1 = (bf16[1,1,24,128,128]{4,3,2,1,0:T(8,128)(2,1)S(1)}, bf16[1,1,24,128,128]{4,3,2,1,0:T(8,128)(2,1)}, u32[]{:S(2)}) copy-start(bf16[1,1,24,128,128]{4,3,2,1,0:T(8,128)(2,1)} %param.8) | copy-start | bytes 2359300
  0.7 10.9 %collective-permute-start.2 = (bf16[128,256]{1,0:T(8,128)(2,1)}, bf16[128,256]{1,0:T(8,128)(2,1)S(1)}, u32[]{:S(2)}, u32[]{:S(2)}) collective-permute-start(bf16[128,256]{1,0:T(8,128)(2,1)} %param.5), channel_id=1, source_target_pairs={{0,24},{2,26},{4,28},{6,30},{8,16},{10,18},{12,20},{14,22},{16,8},... | collective-permute-start | bytes 196616 | tf_op jit(solution)/shard_map/ppermute | solution.py:12
  5.8 5.8 %collective-permute-start.1 = (bf16[128,256]{1,0:T(8,128)(2,1)}, bf16[128,256]{1,0:T(8,128)(2,1)S(1)}, u32[]{:S(2)}, u32[]{:S(2)}) collective-permute-start(bf16[128,256]{1,0:T(8,128)(2,1)} %param.5), channel_id=1, source_target_pairs={{0,16},{2,18},{4,20},{6,22},{8,24},{10,26},{12,28},{14,30},{16,0},... | collective-permute-start | bytes 196616 | tf_op jit(solution)/shard_map/ppermute | solution.py:12
  5.8 4.6 %collective-permute-start = (bf16[128,256]{1,0:T(8,128)(2,1)}, bf16[128,256]{1,0:T(8,128)(2,1)S(1)}, u32[]{:S(2)}, u32[]{:S(2)}) collective-permute-start(bf16[128,256]{1,0:T(8,128)(2,1)} %param.5), channel_id=1, source_target_pairs={{0,8},{2,10},{4,12},{6,14},{8,0},{10,2},{12,4},{14,6},{16,24},{18,... | collective-permute-start | bytes 196616 | tf_op jit(solution)/shard_map/ppermute | solution.py:12
  6.4 7.7 %collective-permute-start.6 = (bf16[128,256]{1,0:T(8,128)(2,1)}, bf16[128,256]{1,0:T(8,128)(2,1)S(1)}, u32[]{:S(2)}, u32[]{:S(2)}) collective-permute-start(bf16[128,256]{1,0:T(8,128)(2,1)} %param.5), channel_id=1, source_target_pairs={{0,4},{2,6},{4,0},{6,2},{8,12},{10,14},{12,8},{14,10},{16,20},{18,... | collective-permute-start | bytes 196616 | tf_op jit(solution)/shard_map/ppermute | solution.py:12
  8.0 5.1 %collective-permute-start.4 = (bf16[128,256]{1,0:T(8,128)(2,1)}, bf16[128,256]{1,0:T(8,128)(2,1)S(1)}, u32[]{:S(2)}, u32[]{:S(2)}) collective-permute-start(bf16[128,256]{1,0:T(8,128)(2,1)} %param.7), channel_id=1, source_target_pairs={{0,1},{1,0},{2,3},{3,2},{4,5},{5,4},{6,7},{7,6},{8,9},{9,8},{10,11... | collective-permute-start | bytes 196616 | tf_op jit(solution)/shard_map/ppermute | solution.py:12
  11.6 6.5 %collective-permute-start.3 = (bf16[384,256]{1,0:T(8,128)(2,1)S(1)}, bf16[384,256]{1,0:T(8,128)(2,1)S(1)}, u32[]{:S(2)}, u32[]{:S(2)}) collective-permute-start(bf16[384,256]{1,0:T(8,128)(2,1)S(1)} %get-tuple-element.29.refs_0_), channel_id=1, source_target_pairs={{0,4},{2,6},{4,0},{6,2},{8,12},{10,14},{12,8},{14,10},{16,20},{18,... | collective-permute-start | bytes 589832 | tf_op jit(solution)/shard_map/ppermute | solution.py:12
  13.2 2.9 %collective-permute-start.5 = (bf16[512,256]{1,0:T(8,128)(2,1)S(1)}, bf16[512,256]{1,0:T(8,128)(2,1)S(1)}, u32[]{:S(2)}, u32[]{:S(2)}) collective-permute-start(bf16[512,256]{1,0:T(8,128)(2,1)S(1)} %get-tuple-element.28), channel_id=1, source_target_pairs={{0,2},{2,0},{4,6},{6,4},{8,10},{10,8},{12,14},{14,12},{16,18},{18,... | collective-permute-start | bytes 786440 | tf_op jit(solution)/shard_map/ppermute | solution.py:12
  14.1 0.7 %copy-start.2 = (s32[1,1,24]{2,1,0:T(1,128)S(1)}, s32[1,1,24]{2,1,0:T(1,128)}, u32[]{:S(2)}) copy-start(s32[1,1,24]{2,1,0:T(1,128)} %param.9) | copy-start | bytes 292
  18.2 1.6 %collective-permute-start.7 = (bf16[512,256]{1,0:T(8,128)(2,1)S(1)}, bf16[512,256]{1,0:T(8,128)(2,1)S(1)}, u32[]{:S(2)}, u32[]{:S(2)}) collective-permute-start(bf16[512,256]{1,0:T(8,128)(2,1)S(1)} %constant_dynamic-update-slice_fusion.7), channel_id=1, source_target_pairs={{0,2},{2,0},{4,6},{6,4},{8,10},{10,8},{12,14},{14,12},{16,18},{18,... | collective-permute-start | bytes 786440 | tf_op jit(solution)/shard_map/ppermute | solution.py:12
  20.0 5.6 %collective-permute-start.8 = (bf16[2,128,256]{2,1,0:T(8,128)(2,1)S(1)}, bf16[2,128,256]{2,1,0:T(8,128)(2,1)S(1)}, u32[]{:S(2)}, u32[]{:S(2)}) collective-permute-start(bf16[2,128,256]{2,1,0:T(8,128)(2,1)S(1)} %add_convert_fusion.1), channel_id=1, source_target_pairs={{0,1},{1,0},{2,3},{3,2},{4,5},{5,4},{6,7},{7,6},{8,9},{9,8},{10,11... | collective-permute-start | bytes 393224 | tf_op jit(solution)/shard_map/ppermute | solution.py:12
  22.1 6.6 %collective-permute-start.9 = (bf16[2,2,4,128,128]{3,4,0,2,1:T(8,128)(2,1)S(1)}, bf16[2,2,4,128,128]{3,4,0,2,1:T(8,128)(2,1)S(1)}, u32[]{:S(2)}, u32[]{:S(2)}) collective-permute-start(bf16[2,2,4,128,128]{3,4,0,2,1:T(8,128)(2,1)S(1)} %copy.13), channel_id=1, source_target_pairs={{0,2},{2,0},{4,6},{6,4},{8,10},{10,8},{12,14},{14,12},{16,18},{18,... | collective-permute-start | bytes 1572872 | tf_op jit(solution)/shard_map/ppermute | solution.py:12
  25.7 2.8 %collective-permute-start.12 = (bf16[256,256]{1,0:T(8,128)(2,1)S(1)}, bf16[256,256]{1,0:T(8,128)(2,1)S(1)}, u32[]{:S(2)}, u32[]{:S(2)}) collective-permute-start(bf16[256,256]{1,0:T(8,128)(2,1)S(1)} %bitcast.128), channel_id=1, source_target_pairs={{0,2},{2,0},{4,6},{6,4},{8,10},{10,8},{12,14},{14,12},{16,18},{18,... | collective-permute-start | bytes 393224 | tf_op jit(solution)/shard_map/ppermute | solution.py:12
  26.3 2.0 %collective-permute-start.10 = (bf16[256,256]{1,0:T(8,128)(2,1)S(1)}, bf16[256,256]{1,0:T(8,128)(2,1)S(1)}, u32[]{:S(2)}, u32[]{:S(2)}) collective-permute-start(bf16[256,256]{1,0:T(8,128)(2,1)S(1)} %get-tuple-element.24), channel_id=1, source_target_pairs={{0,2},{2,0},{4,6},{6,4},{8,10},{10,8},{12,14},{14,12},{16,18},{18,... | collective-permute-start | bytes 393224 | tf_op jit(solution)/shard_map/ppermute | solution.py:12
  28.9 8.3 %collective-permute-start.11 = (bf16[4,128,256]{2,1,0:T(8,128)(2,1)S(1)}, bf16[4,128,256]{2,1,0:T(8,128)(2,1)S(1)}, u32[]{:S(2)}, u32[]{:S(2)}) collective-permute-start(bf16[4,128,256]{2,1,0:T(8,128)(2,1)S(1)} %fusion.3.refs_1_), channel_id=1, source_target_pairs={{0,4},{2,6},{4,0},{6,2},{8,12},{10,14},{12,8},{14,10},{16,20},{18,... | collective-permute-start | bytes 786440 | tf_op jit(solution)/shard_map/ppermute | solution.py:12
  30.7 8.8 %collective-permute-start.15 = (bf16[128,256]{1,0:T(8,128)(2,1)S(1)}, bf16[128,256]{1,0:T(8,128)(2,1)S(1)}, u32[]{:S(2)}, u32[]{:S(2)}) collective-permute-start(bf16[128,256]{1,0:T(8,128)(2,1)S(1)} %shard_map.77.refs_0_), channel_id=1, source_target_pairs={{0,24},{2,26},{4,28},{6,30},{8,16},{10,18},{12,20},{14,22},{16,8},... | collective-permute-start | bytes 196616 | tf_op jit(solution)/shard_map/ppermute | solution.py:12
  32.5 7.0 %collective-permute-start.14 = (bf16[128,256]{1,0:T(8,128)(2,1)S(1)}, bf16[128,256]{1,0:T(8,128)(2,1)S(1)}, u32[]{:S(2)}, u32[]{:S(2)}) collective-permute-start(bf16[128,256]{1,0:T(8,128)(2,1)S(1)} %shard_map.77.refs_0_), channel_id=1, source_target_pairs={{0,16},{2,18},{4,20},{6,22},{8,24},{10,26},{12,28},{14,30},{16,0},... | collective-permute-start | bytes 196616 | tf_op jit(solution)/shard_map/ppermute | solution.py:12
  32.5 7.0 %collective-permute-start.13 = (bf16[128,256]{1,0:T(8,128)(2,1)S(1)}, bf16[128,256]{1,0:T(8,128)(2,1)S(1)}, u32[]{:S(2)}, u32[]{:S(2)}) collective-permute-start(bf16[128,256]{1,0:T(8,128)(2,1)S(1)} %shard_map.77.refs_0_), channel_id=1, source_target_pairs={{0,8},{2,10},{4,12},{6,14},{8,0},{10,2},{12,4},{14,6},{16,24},{18,... | collective-permute-start | bytes 196616 | tf_op jit(solution)/shard_map/ppermute | solution.py:12
  37.5 8.9 %collective-permute-start.18 = (bf16[128,256]{1,0:T(8,128)(2,1)S(1)}, bf16[128,256]{1,0:T(8,128)(2,1)S(1)}, u32[]{:S(2)}, u32[]{:S(2)}) collective-permute-start(bf16[128,256]{1,0:T(8,128)(2,1)S(1)} %get-tuple-element.22.refs_4_), channel_id=1, source_target_pairs={{0,24},{2,26},{4,28},{6,30},{8,16},{10,18},{12,20},{14,22},{16,8},... | collective-permute-start | bytes 196616 | tf_op jit(solution)/shard_map/ppermute | solution.py:12
  39.6 5.5 %collective-permute-start.16 = (bf16[128,256]{1,0:T(8,128)(2,1)S(1)}, bf16[128,256]{1,0:T(8,128)(2,1)S(1)}, u32[]{:S(2)}, u32[]{:S(2)}) collective-permute-start(bf16[128,256]{1,0:T(8,128)(2,1)S(1)} %shard_map.79), channel_id=1, source_target_pairs={{0,8},{2,10},{4,12},{6,14},{8,0},{10,2},{12,4},{14,6},{16,24},{18,... | collective-permute-start | bytes 196616 | tf_op jit(solution)/shard_map/ppermute | solution.py:12
  39.7 4.3 %collective-permute-start.19 = (bf16[128,256]{1,0:T(8,128)(2,1)S(1)}, bf16[128,256]{1,0:T(8,128)(2,1)S(1)}, u32[]{:S(2)}, u32[]{:S(2)}) collective-permute-start(bf16[128,256]{1,0:T(8,128)(2,1)S(1)} %shard_map.81.refs_0_), channel_id=1, source_target_pairs={{0,4},{2,6},{4,0},{6,2},{8,12},{10,14},{12,8},{14,10},{16,20},{18,... | collective-permute-start | bytes 196616 | tf_op jit(solution)/shard_map/ppermute | solution.py:12
  41.2 5.2 %collective-permute-start.17 = (bf16[128,256]{1,0:T(8,128)(2,1)S(1)}, bf16[128,256]{1,0:T(8,128)(2,1)S(1)}, u32[]{:S(2)}, u32[]{:S(2)}) collective-permute-start(bf16[128,256]{1,0:T(8,128)(2,1)S(1)} %get-tuple-element.21), channel_id=1, source_target_pairs={{0,16},{2,18},{4,20},{6,22},{8,24},{10,26},{12,28},{14,30},{16,0},... | collective-permute-start | bytes 196616 | tf_op jit(solution)/shard_map/ppermute | solution.py:12
  44.0 2.4 %collective-permute-start.20 = (f32[128,256]{1,0:T(8,128)S(1)}, f32[128,256]{1,0:T(8,128)S(1)}, u32[]{:S(2)}, u32[]{:S(2)}) collective-permute-start(f32[128,256]{1,0:T(8,128)S(1)} %shard_map.82.refs_1_), channel_id=1, source_target_pairs={{0,2},{2,0},{4,6},{6,4},{8,10},{10,8},{12,14},{14,12},{16,18},{18,... | collective-permute-start | bytes 393224 | tf_op jit(solution)/shard_map/ppermute | solution.py:12

commit v9 on v7

--- a/solution.py
+++ b/solution.py
@@ -132,10 +132,11 @@
         return [swap(features, "row", 4 * k + bit) if k or bit else features for k in reversed(range(low, high))][::-1]
 
     straight = 1
-    far = jnp.concatenate(direct(0, straight, depth))
+    pieces = direct(0, straight, depth)
+    far = jnp.concatenate(pieces)
     near = direct(0, 0, straight)
     near_x = jnp.concatenate(direct(2, 0, straight))
-    panel = jnp.concatenate(near + [far])
+    panel = jnp.concatenate(near + pieces)
     far_x = swap(far, "row", 2)
 
     cotangent = grad_out

time: 47.3 us -> 47.3 us (level)
  no operation moved by 1% of the time
where the time goes in v9:
time: 47.3 us; the launch traced here: 47.1 us
  starting transfers between devices  25.4 us (54%)
  waiting for transfers between devices  12.1 us (26%)
  matrix products  2.95 us (6%)
  Pallas kernels  2.16 us (5%)
  local copies, waits for them, and re-layouts  1.85 us (4%)
  other arithmetic  1.66 us (4%)
  between operations  0.96 us (2%)
    ppermute x21, starting transfers between devices, swap(): lax.ppermute(x, axis, [(i, i ^ bit) for i in range(lax.axis_size(axis))])  25.4 us
    ppermute x21, waiting for transfers between devices, swap(): lax.ppermute(x, axis, [(i, i ^ bit) for i in range(lax.axis_size(axis))])  12.1 us
    unnamed x10, local copies, waits for them, and re-layouts  1.52 us
    pallas_call x1, Pallas kernels, dense_tile(): pl.pallas_call(body, out_shape=(shape, shape), in_specs=[smem, smem, vmem...  1.3 us
  transfers between devices with their start and end apart: 21, of which 9 were waited for; matrix products, arithmetic and copies ran while one was open for 11% of the time, Pallas kernels for 3%

profile of v9, /device:TPU:0, one launch (start us, length us, event | category | flops | bytes accessed | tf_op | source)
XLA Modules:
  0.0 47.1 jit_solution(2680212856818302870)
XLA Ops:
  0.7 5.1 %collective-permute-start.2 = (bf16[128,256]{1,0:T(8,128)(2,1)}, bf16[128,256]{1,0:T(8,128)(2,1)S(1)}, u32[]{:S(2)}, u32[]{:S(2)}) collective-permute-start(bf16[128,256]{1,0:T(8,128)(2,1)} %param.5), channel_id=1, source_target_pairs={{0,24},{2,26},{4,28},{6,30},{8,16},{10,18},{12,20},{14,22},{16,8},... | collective-permute-start | bytes 196616 | tf_op jit(solution)/shard_map/ppermute | solution.py:12
  5.8 0.6 %collective-permute-start = (bf16[128,256]{1,0:T(8,128)(2,1)}, bf16[128,256]{1,0:T(8,128)(2,1)S(1)}, u32[]{:S(2)}, u32[]{:S(2)}) collective-permute-start(bf16[128,256]{1,0:T(8,128)(2,1)} %param.5), channel_id=1, source_target_pairs={{0,8},{2,10},{4,12},{6,14},{8,0},{10,2},{12,4},{14,6},{16,24},{18,... | collective-permute-start | bytes 196616 | tf_op jit(solution)/shard_map/ppermute | solution.py:12
  6.4 1.6 %collective-permute-start.6 = (bf16[128,256]{1,0:T(8,128)(2,1)}, bf16[128,256]{1,0:T(8,128)(2,1)S(1)}, u32[]{:S(2)}, u32[]{:S(2)}) collective-permute-start(bf16[128,256]{1,0:T(8,128)(2,1)} %param.5), channel_id=1, source_target_pairs={{0,4},{2,6},{4,0},{6,2},{8,12},{10,14},{12,8},{14,10},{16,20},{18,... | collective-permute-start | bytes 196616 | tf_op jit(solution)/shard_map/ppermute | solution.py:12
  8.0 1.5 %collective-permute-start.4 = (bf16[128,256]{1,0:T(8,128)(2,1)}, bf16[128,256]{1,0:T(8,128)(2,1)S(1)}, u32[]{:S(2)}, u32[]{:S(2)}) collective-permute-start(bf16[128,256]{1,0:T(8,128)(2,1)} %param.7), channel_id=1, source_target_pairs={{0,1},{1,0},{2,3},{3,2},{4,5},{5,4},{6,7},{7,6},{8,9},{9,8},{10,11... | collective-permute-start | bytes 196616 | tf_op jit(solution)/shard_map/ppermute | solution.py:12
  9.6 0.8 %constant_dynamic-update-slice_fusion.6 = bf16[512,256]{1,0:T(8,128)(2,1)S(1)} fusion(bf16[128,256]{1,0:T(8,128)(2,1)} %param.5), kind=kLoop, calls=%fused_computation.43 | loop fusion | bytes 131072
  10.4 1.2 %collective-permute-done.1 = bf16[128,256]{1,0:T(8,128)(2,1)S(1)} collective-permute-done((bf16[128,256]{1,0:T(8,128)(2,1)}, bf16[128,256]{1,0:T(8,128)(2,1)S(1)}, u32[]{:S(2)}, u32[]{:S(2)}) %collective-permute-start.1) | collective-permute-done | bytes 65568 | tf_op jit(solution)/shard_map/ppermute | solution.py:12
  11.6 1.6 %collective-permute-start.3 = (bf16[384,256]{1,0:T(8,128)(2,1)S(1)}, bf16[384,256]{1,0:T(8,128)(2,1)S(1)}, u32[]{:S(2)}, u32[]{:S(2)}) collective-permute-start(bf16[384,256]{1,0:T(8,128)(2,1)S(1)} %get-tuple-element.33.refs_0_), channel_id=1, source_target_pairs={{0,4},{2,6},{4,0},{6,2},{8,12},{10,14},{12,8},{14,10},{16,20},{18,... | collective-permute-start | bytes 589832 | tf_op jit(solution)/shard_map/ppermute | solution.py:12
  13.2 0.9 %broadcast_select_fusion.1 = (bf16[128,256]{1,0:T(8,128)(2,1)S(1)}, bf16[128,256]{1,0:T(8,128)(2,1)S(1)}) fusion(bf16[128,256]{1,0:T(8,128)(2,1)} %param.7, bf16[128,256]{1,0:T(8,128)(2,1)S(1)} %collective-permute-done.4, pred[]{:T(512)S(6)} %eq.4), kind=kLoop, calls=%fused_computation.36 | loop fusion | flops 65536 | bytes 262145 | tf_op jit(solution)/shard_map/jit(_where)/select_n | solution.py:145
  14.7 1.3 %shard_map.76 = (bf16[16,128,128]{2,1,0:T(8,128)(2,1)S(1)}, bf16[16,128,128]{2,1,0:T(8,128)(2,1)S(1)}) custom-call(s32[24]{0:T(128)S(1)} %bitcast.123, s32[1]{0:T(128)} %bitcast.1.row_ref, bf16[24,128,128]{2,1,0:T(8,128)(2,1)S(1)} %bitcast.122, bf16[384,256]{1,0:T(8,128)(2,1)S(1)} %get-tuple-element.33.refs_0_), custom_call_target="tpu_custom_call" | custom-call | flops 3000000000 | bytes 1000000 | tf_op jit(solution)/shard_map/pallas_call | solution.py:103
  16.5 1.6 %collective-permute-done.3 = bf16[384,256]{1,0:T(8,128)(2,1)S(1)} collective-permute-done((bf16[384,256]{1,0:T(8,128)(2,1)S(1)}, bf16[384,256]{1,0:T(8,128)(2,1)S(1)}, u32[]{:S(2)}, u32[]{:S(2)}) %collective-permute-start.3) | collective-permute-done | bytes 196640 | tf_op jit(solution)/shard_map/ppermute | solution.py:12
  18.5 1.3 %collective-permute-done.7 = bf16[512,256]{1,0:T(8,128)(2,1)S(1)} collective-permute-done((bf16[512,256]{1,0:T(8,128)(2,1)S(1)}, bf16[512,256]{1,0:T(8,128)(2,1)S(1)}, u32[]{:S(2)}, u32[]{:S(2)}) %collective-permute-start.7) | collective-permute-done | bytes 262176 | tf_op jit(solution)/shard_map/ppermute | solution.py:12
  20.0 1.8 %collective-permute-start.8 = (bf16[2,128,256]{2,1,0:T(8,128)(2,1)S(1)}, bf16[2,128,256]{2,1,0:T(8,128)(2,1)S(1)}, u32[]{:S(2)}, u32[]{:S(2)}) collective-permute-start(bf16[2,128,256]{2,1,0:T(8,128)(2,1)S(1)} %add_convert_fusion.1), channel_id=1, source_target_pairs={{0,1},{1,0},{2,3},{3,2},{4,5},{5,4},{6,7},{7,6},{8,9},{9,8},{10,11... | collective-permute-start | bytes 393224 | tf_op jit(solution)/shard_map/ppermute | solution.py:12
  22.1 3.5 %collective-permute-done.8 = bf16[2,128,256]{2,1,0:T(8,128)(2,1)S(1)} collective-permute-done((bf16[2,128,256]{2,1,0:T(8,128)(2,1)S(1)}, bf16[2,128,256]{2,1,0:T(8,128)(2,1)S(1)}, u32[]{:S(2)}, u32[]{:S(2)}) %collective-permute-start.8) | collective-permute-done | bytes 131104 | tf_op jit(solution)/shard_map/ppermute | solution.py:12
  28.5 1.7 %collective-permute-start.11 = (bf16[4,128,256]{2,1,0:T(8,128)(2,1)S(1)}, bf16[4,128,256]{2,1,0:T(8,128)(2,1)S(1)}, u32[]{:S(2)}, u32[]{:S(2)}) collective-permute-start(bf16[4,128,256]{2,1,0:T(8,128)(2,1)S(1)} %fusion.3.refs_1_), channel_id=1, source_target_pairs={{0,4},{2,6},{4,0},{6,2},{8,12},{10,14},{12,8},{14,10},{16,20},{18,... | collective-permute-start | bytes 786440 | tf_op jit(solution)/shard_map/ppermute | solution.py:12
  30.3 1.8 %collective-permute-start.15 = (bf16[128,256]{1,0:T(8,128)(2,1)S(1)}, bf16[128,256]{1,0:T(8,128)(2,1)S(1)}, u32[]{:S(2)}, u32[]{:S(2)}) collective-permute-start(bf16[128,256]{1,0:T(8,128)(2,1)S(1)} %shard_map.77.refs_0_), channel_id=1, source_target_pairs={{0,24},{2,26},{4,28},{6,30},{8,16},{10,18},{12,20},{14,22},{16,8},... | collective-permute-start | bytes 196616 | tf_op jit(solution)/shard_map/ppermute | solution.py:12
  32.1 2.6 %collective-permute-start.13 = (bf16[128,256]{1,0:T(8,128)(2,1)S(1)}, bf16[128,256]{1,0:T(8,128)(2,1)S(1)}, u32[]{:S(2)}, u32[]{:S(2)}) collective-permute-start(bf16[128,256]{1,0:T(8,128)(2,1)S(1)} %shard_map.77.refs_0_), channel_id=1, source_target_pairs={{0,8},{2,10},{4,12},{6,14},{8,0},{10,2},{12,4},{14,6},{16,24},{18,... | collective-permute-start | bytes 196616 | tf_op jit(solution)/shard_map/ppermute | solution.py:12
  34.7 0.6 %multiply_convert_fusion.1 = bf16[128,256]{1,0:T(8,128)(2,1)} fusion(f32[256,256]{1,0:T(8,128)S(1)} %get-tuple-element.29, s32[]{:T(128)S(6)} %select_n.23, f32[256,256]{1,0:T(8,128)S(1)} %fusion.11), kind=kLoop, calls=%fused_computation.28 | loop fusion | flops 65536 | bytes 327684 | tf_op jit(solution)/shard_map/convert_element_type | solution.py:220
  35.4 1.8 %collective-permute-done.11 = bf16[4,128,256]{2,1,0:T(8,128)(2,1)S(1)} collective-permute-done((bf16[4,128,256]{2,1,0:T(8,128)(2,1)S(1)}, bf16[4,128,256]{2,1,0:T(8,128)(2,1)S(1)}, u32[]{:S(2)}, u32[]{:S(2)}) %collective-permute-start.11) | collective-permute-done | bytes 262176 | tf_op jit(solution)/shard_map/ppermute | solution.py:12
  37.4 2.0 %collective-permute-start.18 = (bf16[128,256]{1,0:T(8,128)(2,1)S(1)}, bf16[128,256]{1,0:T(8,128)(2,1)S(1)}, u32[]{:S(2)}, u32[]{:S(2)}) collective-permute-start(bf16[128,256]{1,0:T(8,128)(2,1)S(1)} %get-tuple-element.26.refs_4_), channel_id=1, source_target_pairs={{0,24},{2,26},{4,28},{6,30},{8,16},{10,18},{12,20},{14,22},{16,8},... | collective-permute-start | bytes 196616 | tf_op jit(solution)/shard_map/ppermute | solution.py:12
  39.6 1.6 %collective-permute-start.19 = (bf16[128,256]{1,0:T(8,128)(2,1)S(1)}, bf16[128,256]{1,0:T(8,128)(2,1)S(1)}, u32[]{:S(2)}, u32[]{:S(2)}) collective-permute-start(bf16[128,256]{1,0:T(8,128)(2,1)S(1)} %shard_map.81.refs_0_), channel_id=1, source_target_pairs={{0,4},{2,6},{4,0},{6,2},{8,12},{10,14},{12,8},{14,10},{16,20},{18,... | collective-permute-start | bytes 196616 | tf_op jit(solution)/shard_map/ppermute | solution.py:12
  41.1 2.6 %collective-permute-start.17 = (bf16[128,256]{1,0:T(8,128)(2,1)S(1)}, bf16[128,256]{1,0:T(8,128)(2,1)S(1)}, u32[]{:S(2)}, u32[]{:S(2)}) collective-permute-start(bf16[128,256]{1,0:T(8,128)(2,1)S(1)} %get-tuple-element.25), channel_id=1, source_target_pairs={{0,16},{2,18},{4,20},{6,22},{8,24},{10,26},{12,28},{14,30},{16,0},... | collective-permute-start | bytes 196616 | tf_op jit(solution)/shard_map/ppermute | solution.py:12
  44.0 1.0 %collective-permute-done.16.refs_1_ = bf16[128,256]{1,0:T(8,128)(2,1)S(1)} collective-permute-done((bf16[128,256]{1,0:T(8,128)(2,1)S(1)}, bf16[128,256]{1,0:T(8,128)(2,1)S(1)}, u32[]{:S(2)}, u32[]{:S(2)}) %collective-permute-start.16) | collective-permute-done | bytes 65568 | tf_op jit(solution)/shard_map/ppermute | solution.py:12
  45.0 1.3 %collective-permute-done.17.refs_2_ = bf16[128,256]{1,0:T(8,128)(2,1)S(1)} collective-permute-done((bf16[128,256]{1,0:T(8,128)(2,1)S(1)}, bf16[128,256]{1,0:T(8,128)(2,1)S(1)}, u32[]{:S(2)}, u32[]{:S(2)}) %collective-permute-start.17) | collective-permute-done | bytes 65568 | tf_op jit(solution)/shard_map/ppermute | solution.py:12
  46.3 0.8 %shard_map.83 = (bf16[128,256]{1,0:T(8,128)(2,1)}, f32[256,256]{1,0:T(8,128)}) custom-call(s32[1]{0:T(128)} %bitcast.35.core_ref, f32[128,256]{1,0:T(8,128)S(1)} %shard_map.80.refs_0_, f32[128,256]{1,0:T(8,128)S(1)} %shard_map.82.refs_1_, f32[128,256]{1,0:T(8,128)S(1)} %collective-permute-done.20.refs_2_), custom_call_target="tpu_custom_call" | custom-call | flops 1000000 | bytes 1000000 | tf_op jit(solution)/shard_map/pallas_call | solution.py:63
  (59 shorter events, 5.6 us)
Async XLA Ops:
  0.6 25.1 %copy-start = (bf16[256,256]{1,0:T(8,128)(2,1)S(1)}, bf16[256,256]{1,0:T(8,128)(2,1)}, u32[]{:S(2)}) copy-start(bf16[256,256]{1,0:T(8,128)(2,1)} %param.6) | copy-start | bytes 393220
  0.6 13.5 %copy-start.1 = (bf16[1,1,24,128,128]{4,3,2,1,0:T(8,128)(2,1)S(1)}, bf16[1,1,24,128,128]{4,3,2,1,0:T(8,128)(2,1)}, u32[]{:S(2)}) copy-start(bf16[1,1,24,128,128]{4,3,2,1,0:T(8,128)(2,1)} %param.8) | copy-start | bytes 2359300
  0.7 10.9 %collective-permute-start.2 = (bf16[128,256]{1,0:T(8,128)(2,1)}, bf16[128,256]{1,0:T(8,128)(2,1)S(1)}, u32[]{:S(2)}, u32[]{:S(2)}) collective-permute-start(bf16[128,256]{1,0:T(8,128)(2,1)} %param.5), channel_id=1, source_target_pairs={{0,24},{2,26},{4,28},{6,30},{8,16},{10,18},{12,20},{14,22},{16,8},... | collective-permute-start | bytes 196616 | tf_op jit(solution)/shard_map/ppermute | solution.py:12
  5.8 5.8 %collective-permute-start.1 = (bf16[128,256]{1,0:T(8,128)(2,1)}, bf16[128,256]{1,0:T(8,128)(2,1)S(1)}, u32[]{:S(2)}, u32[]{:S(2)}) collective-permute-start(bf16[128,256]{1,0:T(8,128)(2,1)} %param.5), channel_id=1, source_target_pairs={{0,16},{2,18},{4,20},{6,22},{8,24},{10,26},{12,28},{14,30},{16,0},... | collective-permute-start | bytes 196616 | tf_op jit(solution)/shard_map/ppermute | solution.py:12
  5.8 4.6 %collective-permute-start = (bf16[128,256]{1,0:T(8,128)(2,1)}, bf16[128,256]{1,0:T(8,128)(2,1)S(1)}, u32[]{:S(2)}, u32[]{:S(2)}) collective-permute-start(bf16[128,256]{1,0:T(8,128)(2,1)} %param.5), channel_id=1, source_target_pairs={{0,8},{2,10},{4,12},{6,14},{8,0},{10,2},{12,4},{14,6},{16,24},{18,... | collective-permute-start | bytes 196616 | tf_op jit(solution)/shard_map/ppermute | solution.py:12
  6.4 7.7 %collective-permute-start.6 = (bf16[128,256]{1,0:T(8,128)(2,1)}, bf16[128,256]{1,0:T(8,128)(2,1)S(1)}, u32[]{:S(2)}, u32[]{:S(2)}) collective-permute-start(bf16[128,256]{1,0:T(8,128)(2,1)} %param.5), channel_id=1, source_target_pairs={{0,4},{2,6},{4,0},{6,2},{8,12},{10,14},{12,8},{14,10},{16,20},{18,... | collective-permute-start | bytes 196616 | tf_op jit(solution)/shard_map/ppermute | solution.py:12
  8.0 5.1 %collective-permute-start.4 = (bf16[128,256]{1,0:T(8,128)(2,1)}, bf16[128,256]{1,0:T(8,128)(2,1)S(1)}, u32[]{:S(2)}, u32[]{:S(2)}) collective-permute-start(bf16[128,256]{1,0:T(8,128)(2,1)} %param.7), channel_id=1, source_target_pairs={{0,1},{1,0},{2,3},{3,2},{4,5},{5,4},{6,7},{7,6},{8,9},{9,8},{10,11... | collective-permute-start | bytes 196616 | tf_op jit(solution)/shard_map/ppermute | solution.py:12
  11.6 6.5 %collective-permute-start.3 = (bf16[384,256]{1,0:T(8,128)(2,1)S(1)}, bf16[384,256]{1,0:T(8,128)(2,1)S(1)}, u32[]{:S(2)}, u32[]{:S(2)}) collective-permute-start(bf16[384,256]{1,0:T(8,128)(2,1)S(1)} %get-tuple-element.33.refs_0_), channel_id=1, source_target_pairs={{0,4},{2,6},{4,0},{6,2},{8,12},{10,14},{12,8},{14,10},{16,20},{18,... | collective-permute-start | bytes 589832 | tf_op jit(solution)/shard_map/ppermute | solution.py:12
  13.2 2.9 %collective-permute-start.5 = (bf16[512,256]{1,0:T(8,128)(2,1)S(1)}, bf16[512,256]{1,0:T(8,128)(2,1)S(1)}, u32[]{:S(2)}, u32[]{:S(2)}) collective-permute-start(bf16[512,256]{1,0:T(8,128)(2,1)S(1)} %get-tuple-element.32), channel_id=1, source_target_pairs={{0,2},{2,0},{4,6},{6,4},{8,10},{10,8},{12,14},{14,12},{16,18},{18,... | collective-permute-start | bytes 786440 | tf_op jit(solution)/shard_map/ppermute | solution.py:12
  14.1 0.7 %copy-start.2 = (s32[1,1,24]{2,1,0:T(1,128)S(1)}, s32[1,1,24]{2,1,0:T(1,128)}, u32[]{:S(2)}) copy-start(s32[1,1,24]{2,1,0:T(1,128)} %param.9) | copy-start | bytes 292
  18.2 1.6 %collective-permute-start.7 = (bf16[512,256]{1,0:T(8,128)(2,1)S(1)}, bf16[512,256]{1,0:T(8,128)(2,1)S(1)}, u32[]{:S(2)}, u32[]{:S(2)}) collective-permute-start(bf16[512,256]{1,0:T(8,128)(2,1)S(1)} %constant_dynamic-update-slice_fusion.7), channel_id=1, source_target_pairs={{0,2},{2,0},{4,6},{6,4},{8,10},{10,8},{12,14},{14,12},{16,18},{18,... | collective-permute-start | bytes 786440 | tf_op jit(solution)/shard_map/ppermute | solution.py:12
  20.0 5.6 %collective-permute-start.8 = (bf16[2,128,256]{2,1,0:T(8,128)(2,1)S(1)}, bf16[2,128,256]{2,1,0:T(8,128)(2,1)S(1)}, u32[]{:S(2)}, u32[]{:S(2)}) collective-permute-start(bf16[2,128,256]{2,1,0:T(8,128)(2,1)S(1)} %add_convert_fusion.1), channel_id=1, source_target_pairs={{0,1},{1,0},{2,3},{3,2},{4,5},{5,4},{6,7},{7,6},{8,9},{9,8},{10,11... | collective-permute-start | bytes 393224 | tf_op jit(solution)/shard_map/ppermute | solution.py:12
  22.1 6.2 %collective-permute-start.9 = (bf16[2,2,4,128,128]{3,4,0,2,1:T(8,128)(2,1)S(1)}, bf16[2,2,4,128,128]{3,4,0,2,1:T(8,128)(2,1)S(1)}, u32[]{:S(2)}, u32[]{:S(2)}) collective-permute-start(bf16[2,2,4,128,128]{3,4,0,2,1:T(8,128)(2,1)S(1)} %copy.13), channel_id=1, source_target_pairs={{0,2},{2,0},{4,6},{6,4},{8,10},{10,8},{12,14},{14,12},{16,18},{18,... | collective-permute-start | bytes 1572872 | tf_op jit(solution)/shard_map/ppermute | solution.py:12
  25.7 2.4 %collective-permute-start.12 = (bf16[256,256]{1,0:T(8,128)(2,1)S(1)}, bf16[256,256]{1,0:T(8,128)(2,1)S(1)}, u32[]{:S(2)}, u32[]{:S(2)}) collective-permute-start(bf16[256,256]{1,0:T(8,128)(2,1)S(1)} %bitcast.128), channel_id=1, source_target_pairs={{0,2},{2,0},{4,6},{6,4},{8,10},{10,8},{12,14},{14,12},{16,18},{18,... | collective-permute-start | bytes 393224 | tf_op jit(solution)/shard_map/ppermute | solution.py:12
  26.3 1.5 %collective-permute-start.10 = (bf16[256,256]{1,0:T(8,128)(2,1)S(1)}, bf16[256,256]{1,0:T(8,128)(2,1)S(1)}, u32[]{:S(2)}, u32[]{:S(2)}) collective-permute-start(bf16[256,256]{1,0:T(8,128)(2,1)S(1)} %get-tuple-element.28), channel_id=1, source_target_pairs={{0,2},{2,0},{4,6},{6,4},{8,10},{10,8},{12,14},{14,12},{16,18},{18,... | collective-permute-start | bytes 393224 | tf_op jit(solution)/shard_map/ppermute | solution.py:12
  28.5 8.6 %collective-permute-start.11 = (bf16[4,128,256]{2,1,0:T(8,128)(2,1)S(1)}, bf16[4,128,256]{2,1,0:T(8,128)(2,1)S(1)}, u32[]{:S(2)}, u32[]{:S(2)}) collective-permute-start(bf16[4,128,256]{2,1,0:T(8,128)(2,1)S(1)} %fusion.3.refs_1_), channel_id=1, source_target_pairs={{0,4},{2,6},{4,0},{6,2},{8,12},{10,14},{12,8},{14,10},{16,20},{18,... | collective-permute-start | bytes 786440 | tf_op jit(solution)/shard_map/ppermute | solution.py:12
  30.3 9.1 %collective-permute-start.15 = (bf16[128,256]{1,0:T(8,128)(2,1)S(1)}, bf16[128,256]{1,0:T(8,128)(2,1)S(1)}, u32[]{:S(2)}, u32[]{:S(2)}) collective-permute-start(bf16[128,256]{1,0:T(8,128)(2,1)S(1)} %shard_map.77.refs_0_), channel_id=1, source_target_pairs={{0,24},{2,26},{4,28},{6,30},{8,16},{10,18},{12,20},{14,22},{16,8},... | collective-permute-start | bytes 196616 | tf_op jit(solution)/shard_map/ppermute | solution.py:12
  32.1 7.3 %collective-permute-start.14 = (bf16[128,256]{1,0:T(8,128)(2,1)S(1)}, bf16[128,256]{1,0:T(8,128)(2,1)S(1)}, u32[]{:S(2)}, u32[]{:S(2)}) collective-permute-start(bf16[128,256]{1,0:T(8,128)(2,1)S(1)} %shard_map.77.refs_0_), channel_id=1, source_target_pairs={{0,16},{2,18},{4,20},{6,22},{8,24},{10,26},{12,28},{14,30},{16,0},... | collective-permute-start | bytes 196616 | tf_op jit(solution)/shard_map/ppermute | solution.py:12
  32.1 7.3 %collective-permute-start.13 = (bf16[128,256]{1,0:T(8,128)(2,1)S(1)}, bf16[128,256]{1,0:T(8,128)(2,1)S(1)}, u32[]{:S(2)}, u32[]{:S(2)}) collective-permute-start(bf16[128,256]{1,0:T(8,128)(2,1)S(1)} %shard_map.77.refs_0_), channel_id=1, source_target_pairs={{0,8},{2,10},{4,12},{6,14},{8,0},{10,2},{12,4},{14,6},{16,24},{18,... | collective-permute-start | bytes 196616 | tf_op jit(solution)/shard_map/ppermute | solution.py:12
  37.4 8.9 %collective-permute-start.18 = (bf16[128,256]{1,0:T(8,128)(2,1)S(1)}, bf16[128,256]{1,0:T(8,128)(2,1)S(1)}, u32[]{:S(2)}, u32[]{:S(2)}) collective-permute-start(bf16[128,256]{1,0:T(8,128)(2,1)S(1)} %get-tuple-element.26.refs_4_), channel_id=1, source_target_pairs={{0,24},{2,26},{4,28},{6,30},{8,16},{10,18},{12,20},{14,22},{16,8},... | collective-permute-start | bytes 196616 | tf_op jit(solution)/shard_map/ppermute | solution.py:12
  39.5 5.5 %collective-permute-start.16 = (bf16[128,256]{1,0:T(8,128)(2,1)S(1)}, bf16[128,256]{1,0:T(8,128)(2,1)S(1)}, u32[]{:S(2)}, u32[]{:S(2)}) collective-permute-start(bf16[128,256]{1,0:T(8,128)(2,1)S(1)} %shard_map.79), channel_id=1, source_target_pairs={{0,8},{2,10},{4,12},{6,14},{8,0},{10,2},{12,4},{14,6},{16,24},{18,... | collective-permute-start | bytes 196616 | tf_op jit(solution)/shard_map/ppermute | solution.py:12
  39.6 4.3 %collective-permute-start.19 = (bf16[128,256]{1,0:T(8,128)(2,1)S(1)}, bf16[128,256]{1,0:T(8,128)(2,1)S(1)}, u32[]{:S(2)}, u32[]{:S(2)}) collective-permute-start(bf16[128,256]{1,0:T(8,128)(2,1)S(1)} %shard_map.81.refs_0_), channel_id=1, source_target_pairs={{0,4},{2,6},{4,0},{6,2},{8,12},{10,14},{12,8},{14,10},{16,20},{18,... | collective-permute-start | bytes 196616 | tf_op jit(solution)/shard_map/ppermute | solution.py:12
  41.1 5.2 %collective-permute-start.17 = (bf16[128,256]{1,0:T(8,128)(2,1)S(1)}, bf16[128,256]{1,0:T(8,128)(2,1)S(1)}, u32[]{:S(2)}, u32[]{:S(2)}) collective-permute-start(bf16[128,256]{1,0:T(8,128)(2,1)S(1)} %get-tuple-element.25), channel_id=1, source_target_pairs={{0,16},{2,18},{4,20},{6,22},{8,24},{10,26},{12,28},{14,30},{16,0},... | collective-permute-start | bytes 196616 | tf_op jit(solution)/shard_map/ppermute | solution.py:12
  43.9 2.4 %collective-permute-start.20 = (f32[128,256]{1,0:T(8,128)S(1)}, f32[128,256]{1,0:T(8,128)S(1)}, u32[]{:S(2)}, u32[]{:S(2)}) collective-permute-start(f32[128,256]{1,0:T(8,128)S(1)} %shard_map.82.refs_1_), channel_id=1, source_target_pairs={{0,2},{2,0},{4,6},{6,4},{8,10},{10,8},{12,14},{14,12},{16,18},{18,... | collective-permute-start | bytes 393224 | tf_op jit(solution)/shard_map/ppermute | solution.py:12
